TPU v7x, 32 devices: a whole 2x2x4 slice. The times are simulated.
32 devices in a mesh: wide: 8 (over z, y), narrow: 4 (over x, core).
Axes of the slice: x: 2, y: 2, z: 4, core: 2. Of those that a mesh axis runs over, the one named last changes fastest.
Arguments:
- stream: bfloat16 [1024, 2048], P('wide', 'narrow'), may hold values from -6 to 6
- out_grad: bfloat16 [1024, 2048], P('wide', 'narrow'), may hold values from -6 to 6
- attn_gain: bfloat16 [2048], P('wide'), may hold values from 0.099609375 to 1.8984375
- attn_router: bfloat16 [2048, 4], P('wide'), may hold values from -0.125 to 0.125
- key_value: bfloat16 [2, 2048, 2048], P(None, 'wide', 'narrow'), may hold values from -0.125 to 0.125
- query_proj: bfloat16 [4, 2048, 2048], P(None, 'wide', 'narrow'), may hold values from -0.1875 to 0.1875
- output_proj: bfloat16 [4, 2048, 2048], P(None, 'wide', 'narrow'), may hold values from -0.5 to 0.5
- mlp_gain: bfloat16 [2048], P('wide'), may hold values from 0.099609375 to 1.8984375
- mlp_router: bfloat16 [2048, 4], P('wide'), may hold values from -0.125 to 0.125
- expert_in: bfloat16 [8, 2048, 2, 2816], P('wide', None, None, 'narrow'), may hold values from -0.125 to 0.125
- expert_down: bfloat16 [8, 2816, 2048], P('wide', 'narrow'), may hold values from -0.15625 to 0.15625
- attn_routes: int32 [1024, 2], P('wide'), may hold values from 0 to 3, all different within a row; in each aligned block of 128 rows (0 to 127, 128 to 255, ...) at most 80 rows name the same one
- mlp_routes: int32 [1024, 2], P('wide'), may hold values from 0 to 3, all different within a row; in each aligned block of 128 rows (0 to 127, 128 to 255, ...) at most 80 rows name the same one
- doc_lengths: int32 [8, 4], P('wide'), may hold values from 1 to 96, 128 in all within a row
Outputs:
- layer_out: float32 [1024, 2048], P('wide', 'narrow')
- stream_grad: float32 [1024, 2048], P('wide', 'narrow')
- attn_gain_grad: float32 [2048], P('wide')
- attn_router_grad: float32 [2048, 4], P('wide')
- key_value_grad: float32 [2, 2048, 2048], P(None, 'wide', 'narrow')
- query_grad: float32 [4, 2048, 2048], P(None, 'wide', 'narrow')
- output_grad: float32 [4, 2048, 2048], P(None, 'wide', 'narrow')
- mlp_gain_grad: float32 [2048], P('wide')
- mlp_router_grad: float32 [2048, 4], P('wide')
- expert_in_grad: float32 [8, 2048, 2, 2816], P('wide', None, None, 'narrow')
- expert_down_grad: float32 [8, 2816, 2048], P('wide', 'narrow')
Inputs may be any that keep to these rules, and one draw needn't show every extreme that they name: `attn_routes`: the 2 experts of a token differ. Among the 128 tokens of one block no expert is named more than 80 times, a bound that some block reaches. `mlp_routes`: as for attn_routes. `doc_lengths`: row b holds, in order, the lengths of the documents packed into tokens b * 128 to (b + 1) * 128 - 1; each row sums to 128.
All inputs are finite; a program needn't handle non-finite values.
Results may differ from a plain program's by a relative error of at most 0.019.
Values may be sent and summed in bfloat16 or wider, within the bound.
No kernel may reach another device: no remote copies, remote signals or barrier semaphores. Data moves between devices by JAX's collectives and lax.ppermute only.
A program may use at most 256 MiB of HBM per device.

v0:
```python
import jax
import jax.numpy as jnp
from jax import lax
from jax.experimental import pallas as pl
from jax.experimental.pallas import tpu as pltpu
from jax.sharding import PartitionSpec as P

HS = 128
E = 4
TOPK = 2
TOK = 128
SLOTS = 80

EPSILON = 1e-05
NEGATIVE = -1000000000.0
PRECISE = lax.Precision.HIGHEST
F32 = jnp.float32
BF16 = jnp.bfloat16


def dot(left, right, contract, precision=None):
    return lax.dot_general(
        left, right, ((contract[0], contract[1]), ((), ())), precision=precision, preferred_element_type=F32
    )


def xor_shuffle(values, amount):
    count, bit = values.shape[0], 1
    while bit < count:
        split = values.reshape((count // (2 * bit), 2, bit) + values.shape[1:])
        flipped = split[:, ::-1].reshape(values.shape)
        values = jnp.where((amount & bit) != 0, flipped, values)
        bit *= 2
    return values


NN = (((1,), (0,)), ((), ()))
NT = (((1,), (1,)), ((), ()))
TN = (((0,), (0,)), ((), ()))


def mul(left, right, form):
    return lax.dot_general(left, right, form, preferred_element_type=F32)


def shape(dims, dtype):
    return jax.ShapeDtypeStruct(tuple(dims), dtype)


def run(name, body, outs, args, scratch=()):
    vector = pl.BlockSpec(memory_space=pltpu.VMEM)
    return pl.pallas_call(
        body,
        out_shape=tuple(outs),
        in_specs=[pl.BlockSpec(memory_space=pltpu.SMEM)] + [vector] * (len(args) - 1),
        out_specs=tuple(vector for _ in outs),
        scratch_shapes=list(scratch),
        cost_estimate=pl.CostEstimate(flops=1, transcendentals=0, bytes_accessed=1),
        name=name,
    )(*args)


def place(store, parts, sub, first=0):
    for j, part in enumerate(parts):
        rows = part.shape[1]
        start = pl.multiple_of((sub ^ j) * rows, rows)
        for a in range(part.shape[0]):
            store[first + a, pl.ds(start, rows), :] = part[a]


def block(index):
    return pl.ds(pl.multiple_of(index * TOK, TOK), TOK)


def send_blocks(total, outs, order):
    for k in range(E):
        for a in range(total.shape[0]):
            outs[k][a] = total[a, block(order ^ k), :].astype(outs[k].dtype)


def key_value_body(subs):
    def body(at, *refs):
        rows, gain, parts = refs[:E], refs[E], refs[E + 1 : E + 1 + subs]
        gained, *outs = refs[E + 1 + subs : E + 2 + subs + E]
        weights, total = refs[E + 2 + subs + E :]
        place(weights, parts, at[1])
        for q in range(E):
            gained[q * TOK : (q + 1) * TOK, :] = (rows[q][...].astype(F32) * gain[...]).astype(BF16)
        for a in range(2):
            total[a] = mul(gained[...], weights[a], NN)
        send_blocks(total, outs, at[0])

    return body


def routed_body(subs, joined):
    count = 1 if joined else E

    def body(at, *refs):
        rows, hot, parts = refs[:count], refs[count], refs[count + 1 : count + 1 + subs]
        rest = refs[count + 1 + subs :]
        if joined:
            wide = rows[0]
        else:
            wide, rest = rest[0], rest[1:]
            for q in range(E):
                wide[q * TOK : (q + 1) * TOK, :] = rows[q][...]
        outs, weights, total = rest[:E], rest[E], rest[E + 1]
        place(weights, parts, at[1])
        for e in range(E):
            every = mul(wide[...], weights[e], NN)
            for i in range(TOPK):
                mine = every * hot[:, i * E + e : i * E + e + 1]
                total[i] = mine if e == 0 else total[i] + mine
        send_blocks(total, outs, at[0])

    return body


def spread_pairs(at, rows, hot, out, first=0):
    for k in range(E):
        where = block(at[0] ^ k)
        mask = hot[where, :].astype(BF16)
        for e in range(E):
            out[e, where, :] = (
                rows[k][first] * mask[:, e : e + 1]
                + rows[k][first + 1] * mask[:, E + e : E + e + 1]
            )


def fold_out(total, keep_0, keep_2, send):
    keep_0[...] = total[0:TOK]
    keep_2[...] = total[2 * TOK : 3 * TOK]
    send[0] = total[TOK : 2 * TOK].astype(BF16)
    send[1] = total[3 * TOK : 4 * TOK].astype(BF16)


def output_body(subs):
    def body(at, *refs):
        rows, hot, parts = refs[:E], refs[E], refs[E + 1 : E + 1 + subs]
        mixed, keep_0, keep_2, send, weights = refs[E + 1 + subs :]
        place(weights, parts, at[1])
        spread_pairs(at, rows, hot, mixed)
        total = mul(mixed[0], weights[0], NT)
        for e in range(1, E):
            total = total + mul(mixed[e], weights[e], NT)
        fold_out(total, keep_0, keep_2, send)

    return body


def input_body(subs):
    def body(at, *refs):
        rows, dmixed = refs[:E], refs[E]
        kv_parts = refs[E + 1 : E + 1 + subs]
        query_parts = refs[E + 1 + subs : E + 1 + 2 * subs]
        dkv_all, keep_0, keep_2, send, weights = refs[E + 1 + 2 * subs :]
        place(weights, kv_parts, at[1])
        place(weights, query_parts, at[1], 2)
        for k in range(E):
            for a in range(2):
                dkv_all[a, block(at[0] ^ k), :] = rows[k][a]
        total = mul(dkv_all[0], weights[0], NT) + mul(dkv_all[1], weights[1], NT)
        for e in range(E):
            total = total + mul(dmixed[e], weights[2 + e], NT)
        fold_out(total, keep_0, keep_2, send)

    return body


def split_rows(at, rows, other, parts, total):
    for a in range(other.shape[0]):
        total[...] = mul(rows[...], other[a], TN)
        for j, part in enumerate(parts):
            count = part.shape[1]
            start = pl.multiple_of((at[1] ^ j) * count, count)
            part[a] = total[pl.ds(start, count), :].astype(part.dtype)


def weight_grad_body(at, rows, other, *refs):
    split_rows(at, rows, other, refs[:-1], refs[-1])


def query_grad_body(at, rows, hot, *refs):
    dmixed = refs[E]
    spread_pairs(at, refs[:E], hot, dmixed, 2)
    split_rows(at, rows, dmixed, refs[E + 1 : -1], refs[-1])


def attention_mask(at):
    row = lax.broadcasted_iota(jnp.int32, (TOK, TOK), 0)
    col = lax.broadcasted_iota(jnp.int32, (TOK, TOK), 1)
    row_doc, col_doc, end = jnp.zeros_like(row), jnp.zeros_like(row), 0
    for d in range(4):
        end = end + at[d]
        row_doc = row_doc + (row >= end).astype(jnp.int32)
        col_doc = col_doc + (col >= end).astype(jnp.int32)
    return (row_doc == col_doc) & (col <= row)


def attention_body(at, own_kv, *refs):
    got_kv, own_query, got_query = refs[: E - 1], refs[E - 1], refs[E : 2 * E - 1]
    rows, low, probs, context, gated = refs[2 * E - 1 :]
    cols = columns(rows[...])
    scale = cols[:, 0:1]
    for a in range(4):
        own, got = (own_kv, got_kv) if a < 2 else (own_query, got_query)
        total = own[a % 2]
        for one in got:
            total = total + one[a % 2].astype(F32)
        low[a] = (total * scale).astype(BF16)
    allowed = attention_mask(at)
    for h in range(low.shape[2] // HS):
        head = slice(h * HS, (h + 1) * HS)
        for i in range(TOPK):
            scores = mul(low[2 + i, :, head], low[0, :, head], NT) * HS ** (-0.5)
            scores = jnp.where(allowed, scores, NEGATIVE)
            top = jnp.exp(scores - jnp.max(scores, axis=-1, keepdims=True))
            prob = top / jnp.sum(top, axis=-1, keepdims=True)
            probs[h, i * TOK : (i + 1) * TOK, :] = prob
            mixed = mul(prob.astype(BF16), low[1, :, head], NN).astype(BF16)
            context[i, :, head] = mixed
            gated[i, :, head] = (mixed.astype(F32) * cols[:, 1 + i : 2 + i]).astype(BF16)


def attention_back_body(at, own, *refs):
    got = refs[: E - 1]
    rows, low, probs, context, grads, sums = refs[E - 1 :]
    cols = columns(rows[...])
    scale = cols[:, 0:1]
    inner = jnp.zeros((TOK, 1), F32)
    dprob = []
    dcontext = []
    for i in range(TOPK):
        raw = own[i]
        for one in got:
            raw = raw + one[i].astype(F32)
        dprob.append(jnp.sum(context[i].astype(F32) * raw, axis=-1, keepdims=True))
        dcontext.append((raw * cols[:, 1 + i : 2 + i]).astype(BF16))
    for h in range(low.shape[2] // HS):
        head = slice(h * HS, (h + 1) * HS)
        key, value = low[0, :, head], low[1, :, head]
        dkey = jnp.zeros((TOK, HS), F32)
        dvalue = jnp.zeros((TOK, HS), F32)
        for i in range(TOPK):
            query = low[2 + i, :, head]
            grad = dcontext[i][:, head]
            prob = probs[h, i * TOK : (i + 1) * TOK, :]
            dweight = mul(grad, value, NT)
            dscore = prob * (dweight - jnp.sum(prob * dweight, axis=-1, keepdims=True))
            dscore = dscore.astype(BF16)
            done = mul(dscore, key, NN) * HS ** (-0.5)
            dkey = dkey + mul(dscore, query, TN)
            dvalue = dvalue + mul(prob.astype(BF16), grad, TN)
            inner = inner + jnp.sum(done * query.astype(F32), axis=-1, keepdims=True)
            grads[2 + i, :, head] = (done * scale).astype(BF16)
        dkey = dkey * HS ** (-0.5)
        inner = inner + jnp.sum(
            dkey * key.astype(F32) + dvalue * value.astype(F32), axis=-1, keepdims=True
        )
        grads[0, :, head] = (dkey * scale).astype(BF16)
        grads[1, :, head] = (dvalue * scale).astype(BF16)
    lane = lax.broadcasted_iota(jnp.int32, (TOK, TOK), 1)
    table = jnp.where(lane == 0, dprob[0], jnp.where(lane == 1, dprob[1], jnp.where(lane == 2, inner, 0.0)))
    sums[...] = jnp.transpose(table)[0:8]


def columns(rows):
    return jnp.transpose(jnp.concatenate([rows] * (TOK // rows.shape[0]), axis=0))


def pick_row(values, index):
    line = lax.broadcasted_iota(jnp.int32, values.shape, 0)
    return jnp.sum(jnp.where(line == index, values, 0.0), axis=0, keepdims=True)


def route_body(subs, capacity):
    count = E * subs * 8

    def body(at, *refs):
        tables = refs[:E]
        hot_cols, home, turned, mlp_cols, expert_rows, select = refs[E : E + 6]
        both, rank, kept, hot, mlp_hot = refs[E + 6 :]
        expert = lax.broadcasted_iota(jnp.int32, (E, TOK), 0).astype(F32)
        for k in range(E):
            for j in range(subs):
                line = tables[k][j].astype(F32)
                ones = [(line[r : r + 1] == expert).astype(F32) for r in range(4)]
                start = (k * subs + j) * 8
                both[start : start + 4, :] = ones[0] + ones[1]
                both[start + 4 : start + 8, :] = ones[2] + ones[3]
                if j == 0:
                    hot[k, 0:4, :], hot[k, 4:8, :] = ones[0], ones[1]
                    mlp_hot[k, 0:4, :], mlp_hot[k, 4:8, :] = ones[2], ones[3]
        low = both[...].astype(BF16)
        row = lax.broadcasted_iota(jnp.int32, (TOK, TOK), 0)
        col = lax.broadcasted_iota(jnp.int32, (TOK, TOK), 1)
        rank[...] = mul(low, (row < col).astype(F32).astype(BF16), NN)
        row = lax.broadcasted_iota(jnp.int32, (count, count), 0)
        col = lax.broadcasted_iota(jnp.int32, (count, count), 1)
        own = at[2] * subs + at[1]
        ahead = (((col >> 3) ^ own) < ((row >> 3) ^ own)) & ((col & 7) == (row & 7))
        before = mul(ahead.astype(F32).astype(BF16), low, NN)
        place_of = jnp.sum(before, axis=-1, keepdims=True) + rank[...]
        kept[...] = both[...] * (place_of < capacity).astype(F32)

        for k in range(E):
            hot_cols[block(at[0] ^ k), :] = columns(hot[k])[:, 0:8]
        pad = jnp.zeros((6, TOK), F32)
        home[0:8, :] = hot[0]
        for i in range(TOPK):
            home[8 + i : 9 + i, :] = jnp.sum(
                hot[0, i * E : (i + 1) * E, :] * kept[0:E, :], axis=0, keepdims=True
            )
        home[10:16, :] = pad
        mine = mlp_hot[at[0]]
        start = pl.multiple_of(at[0] * (subs * 8), 8)
        kept_mine = kept[pl.ds(start, 8), :][4:8]
        rank_mine = rank[pl.ds(start, 8), :][4:8]
        turned[0:8, :] = mine
        for i in range(TOPK):
            turned[8 + i : 9 + i, :] = jnp.sum(
                mine[i * E : (i + 1) * E] * kept_mine, axis=0, keepdims=True
            )
        turned[10:16, :] = pad
        mlp_cols[...] = columns(mine)[:, 0:8]
        slot = lax.broadcasted_iota(jnp.int32, (SLOTS, TOK), 0).astype(F32)
        for k in range(E):
            e = at[2] ^ k
            for i in range(TOPK):
                expert_rows[2 * k + i : 2 * k + i + 1, :] = pick_row(mine[i * E : (i + 1) * E], e)
            taken = (slot == pick_row(rank_mine, e)) & (pick_row(kept_mine, e) > 0)
            select[k] = taken.astype(F32).astype(BF16)

    return body


def two_halves(values):
    lane = lax.broadcasted_iota(jnp.int32, (values[0].shape[0], 128), 1)
    table = jnp.zeros((values[0].shape[0], 128), F32)
    for i, one in enumerate(values):
        high = one.astype(BF16).astype(F32)
        table = jnp.where(lane == 2 * i, high, table)
        table = jnp.where(lane == 2 * i + 1, one - high, table)
    return table.astype(BF16)


def pick_body(at, stream, keep, got, other, gain, router, mlp_cols, select, *refs):
    hidden, stats, outs = refs[0], refs[1], refs[2:]
    size = hidden.shape[1]
    total = stream[...].astype(F32) + (keep[...] + got[0].astype(F32) + other[...].astype(F32))
    hidden[...] = total
    gained = total * gain[...]
    square = jnp.sum(total * total, axis=-1, keepdims=True)
    logits = lax.dot_general(
        gained, router[...], NT, precision=lax.Precision.HIGHEST, preferred_element_type=F32
    )
    lane = lax.broadcasted_iota(jnp.int32, logits.shape, 1)
    chosen = jnp.zeros_like(square)
    for e in range(E):
        one = mlp_cols[:, e : e + 1] + mlp_cols[:, E + e : E + e + 1]
        chosen = chosen + one * logits[:, e : e + 1]
    low = gained.astype(BF16)
    for k in range(E):
        own = jnp.sum(jnp.where(lane == (at[2] ^ k), logits, 0.0), axis=-1, keepdims=True)
        extra = two_halves([square, 2.0 * own - chosen])
        outs[k][:, :size] = mul(select[k], low, NN).astype(BF16)
        outs[k][:, size:] = mul(select[k], extra, NN).astype(BF16)
    lane = lax.broadcasted_iota(jnp.int32, (TOK, TOK), 1)
    table = jnp.where(lane == E, square, 0.0)
    for e in range(E):
        table = jnp.where(lane == e, logits[:, e : e + 1], table)
    stats[...] = jnp.transpose(table)[0:8]


def join_rows_body(at, *refs):
    pieces, out = refs[:E], refs[E]
    size = pieces[0].shape[1] - 128
    join_pieces(at, pieces, out, size)
    total = pieces[0][:, size:].astype(F32)
    for k in range(1, E):
        total = total + pieces[k][:, size:].astype(F32)
    square, gap = total[:, 0:1] + total[:, 1:2], total[:, 2:3] + total[:, 3:4]
    scale = lax.rsqrt(square / (E * size) + EPSILON)
    small = jnp.exp(-jnp.abs(gap * scale))
    gate = jnp.where(gap < 0.0, small, 1.0) / (1.0 + small)
    out[:, E * size :] = two_halves([scale, gate])


def join_pieces(at, pieces, out, size):
    for k in range(E):
        for p in range(E):

            @pl.when((at[2] ^ k) == p)
            def _(k=k, p=p):
                out[:, p * size : (p + 1) * size] = pieces[k][:, :size]


def join_body(at, *refs):
    join_pieces(at, refs[:E], refs[E], refs[0].shape[1])


def split_body(extra):
    def body(at, own, got, *refs):
        outs, store = refs[:E], refs[E]
        store[...] = (own[...] + got[...].astype(F32)).astype(BF16)
        size = outs[0].shape[1] - extra
        for k in range(E):
            for p in range(E):

                @pl.when((at[2] ^ k) == p)
                def _(k=k, p=p):
                    outs[k][:, :size] = store[:, p * size : (p + 1) * size]

            if extra:
                outs[k][:, size:] = store[:, E * size :]

    return body


def local(
    stream,
    out_grad,
    attn_gain,
    attn_router,
    key_value,
    query_proj,
    output_proj,
    mlp_gain,
    mlp_router,
    expert_in,
    expert_down,
    attn_routes,
    mlp_routes,
    doc_lengths,
):
    wide_count = lax.axis_size("wide")
    narrow_count = lax.axis_size("narrow")
    subs = wide_count // E
    wide = lax.axis_index("wide")
    narrow = lax.axis_index("narrow")
    plane, sub = wide // subs, wide % subs
    capacity = 9 * TOK * wide_count * TOPK // (8 * E)
    slice_width = stream.shape[1]
    shard_rows = attn_gain.shape[0]
    width = slice_width * narrow_count
    local_width = key_value.shape[2]
    head_count = local_width // HS
    hidden_units = expert_down.shape[1]
    score_scale = HS ** (-0.5)

    def after(values, *others):
        return lax.optimization_barrier((values, others))[0]

    def by_plane(values, k):
        return lax.ppermute(values, "wide", [(i, i ^ (k * subs)) for i in range(wide_count)])

    def by_sub(values, k):
        return lax.ppermute(values, "wide", [(i, i ^ k) for i in range(wide_count)])

    def by_narrow(values, k):
        return lax.ppermute(values, "narrow", [(i, i ^ k) for i in range(narrow_count)])

    def swap(values):
        pairs = []
        for w in range(wide_count):
            for n in range(narrow_count):
                z, y = w // subs, w % subs
                pairs.append((w * narrow_count + n, (n * subs + y) * narrow_count + z))
        return lax.ppermute(values, ("wide", "narrow"), pairs)

    def gather_planes(values):
        return [values] + [by_plane(values, k) for k in range(1, E)]

    def exchange_planes(parts):
        return [parts[0]] + [by_plane(parts[k], k) for k in range(1, E)]

    def gather_subs(values):
        parts, bit = [values], 1
        while bit < subs:
            parts = parts + [by_sub(one, bit) for one in parts]
            bit *= 2
        return parts

    def reduce_subs(parts):
        bit = len(parts) // 2
        while bit >= 1:
            parts = [parts[j] + by_sub(parts[j + bit].astype(BF16), bit).astype(F32) for j in range(bit)]
            bit //= 2
        return parts[0]

    def gather_narrow(values):
        other = by_narrow(values, 2)
        return [values, by_narrow(values, 1), other, by_narrow(other, 1)]

    def reduce_narrow(keep_0, keep_2, send):
        got = by_narrow(send, 1)
        other = by_narrow((keep_2 + got[1].astype(F32)).astype(BF16), 2)
        return keep_0, got, other

    def finish_subs(keep, send):
        bit = len(keep)
        keep = [keep[j] + by_sub(send[j], bit).astype(F32) for j in range(bit)]
        return reduce_subs(keep)

    def sum_narrow(values):
        values = values + by_narrow(values, 2)
        return values + by_narrow(values, 1)

    def sum_planes(values):
        values = values + by_plane(values, 1)
        return values + by_plane(values, 2)

    def sum_subs(values):
        bit = 1
        while bit < subs:
            values = values + by_sub(values, bit)
            bit *= 2
        return values

    own_rows = jnp.concatenate(
        [attn_gain[None, :], attn_router.T, mlp_gain[None, :], mlp_router.T], axis=0
    )
    parts = gather_subs(jnp.pad(own_rows, ((0, 16 - own_rows.shape[0]), (0, 0))))
    near = xor_shuffle(jnp.stack(parts), sub).swapaxes(0, 1).reshape(16, slice_width)
    gain_one_plane = near[0].astype(F32)
    gain_two_plane = near[5].astype(F32)
    router_two_plane = near[6:10].astype(F32)
    home_rows = swap(near)
    gain_one_home = home_rows[0].astype(F32)
    router_one_home = home_rows[1:5].astype(F32)

    own_routes = jnp.concatenate([attn_routes.T, mlp_routes.T], axis=0).astype(BF16)
    route_parts = gather_subs(jnp.pad(own_routes, ((0, 4), (0, 0))))
    at = jnp.stack([narrow ^ plane, sub, plane, narrow]).astype(jnp.int32)
    line_count = wide_count * 8
    hot_cols, home_hot, turned_hot, mlp_cols, expert_hot, select = run(
        "route",
        route_body(subs, capacity),
        [
            shape((E * TOK, 8), F32),
            shape((16, TOK), F32),
            shape((16, TOK), F32),
            shape((TOK, 8), F32),
            shape((8, TOK), F32),
            shape((E, SLOTS, TOK), BF16),
        ],
        [at, *gather_planes(jnp.stack(route_parts))],
        [pltpu.VMEM((line_count, TOK), F32)] * 3 + [pltpu.VMEM((E, 8, TOK), F32)] * 2,
    )
    hot_one, keep_one = home_hot[0:8].reshape(TOPK, E, TOK), home_hot[8:10]
    hot_two, keep_two = turned_hot[0:8].reshape(TOPK, E, TOK), turned_hot[8:10]
    hot_two_k = expert_hot.reshape(E, TOPK, TOK)

    kv_parts = gather_subs(key_value)
    query_parts = gather_subs(query_proj)
    home_stream = stream.astype(F32)
    turned_stream = swap(stream)
    turned_grad = swap(out_grad)

    rows_all = E * TOK
    sent = shape((2, TOK, local_width), BF16)
    kept_own = shape((2, TOK, local_width), F32)
    gained, *kv_blocks = run(
        "key_value",
        key_value_body(subs),
        [shape((rows_all, slice_width), BF16), kept_own] + [sent] * (E - 1),
        [at, *gather_narrow(turned_stream), gain_one_plane[None], *kv_parts],
        [
            pltpu.VMEM((2, slice_width, local_width), BF16),
            pltpu.VMEM((2, rows_all, local_width), F32),
        ],
    )
    kv_blocks = exchange_planes(kv_blocks)
    routed_scratch = [
        pltpu.VMEM((E, slice_width, local_width), BF16),
        pltpu.VMEM((TOPK, rows_all, local_width), F32),
    ]
    query_blocks = run(
        "query",
        routed_body(subs, True),
        [kept_own] + [sent] * (E - 1),
        [at, gained, hot_cols, *query_parts],
        routed_scratch,
    )
    query_blocks = exchange_planes(query_blocks)

    gained_home = home_stream * gain_one_home
    stats_one = jnp.concatenate(
        [
            jnp.sum(home_stream * home_stream, axis=-1)[None],
            dot(router_one_home, gained_home, ((1,), (1,)), PRECISE),
        ],
        axis=0,
    )
    stats_one = sum_narrow(stats_one)
    scale_one = lax.rsqrt(stats_one[0] / width + EPSILON)
    logits_one = stats_one[1:] * scale_one

    def gates(logits, hots):
        picked = jnp.sum(hots * logits[None], axis=1)
        gap = picked[0] - picked[1]
        return jnp.stack([jax.nn.sigmoid(gap), jax.nn.sigmoid(-gap)])

    prob_one = gates(logits_one, hot_one)
    gate_one = prob_one * keep_one

    token_rows = jnp.stack([scale_one, gate_one[0], gate_one[1]] + [scale_one] * 5)
    low, probs, context, gated = run(
        "attention",
        attention_body,
        [
            shape((4, TOK, local_width), BF16),
            shape((head_count, TOPK * TOK, TOK), F32),
            sent,
            sent,
        ],
        [doc_lengths[0], *kv_blocks, *query_blocks, token_rows],
    )

    out_parts = gather_subs(output_proj)

    folded = [shape((TOK, slice_width), F32), shape((TOK, slice_width), F32), shape((2, TOK, slice_width), BF16)]
    mixed, *attention = run(
        "output",
        output_body(subs),
        [shape((E, rows_all, local_width), BF16)] + folded,
        [at, *gather_planes(gated), hot_cols, *out_parts],
        [pltpu.VMEM((E, slice_width, local_width), BF16)],
    )
    def share(full):
        full = jnp.stack(gather_subs(full))
        two = jnp.stack([full, by_narrow(full, 2)])
        one = by_narrow(two, 1)
        return jnp.stack([two[0], one[0], two[1], one[1]]).reshape(-1, full.shape[-1])

    picked = jnp.einsum("kst,td->ksd", select, turned_grad, preferred_element_type=F32).astype(BF16)
    (full,) = run(
        "join",
        join_body,
        [shape((SLOTS, width), BF16)],
        [at, *exchange_planes([picked[k] for k in range(E)])],
    )
    grad_rows = share(full)
    weight_in = expert_in[0]
    weight_down = expert_down[0]
    dact_raw = dot(grad_rows, weight_down, ((1,), (1,)))

    hidden, stats_two, *picked = run(
        "pick",
        pick_body,
        [shape((TOK, slice_width), F32), shape((8, TOK), F32)]
        + [shape((SLOTS, slice_width + 128), BF16)] * E,
        [
            at,
            turned_stream,
            *reduce_narrow(*attention),
            gain_two_plane[None],
            jnp.pad(router_two_plane, ((0, 4), (0, 0))),
            mlp_cols,
            select,
        ],
    )
    (full,) = run(
        "join_rows",
        join_rows_body,
        [shape((SLOTS, width + 128), BF16)],
        [at, *exchange_planes(picked)],
    )
    full = share(full)
    expert_rows = full[:, :width]
    row_pairs = full[:, width : width + 4].astype(F32)
    row_scale = row_pairs[:, 0:1] + row_pairs[:, 1:2]
    row_gate = row_pairs[:, 2:3] + row_pairs[:, 3:4]
    stats_two = sum_planes(stats_two)
    scale_two = lax.rsqrt(stats_two[E] / width + EPSILON)
    logits_two = stats_two[:E] * scale_two
    prob_two = gates(logits_two, hot_two)

    gate_up = jnp.einsum("rd,dkf->krf", expert_rows, weight_in, preferred_element_type=F32)
    gate_pre = gate_up[0] * row_scale
    up_pre = gate_up[1] * row_scale
    gate_sig = jax.nn.sigmoid(gate_pre)
    silu_gate = gate_pre * gate_sig
    activation = (silu_gate * up_pre).astype(BF16)
    dactiv = dact_raw * row_gate
    dgate_pre = (dactiv * up_pre * gate_sig * (1.0 + gate_pre * (1.0 - gate_sig))).astype(BF16)
    dup_pre = (dactiv * silu_gate).astype(BF16)
    dprob_rows = jnp.sum(activation.astype(F32) * dact_raw, axis=-1)
    inner_rows = jnp.sum(dgate_pre.astype(F32) * gate_pre + dup_pre.astype(F32) * up_pre, axis=-1)
    drows = jnp.einsum(
        "krf,dkf->rd", jnp.stack([dgate_pre, dup_pre]), weight_in, preferred_element_type=F32
    )
    lanes = jnp.arange(128)
    row_stats = jnp.where(
        lanes[None, :] == 0, dprob_rows[:, None], jnp.where(lanes[None, :] == 1, inner_rows[:, None], 0.0)
    )

    def give_back(rows):
        shaped = rows.reshape(narrow_count, subs, SLOTS, -1)
        low = shaped.astype(BF16)
        got = by_narrow(jnp.stack([low[1], low[3]]), 1)
        two = jnp.stack([shaped[0], shaped[2]]) + got.astype(F32)
        one = two[0] + by_narrow(two[1].astype(BF16), 2).astype(F32)
        parts, bit = [one[j] for j in range(subs)], subs // 2
        while bit > 1:
            parts = [parts[j] + by_sub(parts[j + bit].astype(BF16), bit).astype(F32) for j in range(bit)]
            bit //= 2
        return parts[0], by_sub(parts[1].astype(BF16), 1)

    def from_planes(own, got, extra, last=None):
        pieces = run(
            "split",
            split_body(extra),
            [shape((SLOTS, slice_width + extra), BF16)] * E,
            [at, own, got],
            [pltpu.VMEM(own.shape, BF16)],
        )
        if last is not None:
            pieces = after(pieces, last)
        return jnp.stack(exchange_planes(pieces))

    returned = give_back(jnp.concatenate([drows, row_stats], axis=1))
    returned = from_planes(*returned, row_stats.shape[1])
    combined = jnp.einsum("kst,ksd->ktd", select, returned, preferred_element_type=F32)
    per_expert = combined[:, :, slice_width : slice_width + 2]
    dprob_two = keep_two * jnp.sum(hot_two_k * per_expert[:, None, :, 0], axis=0)
    inner_two = jnp.sum(per_expert[:, :, 1], axis=0)
    dnormed_two = jnp.sum(combined[:, :, :slice_width], axis=0)

    def gate_back(prob, dprob, hots):
        dselect = prob * (dprob - jnp.sum(prob * dprob, axis=0, keepdims=True))
        return jnp.sum(hots * dselect[:, None, :], axis=0)

    dlogit_two = gate_back(prob_two, dprob_two, hot_two)
    dnormed_two = dnormed_two + dot(dlogit_two, router_two_plane, ((0,), (0,)), PRECISE)
    inner_two = inner_two + jnp.sum(dlogit_two * logits_two, axis=0)
    dhidden = (
        turned_grad.astype(F32)
        + scale_two[:, None] * (dnormed_two * gain_two_plane)
        - hidden * (scale_two * scale_two * inner_two / width)[:, None]
    )
    scaled_hidden = hidden * scale_two[:, None]
    mlp_terms = jnp.concatenate(
        [
            jnp.sum(dnormed_two * scaled_hidden, axis=0)[None],
            dot(dlogit_two, scaled_hidden * gain_two_plane, ((1,), (0,)), PRECISE),
        ],
        axis=0,
    )

    wide_grad, *dcontext_blocks = run(
        "dcontext",
        routed_body(subs, False),
        [shape((rows_all, slice_width), BF16), kept_own] + [sent] * (E - 1),
        [at, *gather_narrow(dhidden.astype(BF16)), hot_cols, *out_parts],
        routed_scratch,
    )
    dcontext_blocks = exchange_planes(dcontext_blocks)

    def weight_parts(count):
        return [
            shape((count, shard_rows, local_width), F32 if j < subs // 2 else BF16)
            for j in range(subs)
        ]

    def weight_sum(parts):
        return finish_subs(parts[: subs // 2], parts[subs // 2 :])

    weight_scratch = [pltpu.VMEM((slice_width, local_width), F32)]
    output_parts = run(
        "output_grad", weight_grad_body, weight_parts(E), [at, wide_grad, mixed], weight_scratch
    )
    output_grad = weight_sum(output_parts)
    gated_act = (activation.astype(F32) * row_gate).astype(BF16)
    down_grad = dot(after(gated_act, dcontext_blocks[1]), grad_rows, ((0,), (0,)))
    grads_low, home_sums = run(
        "attention_back",
        attention_back_body,
        [shape((4, TOK, local_width), BF16), shape((8, TOK), F32)],
        [
            at,
            *after(dcontext_blocks, output_parts[-1], down_grad),
            token_rows,
            low,
            probs,
            context,
        ],
    )
    grad_planes = gather_planes(grads_low)
    home_sums = sum_narrow(home_sums)
    dprob_one = keep_one * home_sums[:2]
    dlogit_one = gate_back(prob_one, dprob_one, hot_one)
    inner_one = home_sums[2] + jnp.sum(dlogit_one * logits_one, axis=0)
    dlogit_scaled = dlogit_one * scale_one
    router_term = swap(dot(dlogit_scaled, gained_home, ((1,), (0,)), PRECISE))
    dmixed, *query_grad_parts = run(
        "query_grad",
        query_grad_body,
        [shape((E, rows_all, local_width), BF16)] + weight_parts(E),
        [at, gained, hot_cols, *after(grad_planes, output_grad, router_term)],
        weight_scratch,
    )
    query_grad = weight_sum(query_grad_parts)
    dkv_all, *dnormed_one = run(
        "input",
        input_body(subs),
        [shape((2, rows_all, local_width), BF16)] + folded,
        [at, *after(grad_planes, query_grad_parts[-1]), dmixed, *kv_parts, *query_parts],
        [pltpu.VMEM((2 + E, slice_width, local_width), BF16)],
    )
    kv_grad_parts = run(
        "key_value_grad", weight_grad_body, weight_parts(2), [at, gained, dkv_all], weight_scratch
    )
    kv_grad = weight_sum(after(kv_grad_parts, query_grad))
    keep, got, other = after(reduce_narrow(*dnormed_one), kv_grad_parts[-1], query_grad)
    dnormed_one = keep + got[0].astype(F32) + other.astype(F32)
    turned_out = dhidden + dnormed_one * gain_one_plane
    home_out = swap(turned_out.astype(BF16)).astype(F32)
    stream_grad = (
        home_out
        + gain_one_home * dot(dlogit_scaled, router_one_home, ((0,), (0,)), PRECISE)
        - home_stream * (scale_one * scale_one * inner_one / width)[:, None]
    )

    gain_term = jnp.sum(dnormed_one * turned_stream.astype(F32), axis=0)
    small = jnp.concatenate([mlp_terms, gain_term[None], router_term], axis=0)
    small = sum_subs(sum_narrow(small))
    mine = lax.dynamic_slice_in_dim(small, sub * shard_rows, shard_rows, 1)
    router_one_grad = mine[6:10]
    gain_one_grad = mine[5] + jnp.sum(
        router_one_grad * attn_router.T.astype(F32), axis=0
    ) / attn_gain.astype(F32)

    expert_out = dot(activation, weight_down, ((1,), (0,))) * row_gate
    mixture = from_planes(*give_back(expert_out), 0, grad_planes[E - 1])
    mixture = jnp.einsum("kst,ksd->td", select, after(mixture, turned_out), preferred_element_type=F32)
    layer_out = swap((hidden + mixture).astype(BF16)).astype(F32)
    dboth = jnp.stack(
        [
            (dgate_pre.astype(F32) * row_scale).astype(BF16),
            (dup_pre.astype(F32) * row_scale).astype(BF16),
        ],
        axis=1,
    )
    up_grad = jnp.einsum(
        "rd,rkf->dkf", expert_rows, after(dboth, turned_out), preferred_element_type=F32
    )

    return (
        layer_out,
        stream_grad,
        gain_one_grad,
        router_one_grad.T,
        kv_grad,
        query_grad,
        output_grad,
        mine[0],
        mine[1:5].T,
        up_grad[None],
        down_grad[None],
    )


def solution(mesh):
    in_specs = (
        P("wide", "narrow"),
        P("wide", "narrow"),
        P("wide"),
        P("wide", None),
        P(None, "wide", "narrow"),
        P(None, "wide", "narrow"),
        P(None, "wide", "narrow"),
        P("wide"),
        P("wide", None),
        P("wide", None, None, "narrow"),
        P("wide", "narrow", None),
        P("wide", None),
        P("wide", None),
        P("wide", None),
    )
    out_specs = (
        P("wide", "narrow"),
        P("wide", "narrow"),
        P("wide"),
        P("wide", None),
        P(None, "wide", "narrow"),
        P(None, "wide", "narrow"),
        P(None, "wide", "narrow"),
        P("wide"),
        P("wide", None),
        P("wide", None, None, "narrow"),
        P("wide", "narrow", None),
    )
    return jax.shard_map(local, mesh=mesh, in_specs=in_specs, out_specs=out_specs, check_vma=False)
```

profile of v0, /device:TPU:2, one launch (start us, length us, event | category | flops | bytes accessed | tf_op | source)
XLA Modules:
  0.0 429.9 jit_solution(9384875390577801455)
XLA Ops:
  53.0 10.8 %collective-permute-done.13.refs_3_.refs_8_ = bf16[4,256,512]{2,1,0:T(8,128)(2,1)} collective-permute-done((bf16[4,256,512]{2,1,0:T(8,128)(2,1)}, bf16[4,256,512]{2,1,0:T(8,128)(2,1)}, u32[]{:S(2)}, u32[]{:S(2)}) %collective-permute-start.13) | collective-permute-done | bytes 1048608 | tf_op jit(solution)/shard_map/ppermute | solution.py:459
  83.1 12.5 %collective-permute-done.15.refs_5_ = bf16[2,128,512]{2,1,0:T(8,128)(2,1)} collective-permute-done((bf16[2,128,512]{2,1,0:T(8,128)(2,1)}, bf16[2,128,512]{2,1,0:T(8,128)(2,1)}, u32[]{:S(2)}, u32[]{:S(2)}) %collective-permute-start.15) | collective-permute-done | bytes 262176 | tf_op jit(solution)/shard_map/ppermute | solution.py:456
  95.5 5.4 %attention.1 = (bf16[4,128,512]{2,1,0:T(8,128)(2,1)}, f32[4,256,128]{2,1,0:T(8,128)}, bf16[2,128,512]{2,1,0:T(8,128)(2,1)}, bf16[2,128,512]{2,1,0:T(8,128)(2,1)}) custom-call(s32[4]{0:T(128)} %bitcast.271, f32[2,128,512]{2,1,0:T(8,128)} %get-tuple-element.90.own_kv, bf16[2,128,512]{2,1,0:T(8,128)(2,1)} %copy-done.29, bf16[2,128,512]{2,1,0:T(8,128)(2,1)} %copy-done.30, ...), custom_call_target="tpu_custom_call" | custom-call | flops 1 | bytes 1 | tf_op jit(solution)/shard_map/attention/pallas_call | solution.py:52
  101.5 7.0 %collective-permute-start.21 = (bf16[2,128,512]{2,1,0:T(8,128)(2,1)}, bf16[2,128,512]{2,1,0:T(8,128)(2,1)}, u32[]{:S(2)}, u32[]{:S(2)}) collective-permute-start(bf16[2,128,512]{2,1,0:T(8,128)(2,1)} %get-tuple-element.101.refs_0_), channel_id=1, source_target_pairs={{0,16},{4,20},{8,24},{12,28},{16,0},{20,4},{24,8},{28,12},{1,17},{... | collective-permute-start | bytes 786440 | tf_op jit(solution)/shard_map/ppermute | solution.py:456
  112.1 16.1 %collective-permute-done.21.refs_2_ = bf16[2,128,512]{2,1,0:T(8,128)(2,1)} collective-permute-done((bf16[2,128,512]{2,1,0:T(8,128)(2,1)}, bf16[2,128,512]{2,1,0:T(8,128)(2,1)}, u32[]{:S(2)}, u32[]{:S(2)}) %collective-permute-start.21) | collective-permute-done | bytes 262176 | tf_op jit(solution)/shard_map/ppermute | solution.py:456
  139.8 16.1 %collective-permute-done.25.other = bf16[128,512]{1,0:T(8,128)(2,1)} collective-permute-done((bf16[128,512]{1,0:T(8,128)(2,1)S(1)}, bf16[128,512]{1,0:T(8,128)(2,1)}, u32[]{:S(2)}, u32[]{:S(2)}) %collective-permute-start.25) | collective-permute-done | bytes 131104 | tf_op jit(solution)/shard_map/ppermute | solution.py:462
  165.0 5.4 %collective-permute-done.27.refs_2_ = bf16[80,640]{1,0:T(8,128)(2,1)} collective-permute-done((bf16[80,640]{1,0:T(8,128)(2,1)}, bf16[80,640]{1,0:T(8,128)(2,1)}, u32[]{:S(2)}, u32[]{:S(2)}) %collective-permute-start.27) | collective-permute-done | bytes 102432 | tf_op jit(solution)/shard_map/ppermute | solution.py:456
  181.2 12.8 %collective-permute-done.30 = bf16[2,80,2176]{2,1,0:T(8,128)(2,1)S(1)} collective-permute-done((bf16[2,80,2176]{2,1,0:T(8,128)(2,1)S(1)}, bf16[2,80,2176]{2,1,0:T(8,128)(2,1)S(1)}, u32[]{:S(2)}, u32[]{:S(2)}) %collective-permute-start.30) | collective-permute-done | bytes 696352 | tf_op jit(solution)/shard_map/ppermute | solution.py:462
  199.6 4.8 %fusion.11 = f32[2,640,704]{1,2,0:T(8,128)S(1)} fusion(bf16[1,2048,2,704]{1,3,2,0:T(8,128)(2,1)S(1)} %bitcast.273, bf16[640,2176]{1,0:T(8,128)(2,1)S(1)} %bitcast.218), kind=kOutput, calls=%fused_computation.29 | convolution fusion | flops 3690987520 | bytes 11993088 | tf_op jit(solution)/shard_map/rd,dkf->krf/dot_general | solution.py:680
  214.0 5.1 %collective-permute-start.36 = (f32[8,128]{1,0:T(8,128)S(1)}, f32[8,128]{1,0:T(8,128)S(1)}, u32[]{:S(2)}, u32[]{:S(2)}) collective-permute-start(f32[8,128]{1,0:T(8,128)S(1)} %copy-done.71), channel_id=1, source_target_pairs={{0,8},{4,12},{8,0},{12,4},{16,24},{20,28},{24,16},{28,20},{1,9},{5... | collective-permute-start | bytes 12296 | tf_op jit(solution)/shard_map/ppermute | solution.py:456
  232.4 9.7 %collective-permute-done.45 = bf16[2,80,2176]{2,1,0:T(8,128)(2,1)S(1)} collective-permute-done((bf16[2,80,2176]{2,1,0:T(8,128)(2,1)S(1)}, bf16[2,80,2176]{2,1,0:T(8,128)(2,1)S(1)}, u32[]{:S(2)}, u32[]{:S(2)}) %collective-permute-start.45) | collective-permute-done | bytes 696352 | tf_op jit(solution)/shard_map/ppermute | solution.py:462
  244.7 5.2 %collective-permute-done.46.got = bf16[80,2176]{1,0:T(8,128)(2,1)S(1)} collective-permute-done((bf16[80,2176]{1,0:T(8,128)(2,1)S(1)}, bf16[80,2176]{1,0:T(8,128)(2,1)S(1)}, u32[]{:S(2)}, u32[]{:S(2)}) %collective-permute-start.46) | collective-permute-done | bytes 348192 | tf_op jit(solution)/shard_map/ppermute | solution.py:459
  286.8 4.8 %output_grad.1 = (f32[4,256,512]{2,1,0:T(8,128)}, bf16[4,256,512]{2,1,0:T(8,128)(2,1)}) custom-call(s32[4]{0:T(128)} %pad_add_fusion.at, bf16[512,512]{1,0:T(8,128)(2,1)} %get-tuple-element.127.rows, bf16[4,512,512]{2,1,0:T(8,128)(2,1)} %get-tuple-element.128.other), custom_call_target="tpu_custom_call" | custom-call | flops 1 | bytes 1 | tf_op jit(solution)/shard_map/output_grad/pallas_call | solution.py:52
  291.6 7.0 %fusion.99 = f32[704,2048]{1,0:T(8,128)} fusion(bf16[640,704]{0,1:T(8,128)(2,1)} %get-tuple-element.130, bf16[640,2048]{1,0:T(8,128)(2,1)} %bitcast.227), kind=kOutput, calls=%fused_computation.215 | convolution fusion | flops 1845493760 | bytes 9289728 | tf_op jit(solution)/shard_map/dot_general | solution.py:22
  298.6 5.5 %collective-permute-done.54.refs_1_ = bf16[2,128,512]{2,1,0:T(8,128)(2,1)S(1)} collective-permute-done((bf16[2,128,512]{2,1,0:T(8,128)(2,1)}, bf16[2,128,512]{2,1,0:T(8,128)(2,1)S(1)}, u32[]{:S(2)}, u32[]{:S(2)}) %collective-permute-start.54) | collective-permute-done | bytes 262176 | tf_op jit(solution)/shard_map/ppermute | solution.py:456
  304.8 5.1 %attention_back.1 = (bf16[4,128,512]{2,1,0:T(8,128)(2,1)}, f32[8,128]{1,0:T(8,128)}) custom-call(s32[4]{0:T(128)} %pad_add_fusion.at, f32[2,128,512]{2,1,0:T(8,128)} %get-tuple-element.131.own, bf16[2,128,512]{2,1,0:T(8,128)(2,1)} %copy-done.31, bf16[2,128,512]{2,1,0:T(8,128)(2,1)} %copy-done.32, bf16[2,128,512]{2,1,0:T(8,128)(2,1)} %collective-permute-done.55.refs_2_, ...), custom_call_target="tpu_custom_call" | custom-call | flops 1 | bytes 1 | tf_op jit(solution)/shard_map/attention_back/pallas_call | solution.py:52
  316.2 5.6 %collective-permute-start.61 = (bf16[4,128,512]{2,1,0:T(8,128)(2,1)S(1)}, bf16[4,128,512]{2,1,0:T(8,128)(2,1)S(1)}, u32[]{:S(2)}, u32[]{:S(2)}) collective-permute-start(bf16[4,128,512]{2,1,0:T(8,128)(2,1)S(1)} %copy-done.12), channel_id=1, source_target_pairs={{0,16},{4,20},{8,24},{12,28},{16,0},{20,4},{24,8},{28,12},{1,17},{... | collective-permute-start | bytes 1572872 | tf_op jit(solution)/shard_map/ppermute | solution.py:456
  325.8 12.7 %collective-permute-done.62 = bf16[4,256,512]{2,1,0:T(8,128)(2,1)S(1)} collective-permute-done((bf16[4,256,512]{2,1,0:T(8,128)(2,1)S(1)}, bf16[4,256,512]{2,1,0:T(8,128)(2,1)S(1)}, u32[]{:S(2)}, u32[]{:S(2)}) %collective-permute-start.62) | collective-permute-done | bytes 1048608 | tf_op jit(solution)/shard_map/ppermute | solution.py:459
  338.4 8.1 %collective-permute-start.65 = (f32[4,512]{1,0:T(4,128)S(1)}, f32[4,512]{1,0:T(4,128)S(1)}, u32[]{:S(2)}, u32[]{:S(2)}) collective-permute-start(f32[4,512]{1,0:T(4,128)S(1)} %fusion.48), channel_id=1, source_target_pairs={{0,0},{1,8},{2,16},{3,24},{4,4},{5,12},{6,20},{7,28},{8,1},{9,9},{... | collective-permute-start | bytes 24584 | tf_op jit(solution)/shard_map/ppermute | solution.py:470
  348.2 20.0 %collective-permute-done.65 = f32[4,512]{1,0:T(4,128)S(1)} collective-permute-done((f32[4,512]{1,0:T(4,128)S(1)}, f32[4,512]{1,0:T(4,128)S(1)}, u32[]{:S(2)}, u32[]{:S(2)}) %collective-permute-start.65) | collective-permute-done | bytes 8224 | tf_op jit(solution)/shard_map/ppermute | solution.py:470
  369.2 5.3 %query_grad.1 = (bf16[4,512,512]{2,1,0:T(8,128)(2,1)}, f32[4,256,512]{2,1,0:T(8,128)}, bf16[4,256,512]{2,1,0:T(8,128)(2,1)}) custom-call(s32[4]{0:T(128)} %pad_add_fusion.at, bf16[512,512]{1,0:T(8,128)(2,1)} %get-tuple-element.94.refs_0_.rows, f32[512,8]{1,0:T(8,128)} %get-tuple-element.95.refs_1_.refs_4_.hot, ...), custom_call_target="tpu_custom_call" | custom-call | flops 1 | bytes 1 | tf_op jit(solution)/shard_map/query_grad/pallas_call | solution.py:52
  383.4 6.0 %input.1 = (bf16[2,512,512]{2,1,0:T(8,128)(2,1)}, f32[128,512]{1,0:T(8,128)}, f32[128,512]{1,0:T(8,128)}, bf16[2,128,512]{2,1,0:T(8,128)(2,1)}) custom-call(s32[4]{0:T(128)} %pad_add_fusion.at, bf16[4,128,512]{2,1,0:T(8,128)(2,1)} %get-tuple-element.150.refs_0_, bf16[4,128,512]{2,1,0:T(8,128)(2,1)} %copy-done.14, bf16[4,128,512]{2,1,0:T(8,128)(2,1)} %copy-done.13, ...), custom_call_target="tpu_custom_call" | custom-call | flops 1 | bytes 1 | tf_op jit(solution)/shard_map/input/pallas_call | solution.py:52
  401.4 6.2 %collective-permute-start.70 = (bf16[128,512]{1,0:T(8,128)(2,1)S(1)}, bf16[128,512]{1,0:T(8,128)(2,1)S(1)}, u32[]{:S(2)}, u32[]{:S(2)}) collective-permute-start(bf16[128,512]{1,0:T(8,128)(2,1)S(1)} %multiply_add_fusion), channel_id=1, source_target_pairs={{0,0},{1,8},{2,16},{3,24},{4,4},{5,12},{6,20},{7,28},{8,1},{9,9},{... | collective-permute-start | bytes 393224 | tf_op jit(solution)/shard_map/ppermute | solution.py:470
  412.9 7.4 %convolution_bitcast_fusion = f32[1,2048,2,704]{1,3,2,0:T(8,128)} fusion(bf16[640,2,704]{0,2,1:T(8,128)(2,1)S(1)} %copy-done.15, bf16[640,2176]{1,0:T(8,128)(2,1)S(1)} %bitcast.219), kind=kOutput, calls=%fused_computation.10 | convolution fusion | flops 3690987520 | bytes 15958016 | tf_op jit(solution)/shard_map/rd,rkf->dkf/dot_general | solution.py:846
  (418 shorter events, 223.3 us)
Async XLA Ops:
  5.7 29.5 %collective-permute-start = (bf16[128,512]{1,0:T(8,128)(2,1)}, bf16[128,512]{1,0:T(8,128)(2,1)S(1)}, u32[]{:S(2)}, u32[]{:S(2)}) collective-permute-start(bf16[128,512]{1,0:T(8,128)(2,1)} %param.14), channel_id=1, source_target_pairs={{0,0},{1,8},{2,16},{3,24},{4,4},{5,12},{6,20},{7,28},{8,1},{9,9},{... | collective-permute-start | bytes 393224 | tf_op jit(solution)/shard_map/ppermute | solution.py:470
  29.0 34.9 %collective-permute-start.13 = (bf16[4,256,512]{2,1,0:T(8,128)(2,1)}, bf16[4,256,512]{2,1,0:T(8,128)(2,1)}, u32[]{:S(2)}, u32[]{:S(2)}) collective-permute-start(bf16[4,256,512]{2,1,0:T(8,128)(2,1)} %refs_7_.1), channel_id=1, source_target_pairs={{0,4},{4,0},{8,12},{12,8},{16,20},{20,16},{24,28},{28,24},{1,5},{5... | collective-permute-start | bytes 3145736 | tf_op jit(solution)/shard_map/ppermute | solution.py:459
  41.6 66.9 %collective-permute-start.23 = (bf16[4,256,512]{2,1,0:T(8,128)(2,1)}, bf16[4,256,512]{2,1,0:T(8,128)(2,1)}, u32[]{:S(2)}, u32[]{:S(2)}) collective-permute-start(bf16[4,256,512]{2,1,0:T(8,128)(2,1)} %refs_5_.6), channel_id=1, source_target_pairs={{0,4},{4,0},{8,12},{12,8},{16,20},{20,16},{24,28},{28,24},{1,5},{5... | collective-permute-start | bytes 3145736 | tf_op jit(solution)/shard_map/ppermute | solution.py:459
  48.4 22.6 %collective-permute-start.6 = (bf16[2,128,512]{2,1,0:T(8,128)(2,1)}, bf16[2,128,512]{2,1,0:T(8,128)(2,1)S(1)}, u32[]{:S(2)}, u32[]{:S(2)}) collective-permute-start(bf16[2,128,512]{2,1,0:T(8,128)(2,1)} %get-tuple-element.91), channel_id=1, source_target_pairs={{0,8},{4,12},{8,0},{12,4},{16,24},{20,28},{24,16},{28,20},{1,9},{5... | collective-permute-start | bytes 786440 | tf_op jit(solution)/shard_map/ppermute | solution.py:456
  49.0 23.7 %collective-permute-start.7 = (bf16[2,128,512]{2,1,0:T(8,128)(2,1)}, bf16[2,128,512]{2,1,0:T(8,128)(2,1)S(1)}, u32[]{:S(2)}, u32[]{:S(2)}) collective-permute-start(bf16[2,128,512]{2,1,0:T(8,128)(2,1)} %get-tuple-element.92), channel_id=1, source_target_pairs={{0,16},{4,20},{8,24},{12,28},{16,0},{20,4},{24,8},{28,12},{1,17},{... | collective-permute-start | bytes 786440 | tf_op jit(solution)/shard_map/ppermute | solution.py:456
  51.0 19.9 %collective-permute-start.38 = (bf16[80,512]{1,0:T(8,128)(2,1)}, bf16[80,512]{1,0:T(8,128)(2,1)S(1)}, u32[]{:S(2)}, u32[]{:S(2)}) collective-permute-start(bf16[80,512]{1,0:T(8,128)(2,1)} %get-tuple-element.205), channel_id=1, source_target_pairs={{0,8},{4,12},{8,0},{12,4},{16,24},{20,28},{24,16},{28,20},{1,9},{5... | collective-permute-start | bytes 245768 | tf_op jit(solution)/shard_map/ppermute | solution.py:456
  71.0 24.5 %collective-permute-start.15 = (bf16[2,128,512]{2,1,0:T(8,128)(2,1)}, bf16[2,128,512]{2,1,0:T(8,128)(2,1)}, u32[]{:S(2)}, u32[]{:S(2)}) collective-permute-start(bf16[2,128,512]{2,1,0:T(8,128)(2,1)} %get-tuple-element.98), channel_id=1, source_target_pairs={{0,16},{4,20},{8,24},{12,28},{16,0},{20,4},{24,8},{28,12},{1,17},{... | collective-permute-start | bytes 786440 | tf_op jit(solution)/shard_map/ppermute | solution.py:456
  72.7 22.8 %collective-permute-start.16 = (bf16[2,128,512]{2,1,0:T(8,128)(2,1)}, bf16[2,128,512]{2,1,0:T(8,128)(2,1)}, u32[]{:S(2)}, u32[]{:S(2)}) collective-permute-start(bf16[2,128,512]{2,1,0:T(8,128)(2,1)} %get-tuple-element.99), channel_id=1, source_target_pairs={{0,24},{4,28},{8,16},{12,20},{16,8},{20,12},{24,0},{28,4},{1,25},{... | collective-permute-start | bytes 786440 | tf_op jit(solution)/shard_map/ppermute | solution.py:456
  78.5 54.4 %collective-permute-start.41 = (bf16[80,2048]{1,0:T(8,128)(2,1)}, bf16[80,2048]{1,0:T(8,128)(2,1)S(1)}, u32[]{:S(2)}, u32[]{:S(2)}) collective-permute-start(bf16[80,2048]{1,0:T(8,128)(2,1)} %join.1), channel_id=1, source_target_pairs={{0,4},{4,0},{8,12},{12,8},{16,20},{20,16},{24,28},{28,24},{1,5},{5... | collective-permute-start | bytes 983048 | tf_op jit(solution)/shard_map/ppermute | solution.py:459
  101.5 26.7 %collective-permute-start.21 = (bf16[2,128,512]{2,1,0:T(8,128)(2,1)}, bf16[2,128,512]{2,1,0:T(8,128)(2,1)}, u32[]{:S(2)}, u32[]{:S(2)}) collective-permute-start(bf16[2,128,512]{2,1,0:T(8,128)(2,1)} %get-tuple-element.101.refs_0_), channel_id=1, source_target_pairs={{0,16},{4,20},{8,24},{12,28},{16,0},{20,4},{24,8},{28,12},{1,17},{... | collective-permute-start | bytes 786440 | tf_op jit(solution)/shard_map/ppermute | solution.py:456
  108.6 19.7 %collective-permute-start.20 = (bf16[2,128,512]{2,1,0:T(8,128)(2,1)}, bf16[2,128,512]{2,1,0:T(8,128)(2,1)}, u32[]{:S(2)}, u32[]{:S(2)}) collective-permute-start(bf16[2,128,512]{2,1,0:T(8,128)(2,1)} %get-tuple-element.101.refs_0_), channel_id=1, source_target_pairs={{0,8},{4,12},{8,0},{12,4},{16,24},{20,28},{24,16},{28,20},{1,9},{5... | collective-permute-start | bytes 786440 | tf_op jit(solution)/shard_map/ppermute | solution.py:456
  135.6 38.9 %collective-permute-start.42 = (bf16[2,80,2048]{2,1,0:T(8,128)(2,1)}, bf16[2,80,2048]{2,1,0:T(8,128)(2,1)}, u32[]{:S(2)}, u32[]{:S(2)}) collective-permute-start(bf16[2,80,2048]{2,1,0:T(8,128)(2,1)} %get-tuple-element.200), channel_id=1, source_target_pairs={{0,2},{1,3},{2,0},{3,1},{4,6},{5,7},{6,4},{7,5},{8,10},{9,11},{10,... | collective-permute-start | bytes 1966088 | tf_op jit(solution)/shard_map/ppermute | solution.py:462
  136.4 19.5 %collective-permute-start.25 = (bf16[128,512]{1,0:T(8,128)(2,1)S(1)}, bf16[128,512]{1,0:T(8,128)(2,1)}, u32[]{:S(2)}, u32[]{:S(2)}) collective-permute-start(bf16[128,512]{1,0:T(8,128)(2,1)S(1)} %fusion.54), channel_id=1, source_target_pairs={{0,2},{1,3},{2,0},{3,1},{4,6},{5,7},{6,4},{7,5},{8,10},{9,11},{10,... | collective-permute-start | bytes 393224 | tf_op jit(solution)/shard_map/ppermute | solution.py:462
  279.7 31.2 %collective-permute-start.33 = (bf16[2,80,2048]{2,1,0:T(8,128)(2,1)}, bf16[2,80,2048]{2,1,0:T(8,128)(2,1)}, u32[]{:S(2)}, u32[]{:S(2)}) collective-permute-start(bf16[2,80,2048]{2,1,0:T(8,128)(2,1)} %fusion.35), channel_id=1, source_target_pairs={{0,2},{1,3},{2,0},{3,1},{4,6},{5,7},{6,4},{7,5},{8,10},{9,11},{10,... | collective-permute-start | bytes 1966088 | tf_op jit(solution)/shard_map/ppermute | solution.py:462
  284.1 20.1 %collective-permute-start.54 = (bf16[2,128,512]{2,1,0:T(8,128)(2,1)}, bf16[2,128,512]{2,1,0:T(8,128)(2,1)S(1)}, u32[]{:S(2)}, u32[]{:S(2)}) collective-permute-start(bf16[2,128,512]{2,1,0:T(8,128)(2,1)} %get-tuple-element.125), channel_id=1, source_target_pairs={{0,16},{4,20},{8,24},{12,28},{16,0},{20,4},{24,8},{28,12},{1,17},{... | collective-permute-start | bytes 786440 | tf_op jit(solution)/shard_map/ppermute | solution.py:456
  284.7 19.4 %collective-permute-start.55 = (bf16[2,128,512]{2,1,0:T(8,128)(2,1)}, bf16[2,128,512]{2,1,0:T(8,128)(2,1)}, u32[]{:S(2)}, u32[]{:S(2)}) collective-permute-start(bf16[2,128,512]{2,1,0:T(8,128)(2,1)} %get-tuple-element.126), channel_id=1, source_target_pairs={{0,24},{4,28},{8,16},{12,20},{16,8},{20,12},{24,0},{28,4},{1,25},{... | collective-permute-start | bytes 786440 | tf_op jit(solution)/shard_map/ppermute | solution.py:456
  312.4 26.1 %collective-permute-start.62 = (bf16[4,256,512]{2,1,0:T(8,128)(2,1)S(1)}, bf16[4,256,512]{2,1,0:T(8,128)(2,1)S(1)}, u32[]{:S(2)}, u32[]{:S(2)}) collective-permute-start(bf16[4,256,512]{2,1,0:T(8,128)(2,1)S(1)} %copy-done.77), channel_id=1, source_target_pairs={{0,4},{4,0},{8,12},{12,8},{16,20},{20,16},{24,28},{28,24},{1,5},{5... | collective-permute-start | bytes 3145736 | tf_op jit(solution)/shard_map/ppermute | solution.py:459
  314.8 61.7 %collective-permute-start.34 = (bf16[80,2048]{1,0:T(8,128)(2,1)}, bf16[80,2048]{1,0:T(8,128)(2,1)}, u32[]{:S(2)}, u32[]{:S(2)}) collective-permute-start(bf16[80,2048]{1,0:T(8,128)(2,1)} %fusion.45), channel_id=1, source_target_pairs={{0,4},{4,0},{8,12},{12,8},{16,20},{20,16},{24,28},{28,24},{1,5},{5... | collective-permute-start | bytes 983048 | tf_op jit(solution)/shard_map/ppermute | solution.py:459
  316.2 52.0 %collective-permute-start.61 = (bf16[4,128,512]{2,1,0:T(8,128)(2,1)S(1)}, bf16[4,128,512]{2,1,0:T(8,128)(2,1)S(1)}, u32[]{:S(2)}, u32[]{:S(2)}) collective-permute-start(bf16[4,128,512]{2,1,0:T(8,128)(2,1)S(1)} %copy-done.12), channel_id=1, source_target_pairs={{0,16},{4,20},{8,24},{12,28},{16,0},{20,4},{24,8},{28,12},{1,17},{... | collective-permute-start | bytes 1572872 | tf_op jit(solution)/shard_map/ppermute | solution.py:456
  321.8 46.4 %collective-permute-start.60 = (bf16[4,128,512]{2,1,0:T(8,128)(2,1)S(1)}, bf16[4,128,512]{2,1,0:T(8,128)(2,1)S(1)}, u32[]{:S(2)}, u32[]{:S(2)}) collective-permute-start(bf16[4,128,512]{2,1,0:T(8,128)(2,1)S(1)} %copy-done.12), channel_id=1, source_target_pairs={{0,8},{4,12},{8,0},{12,4},{16,24},{20,28},{24,16},{28,20},{1,9},{5... | collective-permute-start | bytes 1572872 | tf_op jit(solution)/shard_map/ppermute | solution.py:456
  321.8 46.4 %collective-permute-start.56 = (bf16[4,128,512]{2,1,0:T(8,128)(2,1)S(1)}, bf16[4,128,512]{2,1,0:T(8,128)(2,1)}, u32[]{:S(2)}, u32[]{:S(2)}) collective-permute-start(bf16[4,128,512]{2,1,0:T(8,128)(2,1)S(1)} %copy-done.12), channel_id=1, source_target_pairs={{0,24},{4,28},{8,16},{12,20},{16,8},{20,12},{24,0},{28,4},{1,25},{... | collective-permute-start | bytes 1572872 | tf_op jit(solution)/shard_map/ppermute | solution.py:456
  338.4 29.7 %collective-permute-start.65 = (f32[4,512]{1,0:T(4,128)S(1)}, f32[4,512]{1,0:T(4,128)S(1)}, u32[]{:S(2)}, u32[]{:S(2)}) collective-permute-start(f32[4,512]{1,0:T(4,128)S(1)} %fusion.48), channel_id=1, source_target_pairs={{0,0},{1,8},{2,16},{3,24},{4,4},{5,12},{6,20},{7,28},{8,1},{9,9},{... | collective-permute-start | bytes 24584 | tf_op jit(solution)/shard_map/ppermute | solution.py:470
  374.5 19.6 %collective-permute-start.68 = (bf16[4,256,512]{2,1,0:T(8,128)(2,1)}, bf16[4,256,512]{2,1,0:T(8,128)(2,1)}, u32[]{:S(2)}, u32[]{:S(2)}) collective-permute-start(bf16[4,256,512]{2,1,0:T(8,128)(2,1)} %get-tuple-element.149), channel_id=1, source_target_pairs={{0,4},{4,0},{8,12},{12,8},{16,20},{20,16},{24,28},{28,24},{1,5},{5... | collective-permute-start | bytes 3145736 | tf_op jit(solution)/shard_map/ppermute | solution.py:459
  401.4 26.1 %collective-permute-start.70 = (bf16[128,512]{1,0:T(8,128)(2,1)S(1)}, bf16[128,512]{1,0:T(8,128)(2,1)S(1)}, u32[]{:S(2)}, u32[]{:S(2)}) collective-permute-start(bf16[128,512]{1,0:T(8,128)(2,1)S(1)} %multiply_add_fusion), channel_id=1, source_target_pairs={{0,0},{1,8},{2,16},{3,24},{4,4},{5,12},{6,20},{7,28},{8,1},{9,9},{... | collective-permute-start | bytes 393224 | tf_op jit(solution)/shard_map/ppermute | solution.py:470
  (132 other events, 1359.0 us)
where the time goes:
time: 438 us; the launch traced here: 430 us
  waiting for transfers between devices  159 us (36%)
  starting transfers between devices  116 us (26%)
  Pallas kernels  60.7 us (14%)
  matrix products  37.9 us (9%)
  other arithmetic  37.5 us (9%)
  local copies, waits for them, and re-layouts  17 us (4%)
    pallas_call x16, Pallas kernels, run(): pl.pallas_call(body, out_shape=tuple(outs), in_specs=[pl.BlockSpec(memory...  60.7 us
    ppermute x32, starting transfers between devices, by_plane(): lax.ppermute(values, 'wide', [(i, i ^ k * subs) for i in range(wide_count)])  59.4 us
    ppermute x32, waiting for transfers between devices, by_plane(): lax.ppermute(values, 'wide', [(i, i ^ k * subs) for i in range(wide_count)])  54.4 us
    ppermute x24, waiting for transfers between devices, by_narrow(): lax.ppermute(values, 'narrow', [(i, i ^ k) for i in range(narrow_count)])  46.3 us
    ppermute x13, waiting for transfers between devices, by_sub(): return lax.ppermute(values, 'wide', [(i, i ^ k) for i in range(wide_count)])  38.2 us
    ppermute x6, starting transfers between devices, swap(): return lax.ppermute(values, ('wide', 'narrow'), pairs)  28.3 us
    ppermute x6, waiting for transfers between devices, swap(): return lax.ppermute(values, ('wide', 'narrow'), pairs)  20 us
    dot_general x8, matrix products, dot(): lax.dot_general(left, right, ((contract[0], contract[1]), ((), ())), prec...  19.5 us
  transfers between devices with their start and end apart: 75, of which 25 were waited for; matrix products, arithmetic and copies ran while one was open for 16% of the time, Pallas kernels for 13%

commit v1 on v0

--- a/solution.py
+++ b/solution.py
@@ -154,7 +154,8 @@
         rows, dmixed = refs[:E], refs[E]
         kv_parts = refs[E + 1 : E + 1 + subs]
         query_parts = refs[E + 1 + subs : E + 1 + 2 * subs]
-        dkv_all, keep_0, keep_2, send, weights = refs[E + 1 + 2 * subs :]
+        streams = refs[E + 1 + 2 * subs : 2 * E + 1 + 2 * subs]
+        dkv_all, gain_row, keep_0, keep_2, send, weights = refs[2 * E + 1 + 2 * subs :]
         place(weights, kv_parts, at[1])
         place(weights, query_parts, at[1], 2)
         for k in range(E):
@@ -163,6 +164,11 @@
         total = mul(dkv_all[0], weights[0], NT) + mul(dkv_all[1], weights[1], NT)
         for e in range(E):
             total = total + mul(dmixed[e], weights[2 + e], NT)
+        gain = jnp.zeros((1, total.shape[1]), F32)
+        for q in range(E):
+            part = total[q * TOK : (q + 1) * TOK] * streams[q][...].astype(F32)
+            gain = gain + jnp.sum(part, axis=0, keepdims=True)
+        gain_row[...] = gain
         fold_out(total, keep_0, keep_2, send)
 
     return body
@@ -469,16 +475,24 @@
                 pairs.append((w * narrow_count + n, (n * subs + y) * narrow_count + z))
         return lax.ppermute(values, ("wide", "narrow"), pairs)
 
+    def by_side(values, side):
+        pairs = []
+        for w in range(wide_count):
+            for n in range(narrow_count):
+                other = (w ^ 1, n) if (n & 1) == side else (w, n ^ 2)
+                pairs.append((w * narrow_count + n, other[0] * narrow_count + other[1]))
+        return lax.ppermute(values, ("wide", "narrow"), pairs)
+
     def gather_planes(values):
         return [values] + [by_plane(values, k) for k in range(1, E)]
 
     def exchange_planes(parts):
         return [parts[0]] + [by_plane(parts[k], k) for k in range(1, E)]
 
-    def gather_subs(values):
+    def gather_subs(values, *others):
         parts, bit = [values], 1
         while bit < subs:
-            parts = parts + [by_sub(one, bit) for one in parts]
+            parts = parts + [by_sub(after(one, *others) if others else one, bit) for one in parts]
             bit *= 2
         return parts
 
@@ -500,8 +514,8 @@
 
     def finish_subs(keep, send):
         bit = len(keep)
-        keep = [keep[j] + by_sub(send[j], bit).astype(F32) for j in range(bit)]
-        return reduce_subs(keep)
+        got = [by_sub(send[j], bit) for j in range(bit)]
+        return reduce_subs([keep[j] + got[j].astype(F32) for j in range(bit)]), got
 
     def sum_narrow(values):
         values = values + by_narrow(values, 2)
@@ -517,6 +531,8 @@
             values = values + by_sub(values, bit)
             bit *= 2
         return values
+
+    turned_stream = swap(stream)
 
     own_rows = jnp.concatenate(
         [attn_gain[None, :], attn_router.T, mlp_gain[None, :], mlp_router.T], axis=0
@@ -545,7 +561,7 @@
             shape((8, TOK), F32),
             shape((E, SLOTS, TOK), BF16),
         ],
-        [at, *gather_planes(jnp.stack(route_parts))],
+        [at, *after(gather_planes(jnp.stack(route_parts)), turned_stream)],
         [pltpu.VMEM((line_count, TOK), F32)] * 3 + [pltpu.VMEM((E, 8, TOK), F32)] * 2,
     )
     hot_one, keep_one = home_hot[0:8].reshape(TOPK, E, TOK), home_hot[8:10]
@@ -553,19 +569,20 @@
     hot_two_k = expert_hot.reshape(E, TOPK, TOK)
 
     kv_parts = gather_subs(key_value)
-    query_parts = gather_subs(query_proj)
+    query_parts = gather_subs(query_proj, kv_parts[-1])
+    out_parts = gather_subs(output_proj, query_parts[-1])
     home_stream = stream.astype(F32)
-    turned_stream = swap(stream)
     turned_grad = swap(out_grad)
 
     rows_all = E * TOK
     sent = shape((2, TOK, local_width), BF16)
     kept_own = shape((2, TOK, local_width), F32)
+    all_streams = gather_narrow(turned_stream)
     gained, *kv_blocks = run(
         "key_value",
         key_value_body(subs),
         [shape((rows_all, slice_width), BF16), kept_own] + [sent] * (E - 1),
-        [at, *gather_narrow(turned_stream), gain_one_plane[None], *kv_parts],
+        [at, *all_streams, gain_one_plane[None], *kv_parts],
         [
             pltpu.VMEM((2, slice_width, local_width), BF16),
             pltpu.VMEM((2, rows_all, local_width), F32),
@@ -576,15 +593,6 @@
         pltpu.VMEM((E, slice_width, local_width), BF16),
         pltpu.VMEM((TOPK, rows_all, local_width), F32),
     ]
-    query_blocks = run(
-        "query",
-        routed_body(subs, True),
-        [kept_own] + [sent] * (E - 1),
-        [at, gained, hot_cols, *query_parts],
-        routed_scratch,
-    )
-    query_blocks = exchange_planes(query_blocks)
-
     gained_home = home_stream * gain_one_home
     stats_one = jnp.concatenate(
         [
@@ -594,6 +602,15 @@
         axis=0,
     )
     stats_one = sum_narrow(stats_one)
+    query_blocks = run(
+        "query",
+        routed_body(subs, True),
+        [kept_own] + [sent] * (E - 1),
+        [at, after(gained, *kv_blocks[1:], stats_one), hot_cols, *query_parts],
+        routed_scratch,
+    )
+    query_blocks = exchange_planes(query_blocks)
+
     scale_one = lax.rsqrt(stats_one[0] / width + EPSILON)
     logits_one = stats_one[1:] * scale_one
 
@@ -605,6 +622,18 @@
     prob_one = gates(logits_one, hot_one)
     gate_one = prob_one * keep_one
 
+    def share(full):
+        size = full.shape[-1]
+        full = jnp.concatenate([full, by_side(full, 0)], axis=0)
+        got = by_side(full, 1)
+        full = jnp.concatenate([full, got], axis=0)
+        bit = 2
+        while bit < subs:
+            full = jnp.concatenate([full, by_sub(full, bit)], axis=0)
+            bit *= 2
+        return jnp.concatenate([full, by_narrow(full, 1)], axis=0).reshape(-1, size), got
+
+    picked = jnp.einsum("kst,td->ksd", select, turned_grad, preferred_element_type=F32).astype(BF16)
     token_rows = jnp.stack([scale_one, gate_one[0], gate_one[1]] + [scale_one] * 5)
     low, probs, context, gated = run(
         "attention",
@@ -618,8 +647,13 @@
         [doc_lengths[0], *kv_blocks, *query_blocks, token_rows],
     )
 
-    out_parts = gather_subs(output_proj)
-
+    (full,) = run(
+        "join",
+        join_body,
+        [shape((SLOTS, width), BF16)],
+        [at, *after(exchange_planes([picked[k] for k in range(E)]), gated)],
+    )
+    grad_rows, grad_got = share(full)
     folded = [shape((TOK, slice_width), F32), shape((TOK, slice_width), F32), shape((2, TOK, slice_width), BF16)]
     mixed, *attention = run(
         "output",
@@ -628,20 +662,6 @@
         [at, *gather_planes(gated), hot_cols, *out_parts],
         [pltpu.VMEM((E, slice_width, local_width), BF16)],
     )
-    def share(full):
-        full = jnp.stack(gather_subs(full))
-        two = jnp.stack([full, by_narrow(full, 2)])
-        one = by_narrow(two, 1)
-        return jnp.stack([two[0], one[0], two[1], one[1]]).reshape(-1, full.shape[-1])
-
-    picked = jnp.einsum("kst,td->ksd", select, turned_grad, preferred_element_type=F32).astype(BF16)
-    (full,) = run(
-        "join",
-        join_body,
-        [shape((SLOTS, width), BF16)],
-        [at, *exchange_planes([picked[k] for k in range(E)])],
-    )
-    grad_rows = share(full)
     weight_in = expert_in[0]
     weight_down = expert_down[0]
     dact_raw = dot(grad_rows, weight_down, ((1,), (1,)))
@@ -654,7 +674,7 @@
         [
             at,
             turned_stream,
-            *reduce_narrow(*attention),
+            *after(reduce_narrow(*attention), grad_got),
             gain_two_plane[None],
             jnp.pad(router_two_plane, ((0, 4), (0, 0))),
             mlp_cols,
@@ -667,12 +687,13 @@
         [shape((SLOTS, width + 128), BF16)],
         [at, *exchange_planes(picked)],
     )
-    full = share(full)
+    stats_two = sum_planes(stats_two)
+    full, _ = share(full)
+    full = after(full, stats_two)
     expert_rows = full[:, :width]
     row_pairs = full[:, width : width + 4].astype(F32)
     row_scale = row_pairs[:, 0:1] + row_pairs[:, 1:2]
     row_gate = row_pairs[:, 2:3] + row_pairs[:, 3:4]
-    stats_two = sum_planes(stats_two)
     scale_two = lax.rsqrt(stats_two[E] / width + EPSILON)
     logits_two = stats_two[:E] * scale_two
     prob_two = gates(logits_two, hot_two)
@@ -697,18 +718,20 @@
     )
 
     def give_back(rows):
-        shaped = rows.reshape(narrow_count, subs, SLOTS, -1)
-        low = shaped.astype(BF16)
-        got = by_narrow(jnp.stack([low[1], low[3]]), 1)
-        two = jnp.stack([shaped[0], shaped[2]]) + got.astype(F32)
-        one = two[0] + by_narrow(two[1].astype(BF16), 2).astype(F32)
-        parts, bit = [one[j] for j in range(subs)], subs // 2
+        half = rows.shape[0] // 2
+        rows = rows[:half] + by_narrow(rows[half:].astype(BF16), 1).astype(F32)
+        bit = subs // 2
         while bit > 1:
-            parts = [parts[j] + by_sub(parts[j + bit].astype(BF16), bit).astype(F32) for j in range(bit)]
+            half = rows.shape[0] // 2
+            rows = rows[:half] + by_sub(rows[half:].astype(BF16), bit).astype(F32)
             bit //= 2
-        return parts[0], by_sub(parts[1].astype(BF16), 1)
+        half = rows.shape[0] // 2
+        rows = rows[:half] + by_side(rows[half:].astype(BF16), 1).astype(F32)
+        return rows[:SLOTS], by_side(rows[SLOTS:].astype(BF16), 0)
 
     def from_planes(own, got, extra, last=None):
+        if last is not None:
+            own = after(own, last)
         pieces = run(
             "split",
             split_body(extra),
@@ -716,8 +739,6 @@
             [at, own, got],
             [pltpu.VMEM(own.shape, BF16)],
         )
-        if last is not None:
-            pieces = after(pieces, last)
         return jnp.stack(exchange_planes(pieces))
 
     returned = give_back(jnp.concatenate([drows, row_stats], axis=1))
@@ -771,9 +792,11 @@
     output_parts = run(
         "output_grad", weight_grad_body, weight_parts(E), [at, wide_grad, mixed], weight_scratch
     )
-    output_grad = weight_sum(output_parts)
+    expert_out = dot(activation, weight_down, ((1,), (0,))) * row_gate
+    mixture = give_back(expert_out)
+    output_grad, output_got = weight_sum(output_parts)
     gated_act = (activation.astype(F32) * row_gate).astype(BF16)
-    down_grad = dot(after(gated_act, dcontext_blocks[1]), grad_rows, ((0,), (0,)))
+    down_grad = dot(after(gated_act, dcontext_blocks[0]), grad_rows, ((0,), (0,)))
     grads_low, home_sums = run(
         "attention_back",
         attention_back_body,
@@ -788,32 +811,39 @@
         ],
     )
     grad_planes = gather_planes(grads_low)
-    home_sums = sum_narrow(home_sums)
+    dmixed, *query_grad_parts = run(
+        "query_grad",
+        query_grad_body,
+        [shape((E, rows_all, local_width), BF16)] + weight_parts(E),
+        [at, gained, hot_cols, *after(grad_planes, output_got)],
+        weight_scratch,
+    )
+    query_grad, query_got = weight_sum(query_grad_parts)
+    dkv_all, gain_row, *dnormed_one = run(
+        "input",
+        input_body(subs),
+        [shape((2, rows_all, local_width), BF16), shape((1, slice_width), F32)] + folded,
+        [
+            at,
+            *after(grad_planes, query_grad_parts[-1]),
+            dmixed,
+            *kv_parts,
+            *query_parts,
+            *all_streams,
+        ],
+        [pltpu.VMEM((2 + E, slice_width, local_width), BF16)],
+    )
+    home_sums = sum_narrow(after(home_sums, gain_row))
     dprob_one = keep_one * home_sums[:2]
     dlogit_one = gate_back(prob_one, dprob_one, hot_one)
     inner_one = home_sums[2] + jnp.sum(dlogit_one * logits_one, axis=0)
     dlogit_scaled = dlogit_one * scale_one
     router_term = swap(dot(dlogit_scaled, gained_home, ((1,), (0,)), PRECISE))
-    dmixed, *query_grad_parts = run(
-        "query_grad",
-        query_grad_body,
-        [shape((E, rows_all, local_width), BF16)] + weight_parts(E),
-        [at, gained, hot_cols, *after(grad_planes, output_grad, router_term)],
-        weight_scratch,
-    )
-    query_grad = weight_sum(query_grad_parts)
-    dkv_all, *dnormed_one = run(
-        "input",
-        input_body(subs),
-        [shape((2, rows_all, local_width), BF16)] + folded,
-        [at, *after(grad_planes, query_grad_parts[-1]), dmixed, *kv_parts, *query_parts],
-        [pltpu.VMEM((2 + E, slice_width, local_width), BF16)],
-    )
     kv_grad_parts = run(
         "key_value_grad", weight_grad_body, weight_parts(2), [at, gained, dkv_all], weight_scratch
     )
-    kv_grad = weight_sum(after(kv_grad_parts, query_grad))
-    keep, got, other = after(reduce_narrow(*dnormed_one), kv_grad_parts[-1], query_grad)
+    kv_grad, _ = weight_sum(after(kv_grad_parts, query_got))
+    keep, got, other = after(reduce_narrow(*dnormed_one), kv_grad_parts[-1], query_got)
     dnormed_one = keep + got[0].astype(F32) + other.astype(F32)
     turned_out = dhidden + dnormed_one * gain_one_plane
     home_out = swap(turned_out.astype(BF16)).astype(F32)
@@ -823,17 +853,15 @@
         - home_stream * (scale_one * scale_one * inner_one / width)[:, None]
     )
 
-    gain_term = jnp.sum(dnormed_one * turned_stream.astype(F32), axis=0)
-    small = jnp.concatenate([mlp_terms, gain_term[None], router_term], axis=0)
-    small = sum_subs(sum_narrow(small))
+    small = jnp.concatenate([mlp_terms, gain_row, router_term], axis=0)
+    small = sum_subs(sum_narrow(after(small, query_got)))
     mine = lax.dynamic_slice_in_dim(small, sub * shard_rows, shard_rows, 1)
     router_one_grad = mine[6:10]
     gain_one_grad = mine[5] + jnp.sum(
         router_one_grad * attn_router.T.astype(F32), axis=0
     ) / attn_gain.astype(F32)
 
-    expert_out = dot(activation, weight_down, ((1,), (0,))) * row_gate
-    mixture = from_planes(*give_back(expert_out), 0, grad_planes[E - 1])
+    mixture = from_planes(*mixture, 0, gain_row)
     mixture = jnp.einsum("kst,ksd->td", select, after(mixture, turned_out), preferred_element_type=F32)
     layer_out = swap((hidden + mixture).astype(BF16)).astype(F32)
     dboth = jnp.stack(

time: 438 us -> 430 us (0.982); the launches traced: 430 us -> 427 us
  starting transfers between devices: 116 us -> 94.7 us
  waiting for transfers between devices: 159 us -> 173 us
  matrix products: 37.9 us -> 48.8 us
  local copies, waits for them, and re-layouts: 17 us -> 10.8 us
    ppermute x32, waiting for transfers between devices: 54.4 us -> 109 us  [by_plane(): lax.ppermute(values, 'wide', [(i, i ^ k * subs) for i in range(wide_count)])]
    ppermute x13 -> x9, waiting for transfers between devices: 38.2 us -> 2.4 us  [by_sub(): return lax.ppermute(values, 'wide', [(i, i ^ k) for i in range(wide_count)])]
    ppermute x0 -> x8, waiting for transfers between devices: none -> 35.7 us  [by_side(): return lax.ppermute(values, ('wide', 'narrow'), pairs)]
    ppermute x24 -> x20, waiting for transfers between devices: 46.3 us -> 18.9 us  [by_narrow(): lax.ppermute(values, 'narrow', [(i, i ^ k) for i in range(narrow_count)])]
    ppermute x6, waiting for transfers between devices: 20 us -> 6.57 us  [swap(): return lax.ppermute(values, ('wide', 'narrow'), pairs)]
    dot_general x1, matrix products: 4.43 us -> 14.9 us  [local(): jnp.einsum('krf,dkf->rd', jnp.stack([dgate_pre, dup_pre]), weight_in, pre...]
    ppermute x24 -> x20, starting transfers between devices: 11.5 us -> 3.16 us  [by_narrow(): lax.ppermute(values, 'narrow', [(i, i ^ k) for i in range(narrow_count)])]
    ppermute x13 -> x9, starting transfers between devices: 16.5 us -> 8.98 us  [by_sub(): return lax.ppermute(values, 'wide', [(i, i ^ k) for i in range(wide_count)])]
  transfers between devices with their start and end apart: 75 -> 75, of which waited for: 25 -> 32; matrix products, arithmetic and copies ran while one was open for 16% -> 15% of each run, Pallas kernels for 13% -> 12%
where the time goes in v1:
time: 430 us; the launch traced here: 427 us
  waiting for transfers between devices  173 us (40%)
  starting transfers between devices  94.7 us (22%)
  Pallas kernels  60.9 us (14%)
  matrix products  48.8 us (11%)
  other arithmetic  37.1 us (9%)
  local copies, waits for them, and re-layouts  10.8 us (3%)
    ppermute x32, waiting for transfers between devices, by_plane(): lax.ppermute(values, 'wide', [(i, i ^ k * subs) for i in range(wide_count)])  109 us
    pallas_call x16, Pallas kernels, run(): pl.pallas_call(body, out_shape=tuple(outs), in_specs=[pl.BlockSpec(memory...  60.9 us
    ppermute x32, starting transfers between devices, by_plane(): lax.ppermute(values, 'wide', [(i, i ^ k * subs) for i in range(wide_count)])  54 us
    ppermute x8, waiting for transfers between devices, by_side(): return lax.ppermute(values, ('wide', 'narrow'), pairs)  35.7 us
    ppermute x6, starting transfers between devices, swap(): return lax.ppermute(values, ('wide', 'narrow'), pairs)  22.8 us
    dot_general x8, matrix products, dot(): lax.dot_general(left, right, ((contract[0], contract[1]), ((), ())), prec...  19.9 us
    ppermute x20, waiting for transfers between devices, by_narrow(): lax.ppermute(values, 'narrow', [(i, i ^ k) for i in range(narrow_count)])  18.9 us
    dot_general x1, matrix products, local(): jnp.einsum('krf,dkf->rd', jnp.stack([dgate_pre, dup_pre]), weight_in, pre...  14.9 us
  transfers between devices with their start and end apart: 75, of which 32 were waited for; matrix products, arithmetic and copies ran while one was open for 15% of the time, Pallas kernels for 12%

profile of v1, /device:TPU:2, one launch (start us, length us, event | category | flops | bytes accessed | tf_op | source)
XLA Modules:
  0.0 426.7 jit_solution(14362551151226819983)
XLA Ops:
  28.5 5.1 %collective-permute-start.15 = (bf16[2,8,128]{2,1,0:T(8,128)(2,1)S(1)}, bf16[2,8,128]{2,1,0:T(8,128)(2,1)S(1)}, u32[]{:S(2)}, u32[]{:S(2)}) collective-permute-start(bf16[2,8,128]{2,1,0:T(8,128)(2,1)S(1)} %pad_maximum_fusion.14.refs_0_), channel_id=1, source_target_pairs={{0,24},{4,28},{8,16},{12,20},{16,8},{20,12},{24,0},{28,4},{1,25},{... | collective-permute-start | bytes 12296 | tf_op jit(solution)/shard_map/ppermute | solution.py:462
  54.0 6.5 %collective-permute-done.6.refs_0_ = bf16[2,128,512]{2,1,0:T(8,128)(2,1)S(1)} collective-permute-done((bf16[2,128,512]{2,1,0:T(8,128)(2,1)}, bf16[2,128,512]{2,1,0:T(8,128)(2,1)S(1)}, u32[]{:S(2)}, u32[]{:S(2)}) %collective-permute-start.6) | collective-permute-done | bytes 262176 | tf_op jit(solution)/shard_map/ppermute | solution.py:462
  60.5 10.0 %collective-permute-done.7.refs_1_ = bf16[2,128,512]{2,1,0:T(8,128)(2,1)S(1)} collective-permute-done((bf16[2,128,512]{2,1,0:T(8,128)(2,1)}, bf16[2,128,512]{2,1,0:T(8,128)(2,1)S(1)}, u32[]{:S(2)}, u32[]{:S(2)}) %collective-permute-start.7) | collective-permute-done | bytes 262176 | tf_op jit(solution)/shard_map/ppermute | solution.py:462
  91.8 14.4 %collective-permute-done.18.refs_5_ = bf16[2,128,512]{2,1,0:T(8,128)(2,1)} collective-permute-done((bf16[2,128,512]{2,1,0:T(8,128)(2,1)}, bf16[2,128,512]{2,1,0:T(8,128)(2,1)}, u32[]{:S(2)}, u32[]{:S(2)}) %collective-permute-start.18) | collective-permute-done | bytes 262176 | tf_op jit(solution)/shard_map/ppermute | solution.py:462
  107.6 5.4 %attention.1 = (bf16[4,128,512]{2,1,0:T(8,128)(2,1)}, f32[4,256,128]{2,1,0:T(8,128)}, bf16[2,128,512]{2,1,0:T(8,128)(2,1)}, bf16[2,128,512]{2,1,0:T(8,128)(2,1)}) custom-call(s32[4]{0:T(128)} %bitcast.199, f32[2,128,512]{2,1,0:T(8,128)} %get-tuple-element.105.own_kv, bf16[2,128,512]{2,1,0:T(8,128)(2,1)} %copy-done.24, bf16[2,128,512]{2,1,0:T(8,128)(2,1)} %copy-done.25, ...), custom_call_target="tpu_custom_call" | custom-call | flops 1 | bytes 1 | tf_op jit(solution)/shard_map/attention/pallas_call | solution.py:52
  126.7 15.4 %collective-permute-done.21.refs_2_ = bf16[2,128,512]{2,1,0:T(8,128)(2,1)} collective-permute-done((bf16[2,128,512]{2,1,0:T(8,128)(2,1)}, bf16[2,128,512]{2,1,0:T(8,128)(2,1)}, u32[]{:S(2)}, u32[]{:S(2)}) %collective-permute-start.21) | collective-permute-done | bytes 262176 | tf_op jit(solution)/shard_map/ppermute | solution.py:462
  164.7 5.4 %collective-permute-done.33.refs_2_ = bf16[80,640]{1,0:T(8,128)(2,1)} collective-permute-done((bf16[80,640]{1,0:T(8,128)(2,1)}, bf16[80,640]{1,0:T(8,128)(2,1)}, u32[]{:S(2)}, u32[]{:S(2)}) %collective-permute-start.33) | collective-permute-done | bytes 102432 | tf_op jit(solution)/shard_map/ppermute | solution.py:462
  173.0 8.2 %collective-permute-done.35 = bf16[80,2176]{1,0:T(8,128)(2,1)S(1)} collective-permute-done((bf16[80,2176]{1,0:T(8,128)(2,1)}, bf16[80,2176]{1,0:T(8,128)(2,1)S(1)}, u32[]{:S(2)}, u32[]{:S(2)}) %collective-permute-start.35) | collective-permute-done | bytes 348192 | tf_op jit(solution)/shard_map/ppermute | solution.py:484
  183.7 9.7 %collective-permute-done.36 = bf16[160,2176]{1,0:T(8,128)(2,1)S(1)} collective-permute-done((bf16[160,2176]{1,0:T(8,128)(2,1)S(1)}, bf16[160,2176]{1,0:T(8,128)(2,1)S(1)}, u32[]{:S(2)}, u32[]{:S(2)}) %collective-permute-start.36) | collective-permute-done | bytes 696352 | tf_op jit(solution)/shard_map/ppermute | solution.py:484
  206.7 4.8 %fusion.17 = f32[2,640,704]{1,2,0:T(8,128)S(1)} fusion(bf16[1,2048,2,704]{1,3,2,0:T(8,128)(2,1)S(1)} %bitcast.201, bf16[640,2176]{1,0:T(8,128)(2,1)S(1)} %pad_maximum_fusion.1), kind=kOutput, calls=%fused_computation.32 | convolution fusion | flops 3690987520 | bytes 11993088 | tf_op jit(solution)/shard_map/rd,dkf->krf/dot_general | solution.py:701
  215.3 14.9 %fusion.4 = f32[640,2048]{1,0:T(8,128)S(1)} fusion(bf16[1,2048,2,704]{1,3,2,0:T(8,128)(2,1)S(1)} %bitcast.201, bf16[1,640,704]{1,2,0:T(8,128)(2,1)S(1)} %bitcast.163, bf16[1,640,704]{1,2,0:T(8,128)(2,1)S(1)} %bitcast.164), kind=kOutput, calls=%fused_computation.8 | convolution fusion | flops 3691888640 | bytes 12812288 | tf_op jit(solution)/shard_map/krf,dkf->rd/dot_general | solution.py:712
  234.3 11.0 %collective-permute-done.44 = bf16[160,2176]{1,0:T(8,128)(2,1)S(1)} collective-permute-done((bf16[160,2176]{1,0:T(8,128)(2,1)S(1)}, bf16[160,2176]{1,0:T(8,128)(2,1)S(1)}, u32[]{:S(2)}, u32[]{:S(2)}) %collective-permute-start.44) | collective-permute-done | bytes 696352 | tf_op jit(solution)/shard_map/ppermute | solution.py:484
  246.9 6.0 %collective-permute-done.45.got = bf16[80,2176]{1,0:T(8,128)(2,1)} collective-permute-done((bf16[80,2176]{1,0:T(8,128)(2,1)S(1)}, bf16[80,2176]{1,0:T(8,128)(2,1)}, u32[]{:S(2)}, u32[]{:S(2)}) %collective-permute-start.45) | collective-permute-done | bytes 348192 | tf_op jit(solution)/shard_map/ppermute | solution.py:484
  283.6 4.8 %output_grad.1 = (f32[4,256,512]{2,1,0:T(8,128)}, bf16[4,256,512]{2,1,0:T(8,128)(2,1)}) custom-call(s32[4]{0:T(128)} %pad_add_fusion.at, bf16[512,512]{1,0:T(8,128)(2,1)} %get-tuple-element.153.rows, bf16[4,512,512]{2,1,0:T(8,128)(2,1)} %get-tuple-element.154.other), custom_call_target="tpu_custom_call" | custom-call | flops 1 | bytes 1 | tf_op jit(solution)/shard_map/output_grad/pallas_call | solution.py:52
  288.8 6.8 %fusion.38 = f32[704,2048]{1,0:T(8,128)} fusion(bf16[640,704]{0,1:T(8,128)(2,1)} %get-tuple-element.156, bf16[320,2048]{1,0:T(8,128)(2,1)} %copy-done.57, bf16[160,2048]{1,0:T(8,128)(2,1)} %collective-permute-done.31, bf16[80,2048]{1,0:T(8,128)(2,1)} %copy-done.17, bf16[80,2048]{1,0:T(8,128)(2,1)S(1)} %copy-done.9), kind=kOutput, calls=%fused_computation.73 | convolution fusion | flops 1855979520 | bytes 9289728 | tf_op jit(solution)/shard_map/dot_general | solution.py:22
  295.6 6.7 %collective-permute-done.53.refs_1_ = bf16[2,128,512]{2,1,0:T(8,128)(2,1)} collective-permute-done((bf16[2,128,512]{2,1,0:T(8,128)(2,1)}, bf16[2,128,512]{2,1,0:T(8,128)(2,1)}, u32[]{:S(2)}, u32[]{:S(2)}) %collective-permute-start.53) | collective-permute-done | bytes 262176 | tf_op jit(solution)/shard_map/ppermute | solution.py:462
  302.3 5.1 %attention_back.1 = (bf16[4,128,512]{2,1,0:T(8,128)(2,1)}, f32[8,128]{1,0:T(8,128)}) custom-call(s32[4]{0:T(128)} %pad_add_fusion.at, f32[2,128,512]{2,1,0:T(8,128)} %get-tuple-element.157.own, bf16[2,128,512]{2,1,0:T(8,128)(2,1)} %collective-permute-done.52.refs_0_, bf16[2,128,512]{2,1,0:T(8,128)(2,1)} %collective-permute-done.53.refs_1_, ...), custom_call_target="tpu_custom_call" | custom-call | flops 1 | bytes 1 | tf_op jit(solution)/shard_map/attention_back/pallas_call | solution.py:52
  308.8 5.2 %collective-permute-start.56 = (bf16[4,128,512]{2,1,0:T(8,128)(2,1)}, bf16[4,128,512]{2,1,0:T(8,128)(2,1)}, u32[]{:S(2)}, u32[]{:S(2)}) collective-permute-start(bf16[4,128,512]{2,1,0:T(8,128)(2,1)} %get-tuple-element.170.refs_0_), channel_id=1, source_target_pairs={{0,16},{4,20},{8,24},{12,28},{16,0},{20,4},{24,8},{28,12},{1,17},{... | collective-permute-start | bytes 1572872 | tf_op jit(solution)/shard_map/ppermute | solution.py:462
  319.0 5.4 %collective-permute-done.57.refs_3_ = bf16[4,128,512]{2,1,0:T(8,128)(2,1)S(1)} collective-permute-done((bf16[4,128,512]{2,1,0:T(8,128)(2,1)}, bf16[4,128,512]{2,1,0:T(8,128)(2,1)S(1)}, u32[]{:S(2)}, u32[]{:S(2)}) %collective-permute-start.57) | collective-permute-done | bytes 524320 | tf_op jit(solution)/shard_map/ppermute | solution.py:462
  324.4 30.7 %collective-permute-done.56.refs_2_ = bf16[4,128,512]{2,1,0:T(8,128)(2,1)} collective-permute-done((bf16[4,128,512]{2,1,0:T(8,128)(2,1)}, bf16[4,128,512]{2,1,0:T(8,128)(2,1)}, u32[]{:S(2)}, u32[]{:S(2)}) %collective-permute-start.56) | collective-permute-done | bytes 524320 | tf_op jit(solution)/shard_map/ppermute | solution.py:462
  355.1 5.5 %query_grad.1 = (bf16[4,512,512]{2,1,0:T(8,128)(2,1)}, f32[4,256,512]{2,1,0:T(8,128)}, bf16[4,256,512]{2,1,0:T(8,128)(2,1)}) custom-call(s32[4]{0:T(128)} %pad_add_fusion.at, bf16[512,512]{1,0:T(8,128)(2,1)} %get-tuple-element.110.refs_0_.rows, f32[512,8]{1,0:T(8,128)} %get-tuple-element.115.refs_1_.refs_4_.hot, ...), custom_call_target="tpu_custom_call" | custom-call | flops 1 | bytes 1 | tf_op jit(solution)/shard_map/query_grad/pallas_call | solution.py:52
  360.6 6.2 %input.1 = (bf16[2,512,512]{2,1,0:T(8,128)(2,1)}, f32[1,512]{1,0:T(1,128)}, f32[128,512]{1,0:T(8,128)}, f32[128,512]{1,0:T(8,128)}, bf16[2,128,512]{2,1,0:T(8,128)(2,1)}) custom-call(s32[4]{0:T(128)} %pad_add_fusion.at, bf16[4,128,512]{2,1,0:T(8,128)(2,1)} %get-tuple-element.170.refs_0_, bf16[4,128,512]{2,1,0:T(8,128)(2,1)} %collective-permute-done.55.refs_1_, ...), custom_call_target="tpu_custom_call" | custom-call | flops 1 | bytes 1 | tf_op jit(solution)/shard_map/input/pallas_call | solution.py:52
  400.7 5.7 %collective-permute-start.66 = (bf16[128,512]{1,0:T(8,128)(2,1)S(1)}, bf16[128,512]{1,0:T(8,128)(2,1)S(1)}, u32[]{:S(2)}, u32[]{:S(2)}) collective-permute-start(bf16[128,512]{1,0:T(8,128)(2,1)S(1)} %fusion.33), channel_id=1, source_target_pairs={{0,0},{1,8},{2,16},{3,24},{4,4},{5,12},{6,20},{7,28},{8,1},{9,9},{... | collective-permute-start | bytes 393224 | tf_op jit(solution)/shard_map/ppermute | solution.py:476
  408.5 7.4 %convolution_bitcast_fusion = f32[1,2048,2,704]{1,3,2,0:T(8,128)} fusion(bf16[640,2,704]{0,2,1:T(8,128)(2,1)S(1)} %copy-done.15, bf16[640,2176]{1,0:T(8,128)(2,1)S(1)} %copy-done.8), kind=kOutput, calls=%fused_computation.6 | convolution fusion | flops 3690987520 | bytes 15958016 | tf_op jit(solution)/shard_map/rd,rkf->dkf/dot_general | solution.py:874
  (367 shorter events, 218.6 us)
Async XLA Ops:
  2.1 25.6 %collective-permute-start.12 = (bf16[8,128]{1,0:T(8,128)(2,1)}, bf16[8,128]{1,0:T(8,128)(2,1)}, u32[]{:S(2)}, u32[]{:S(2)}) collective-permute-start(bf16[8,128]{1,0:T(8,128)(2,1)} %get-tuple-element.235), channel_id=1, source_target_pairs={{0,4},{4,0},{8,12},{12,8},{16,20},{20,16},{24,28},{28,24},{1,5},{5... | collective-permute-start | bytes 6152 | tf_op jit(solution)/shard_map/ppermute | solution.py:465
  6.2 45.2 %collective-permute-start.26 = (bf16[128,512]{1,0:T(8,128)(2,1)}, bf16[128,512]{1,0:T(8,128)(2,1)}, u32[]{:S(2)}, u32[]{:S(2)}) collective-permute-start(bf16[128,512]{1,0:T(8,128)(2,1)} %param.15), channel_id=1, source_target_pairs={{0,0},{1,8},{2,16},{3,24},{4,4},{5,12},{6,20},{7,28},{8,1},{9,9},{... | collective-permute-start | bytes 393224 | tf_op jit(solution)/shard_map/ppermute | solution.py:476
  10.7 25.3 %collective-permute-start = (bf16[128,512]{1,0:T(8,128)(2,1)}, bf16[128,512]{1,0:T(8,128)(2,1)S(1)}, u32[]{:S(2)}, u32[]{:S(2)}) collective-permute-start(bf16[128,512]{1,0:T(8,128)(2,1)} %param.14), channel_id=1, source_target_pairs={{0,0},{1,8},{2,16},{3,24},{4,4},{5,12},{6,20},{7,28},{8,1},{9,9},{... | collective-permute-start | bytes 393224 | tf_op jit(solution)/shard_map/ppermute | solution.py:476
  13.9 21.5 %collective-permute-start.5 = (bf16[2,256,512]{2,1,0:T(8,128)(2,1)}, bf16[2,256,512]{2,1,0:T(8,128)(2,1)S(1)}, u32[]{:S(2)}, u32[]{:S(2)}) collective-permute-start(bf16[2,256,512]{2,1,0:T(8,128)(2,1)} %refs_5_.7), channel_id=1, source_target_pairs={{0,4},{4,0},{8,12},{12,8},{16,20},{20,16},{24,28},{28,24},{1,5},{5... | collective-permute-start | bytes 1572872 | tf_op jit(solution)/shard_map/ppermute | solution.py:465
  35.4 35.1 %collective-permute-start.16 = (bf16[4,256,512]{2,1,0:T(8,128)(2,1)}, bf16[4,256,512]{2,1,0:T(8,128)(2,1)}, u32[]{:S(2)}, u32[]{:S(2)}) collective-permute-start(bf16[4,256,512]{2,1,0:T(8,128)(2,1)} %refs_7_.1), channel_id=1, source_target_pairs={{0,4},{4,0},{8,12},{12,8},{16,20},{20,16},{24,28},{28,24},{1,5},{5... | collective-permute-start | bytes 3145736 | tf_op jit(solution)/shard_map/ppermute | solution.py:465
  49.0 21.5 %collective-permute-start.7 = (bf16[2,128,512]{2,1,0:T(8,128)(2,1)}, bf16[2,128,512]{2,1,0:T(8,128)(2,1)S(1)}, u32[]{:S(2)}, u32[]{:S(2)}) collective-permute-start(bf16[2,128,512]{2,1,0:T(8,128)(2,1)} %get-tuple-element.107), channel_id=1, source_target_pairs={{0,16},{4,20},{8,24},{12,28},{16,0},{20,4},{24,8},{28,12},{1,17},{... | collective-permute-start | bytes 786440 | tf_op jit(solution)/shard_map/ppermute | solution.py:462
  70.5 71.6 %collective-permute-start.23 = (bf16[4,256,512]{2,1,0:T(8,128)(2,1)}, bf16[4,256,512]{2,1,0:T(8,128)(2,1)}, u32[]{:S(2)}, u32[]{:S(2)}) collective-permute-start(bf16[4,256,512]{2,1,0:T(8,128)(2,1)} %refs_5_.6), channel_id=1, source_target_pairs={{0,4},{4,0},{8,12},{12,8},{16,20},{20,16},{24,28},{28,24},{1,5},{5... | collective-permute-start | bytes 3145736 | tf_op jit(solution)/shard_map/ppermute | solution.py:465
  81.1 25.1 %collective-permute-start.18 = (bf16[2,128,512]{2,1,0:T(8,128)(2,1)}, bf16[2,128,512]{2,1,0:T(8,128)(2,1)}, u32[]{:S(2)}, u32[]{:S(2)}) collective-permute-start(bf16[2,128,512]{2,1,0:T(8,128)(2,1)} %get-tuple-element.119), channel_id=1, source_target_pairs={{0,16},{4,20},{8,24},{12,28},{16,0},{20,4},{24,8},{28,12},{1,17},{... | collective-permute-start | bytes 786440 | tf_op jit(solution)/shard_map/ppermute | solution.py:462
  82.4 25.2 %collective-permute-start.19 = (bf16[2,128,512]{2,1,0:T(8,128)(2,1)}, bf16[2,128,512]{2,1,0:T(8,128)(2,1)}, u32[]{:S(2)}, u32[]{:S(2)}) collective-permute-start(bf16[2,128,512]{2,1,0:T(8,128)(2,1)} %get-tuple-element.120), channel_id=1, source_target_pairs={{0,24},{4,28},{8,16},{12,20},{16,8},{20,12},{24,0},{28,4},{1,25},{... | collective-permute-start | bytes 786440 | tf_op jit(solution)/shard_map/ppermute | solution.py:462
  83.9 29.1 %collective-permute-start.29 = (bf16[80,512]{1,0:T(8,128)(2,1)}, bf16[80,512]{1,0:T(8,128)(2,1)}, u32[]{:S(2)}, u32[]{:S(2)}) collective-permute-start(bf16[80,512]{1,0:T(8,128)(2,1)} %get-tuple-element.217), channel_id=1, source_target_pairs={{0,24},{4,28},{8,16},{12,20},{16,8},{20,12},{24,0},{28,4},{1,25},{... | collective-permute-start | bytes 245768 | tf_op jit(solution)/shard_map/ppermute | solution.py:462
  90.7 22.3 %collective-permute-start.28 = (bf16[80,512]{1,0:T(8,128)(2,1)}, bf16[80,512]{1,0:T(8,128)(2,1)}, u32[]{:S(2)}, u32[]{:S(2)}) collective-permute-start(bf16[80,512]{1,0:T(8,128)(2,1)} %get-tuple-element.218), channel_id=1, source_target_pairs={{0,16},{4,20},{8,24},{12,28},{16,0},{20,4},{24,8},{28,12},{1,17},{... | collective-permute-start | bytes 245768 | tf_op jit(solution)/shard_map/ppermute | solution.py:462
  118.3 23.8 %collective-permute-start.21 = (bf16[2,128,512]{2,1,0:T(8,128)(2,1)}, bf16[2,128,512]{2,1,0:T(8,128)(2,1)}, u32[]{:S(2)}, u32[]{:S(2)}) collective-permute-start(bf16[2,128,512]{2,1,0:T(8,128)(2,1)} %get-tuple-element.122.refs_0_), channel_id=1, source_target_pairs={{0,16},{4,20},{8,24},{12,28},{16,0},{20,4},{24,8},{28,12},{1,17},{... | collective-permute-start | bytes 786440 | tf_op jit(solution)/shard_map/ppermute | solution.py:462
  120.8 21.3 %collective-permute-start.20 = (bf16[2,128,512]{2,1,0:T(8,128)(2,1)}, bf16[2,128,512]{2,1,0:T(8,128)(2,1)}, u32[]{:S(2)}, u32[]{:S(2)}) collective-permute-start(bf16[2,128,512]{2,1,0:T(8,128)(2,1)} %get-tuple-element.122.refs_0_), channel_id=1, source_target_pairs={{0,8},{4,12},{8,0},{12,4},{16,24},{20,28},{24,16},{28,20},{1,9},{5... | collective-permute-start | bytes 786440 | tf_op jit(solution)/shard_map/ppermute | solution.py:462
  124.1 27.7 %collective-permute-start.31 = (bf16[160,2048]{1,0:T(8,128)(2,1)}, bf16[160,2048]{1,0:T(8,128)(2,1)}, u32[]{:S(2)}, u32[]{:S(2)}) collective-permute-start(bf16[160,2048]{1,0:T(8,128)(2,1)} %pad_maximum_fusion.7), channel_id=1, source_target_pairs={{0,2},{1,5},{2,0},{3,7},{4,6},{5,1},{6,4},{7,3},{8,10},{9,13},{10,... | collective-permute-start | bytes 1966088 | tf_op jit(solution)/shard_map/ppermute | solution.py:484
  269.6 44.5 %collective-permute-start.41 = (bf16[160,2048]{1,0:T(8,128)(2,1)}, bf16[160,2048]{1,0:T(8,128)(2,1)}, u32[]{:S(2)}, u32[]{:S(2)}) collective-permute-start(bf16[160,2048]{1,0:T(8,128)(2,1)} %slice.396), channel_id=1, source_target_pairs={{0,2},{1,5},{2,0},{3,7},{4,6},{5,1},{6,4},{7,3},{8,10},{9,13},{10,... | collective-permute-start | bytes 1966088 | tf_op jit(solution)/shard_map/ppermute | solution.py:484
  280.7 21.6 %collective-permute-start.53 = (bf16[2,128,512]{2,1,0:T(8,128)(2,1)}, bf16[2,128,512]{2,1,0:T(8,128)(2,1)}, u32[]{:S(2)}, u32[]{:S(2)}) collective-permute-start(bf16[2,128,512]{2,1,0:T(8,128)(2,1)} %get-tuple-element.151), channel_id=1, source_target_pairs={{0,16},{4,20},{8,24},{12,28},{16,0},{20,4},{24,8},{28,12},{1,17},{... | collective-permute-start | bytes 786440 | tf_op jit(solution)/shard_map/ppermute | solution.py:462
  280.9 21.4 %collective-permute-start.54 = (bf16[2,128,512]{2,1,0:T(8,128)(2,1)}, bf16[2,128,512]{2,1,0:T(8,128)(2,1)}, u32[]{:S(2)}, u32[]{:S(2)}) collective-permute-start(bf16[2,128,512]{2,1,0:T(8,128)(2,1)} %get-tuple-element.152), channel_id=1, source_target_pairs={{0,24},{4,28},{8,16},{12,20},{16,8},{20,12},{24,0},{28,4},{1,25},{... | collective-permute-start | bytes 786440 | tf_op jit(solution)/shard_map/ppermute | solution.py:462
  288.3 66.8 %collective-permute-start.58 = (bf16[4,256,512]{2,1,0:T(8,128)(2,1)}, bf16[4,256,512]{2,1,0:T(8,128)(2,1)}, u32[]{:S(2)}, u32[]{:S(2)}) collective-permute-start(bf16[4,256,512]{2,1,0:T(8,128)(2,1)} %get-tuple-element.155), channel_id=1, source_target_pairs={{0,4},{4,0},{8,12},{12,8},{16,20},{20,16},{24,28},{28,24},{1,5},{5... | collective-permute-start | bytes 3145736 | tf_op jit(solution)/shard_map/ppermute | solution.py:465
  308.8 46.3 %collective-permute-start.56 = (bf16[4,128,512]{2,1,0:T(8,128)(2,1)}, bf16[4,128,512]{2,1,0:T(8,128)(2,1)}, u32[]{:S(2)}, u32[]{:S(2)}) collective-permute-start(bf16[4,128,512]{2,1,0:T(8,128)(2,1)} %get-tuple-element.170.refs_0_), channel_id=1, source_target_pairs={{0,16},{4,20},{8,24},{12,28},{16,0},{20,4},{24,8},{28,12},{1,17},{... | collective-permute-start | bytes 1572872 | tf_op jit(solution)/shard_map/ppermute | solution.py:462
  314.1 41.1 %collective-permute-start.55 = (bf16[4,128,512]{2,1,0:T(8,128)(2,1)}, bf16[4,128,512]{2,1,0:T(8,128)(2,1)}, u32[]{:S(2)}, u32[]{:S(2)}) collective-permute-start(bf16[4,128,512]{2,1,0:T(8,128)(2,1)} %get-tuple-element.170.refs_0_), channel_id=1, source_target_pairs={{0,8},{4,12},{8,0},{12,4},{16,24},{20,28},{24,16},{28,20},{1,9},{5... | collective-permute-start | bytes 1572872 | tf_op jit(solution)/shard_map/ppermute | solution.py:462
  316.1 52.2 %collective-permute-start.59 = (bf16[80,2048]{1,0:T(8,128)(2,1)}, bf16[80,2048]{1,0:T(8,128)(2,1)S(1)}, u32[]{:S(2)}, u32[]{:S(2)}) collective-permute-start(bf16[80,2048]{1,0:T(8,128)(2,1)} %slice.398), channel_id=1, source_target_pairs={{0,4},{1,3},{2,6},{3,1},{4,0},{5,7},{6,2},{7,5},{8,12},{9,11},{10,... | collective-permute-start | bytes 983048 | tf_op jit(solution)/shard_map/ppermute | solution.py:484
  367.8 25.1 %collective-permute-start.65 = (bf16[4,256,512]{2,1,0:T(8,128)(2,1)}, bf16[4,256,512]{2,1,0:T(8,128)(2,1)}, u32[]{:S(2)}, u32[]{:S(2)}) collective-permute-start(bf16[4,256,512]{2,1,0:T(8,128)(2,1)} %get-tuple-element.169), channel_id=1, source_target_pairs={{0,4},{4,0},{8,12},{12,8},{16,20},{20,16},{24,28},{28,24},{1,5},{5... | collective-permute-start | bytes 3145736 | tf_op jit(solution)/shard_map/ppermute | solution.py:465
  398.5 25.9 %collective-permute-start.67 = (bf16[128,512]{1,0:T(8,128)(2,1)S(1)}, bf16[128,512]{1,0:T(8,128)(2,1)S(1)}, u32[]{:S(2)}, u32[]{:S(2)}) collective-permute-start(bf16[128,512]{1,0:T(8,128)(2,1)S(1)} %fusion.55), channel_id=1, source_target_pairs={{0,0},{1,8},{2,16},{3,24},{4,4},{5,12},{6,20},{7,28},{8,1},{9,9},{... | collective-permute-start | bytes 393224 | tf_op jit(solution)/shard_map/ppermute | solution.py:476
  400.7 22.9 %collective-permute-start.66 = (bf16[128,512]{1,0:T(8,128)(2,1)S(1)}, bf16[128,512]{1,0:T(8,128)(2,1)S(1)}, u32[]{:S(2)}, u32[]{:S(2)}) collective-permute-start(bf16[128,512]{1,0:T(8,128)(2,1)S(1)} %fusion.33), channel_id=1, source_target_pairs={{0,0},{1,8},{2,16},{3,24},{4,4},{5,12},{6,20},{7,28},{8,1},{9,9},{... | collective-permute-start | bytes 393224 | tf_op jit(solution)/shard_map/ppermute | solution.py:476
  (111 other events, 1486.4 us)

commit v2 on v1

--- a/solution.py
+++ b/solution.py
@@ -78,17 +78,45 @@
             outs[k][a] = total[a, block(order ^ k), :].astype(outs[k].dtype)
 
 
+def stat_rows(square, logits):
+    lane = lax.broadcasted_iota(jnp.int32, (TOK, TOK), 1)
+    table = jnp.where(lane == E, square, 0.0)
+    for e in range(E):
+        table = jnp.where(lane == e, logits[:, e : e + 1], table)
+    return jnp.transpose(table)[0:8]
+
+
 def key_value_body(subs):
     def body(at, *refs):
-        rows, gain, parts = refs[:E], refs[E], refs[E + 1 : E + 1 + subs]
-        gained, *outs = refs[E + 1 + subs : E + 2 + subs + E]
-        weights, total = refs[E + 2 + subs + E :]
+        rows, gain, router, parts = refs[:E], refs[E], refs[E + 1], refs[E + 2 : E + 2 + subs]
+        gained, own_stats, *outs = refs[E + 2 + subs : E + 4 + subs + E]
+        weights, total, stats = refs[E + 4 + subs + E :]
         place(weights, parts, at[1])
         for q in range(E):
-            gained[q * TOK : (q + 1) * TOK, :] = (rows[q][...].astype(F32) * gain[...]).astype(BF16)
+            wide = rows[q][...].astype(F32)
+            scaled = wide * gain[...]
+            gained[q * TOK : (q + 1) * TOK, :] = scaled.astype(BF16)
+            logits = lax.dot_general(
+                scaled, router[...], NT, precision=lax.Precision.HIGHEST, preferred_element_type=F32
+            )
+            stats[q] = stat_rows(jnp.sum(wide * wide, axis=-1, keepdims=True), logits)
         for a in range(2):
             total[a] = mul(gained[...], weights[a], NN)
-        send_blocks(total, outs, at[0])
+        own_stats[...] = stats[at[0]]
+        for k in range(E):
+            where = block(at[0] ^ k)
+            for a in range(2):
+                piece = total[a, where, :].astype(outs[k].dtype)
+                if k == 0:
+                    outs[k][a] = piece
+                else:
+                    outs[k][a * TOK : (a + 1) * TOK, :] = piece
+            if k > 0:
+                mine = stats[at[0] ^ k]
+                high = mine.astype(BF16).astype(F32)
+                pair = jnp.concatenate([high, mine - high], axis=0).astype(BF16)
+                outs[k][2 * TOK :, :] = jnp.zeros((16, outs[k].shape[1]), BF16)
+                outs[k][2 * TOK :, 0:TOK] = pair
 
     return body
 
@@ -206,15 +234,35 @@
 
 def attention_body(at, own_kv, *refs):
     got_kv, own_query, got_query = refs[: E - 1], refs[E - 1], refs[E : 2 * E - 1]
-    rows, low, probs, context, gated = refs[2 * E - 1 :]
+    own_stats, hot, rows, low, probs, context, gated = refs[2 * E - 1 :]
+    stats = own_stats[...]
+    for one in got_kv:
+        pair = one[2 * TOK :, 0:TOK].astype(F32)
+        stats = stats + pair[0:8] + pair[8:16]
+    scale_row = lax.rsqrt(stats[E : E + 1] / (E * own_kv.shape[2]) + EPSILON)
+    logits = stats[0:E] * scale_row
+    picked = [
+        jnp.sum(hot[i * E : (i + 1) * E, :] * logits, axis=0, keepdims=True) for i in range(TOPK)
+    ]
+    gap = picked[0] - picked[1]
+    prob_rows = [1.0 / (1.0 + jnp.exp(-gap)), 1.0 / (1.0 + jnp.exp(gap))]
+    rows[0:1, :] = scale_row
+    for i in range(TOPK):
+        rows[1 + i : 2 + i, :] = prob_rows[i] * hot[8 + i : 9 + i, :]
+        rows[3 + i : 4 + i, :] = prob_rows[i]
+    rows[5:9, :] = logits
+    rows[9:16, :] = jnp.zeros((7, TOK), F32)
     cols = columns(rows[...])
     scale = cols[:, 0:1]
-    for a in range(4):
-        own, got = (own_kv, got_kv) if a < 2 else (own_query, got_query)
-        total = own[a % 2]
-        for one in got:
-            total = total + one[a % 2].astype(F32)
+    for a in range(2):
+        where = slice(a * TOK, (a + 1) * TOK)
+        total, query = own_kv[a], own_query[a]
+        for one in got_kv:
+            total = total + one[where, :].astype(F32)
+        for one in got_query:
+            query = query + one[a].astype(F32)
         low[a] = (total * scale).astype(BF16)
+        low[2 + a] = (query * scale).astype(BF16)
     allowed = attention_mask(at)
     for h in range(low.shape[2] // HS):
         head = slice(h * HS, (h + 1) * HS)
@@ -372,11 +420,7 @@
         extra = two_halves([square, 2.0 * own - chosen])
         outs[k][:, :size] = mul(select[k], low, NN).astype(BF16)
         outs[k][:, size:] = mul(select[k], extra, NN).astype(BF16)
-    lane = lax.broadcasted_iota(jnp.int32, (TOK, TOK), 1)
-    table = jnp.where(lane == E, square, 0.0)
-    for e in range(E):
-        table = jnp.where(lane == e, logits[:, e : e + 1], table)
-    stats[...] = jnp.transpose(table)[0:8]
+    stats[...] = stat_rows(square, logits)
 
 
 def join_rows_body(at, *refs):
@@ -534,20 +578,23 @@
 
     turned_stream = swap(stream)
 
+    size = max(shard_rows, TOK)
+
+    def pad(rows, count):
+        return jnp.pad(rows, ((0, count - rows.shape[0]), (0, size - rows.shape[1])))
+
+    own_routes = jnp.concatenate([attn_routes.T, mlp_routes.T], axis=0).astype(BF16)
     own_rows = jnp.concatenate(
         [attn_gain[None, :], attn_router.T, mlp_gain[None, :], mlp_router.T], axis=0
     )
-    parts = gather_subs(jnp.pad(own_rows, ((0, 16 - own_rows.shape[0]), (0, 0))))
-    near = xor_shuffle(jnp.stack(parts), sub).swapaxes(0, 1).reshape(16, slice_width)
+    parts = gather_subs(jnp.concatenate([pad(own_routes, 8), pad(own_rows, 16)], axis=0))
+    parts = jnp.stack(parts)
+    near = xor_shuffle(parts[:, 8:, :shard_rows], sub).swapaxes(0, 1).reshape(16, slice_width)
     gain_one_plane = near[0].astype(F32)
+    router_one_plane = near[1:5].astype(F32)
     gain_two_plane = near[5].astype(F32)
     router_two_plane = near[6:10].astype(F32)
-    home_rows = swap(near)
-    gain_one_home = home_rows[0].astype(F32)
-    router_one_home = home_rows[1:5].astype(F32)
-
-    own_routes = jnp.concatenate([attn_routes.T, mlp_routes.T], axis=0).astype(BF16)
-    route_parts = gather_subs(jnp.pad(own_routes, ((0, 4), (0, 0))))
+
     at = jnp.stack([narrow ^ plane, sub, plane, narrow]).astype(jnp.int32)
     line_count = wide_count * 8
     hot_cols, home_hot, turned_hot, mlp_cols, expert_hot, select = run(
@@ -561,7 +608,7 @@
             shape((8, TOK), F32),
             shape((E, SLOTS, TOK), BF16),
         ],
-        [at, *after(gather_planes(jnp.stack(route_parts)), turned_stream)],
+        [at, *gather_planes(parts[:, :8, :TOK])],
         [pltpu.VMEM((line_count, TOK), F32)] * 3 + [pltpu.VMEM((E, 8, TOK), F32)] * 2,
     )
     hot_one, keep_one = home_hot[0:8].reshape(TOPK, E, TOK), home_hot[8:10]
@@ -572,55 +619,48 @@
     query_parts = gather_subs(query_proj, kv_parts[-1])
     out_parts = gather_subs(output_proj, query_parts[-1])
     home_stream = stream.astype(F32)
-    turned_grad = swap(out_grad)
 
     rows_all = E * TOK
     sent = shape((2, TOK, local_width), BF16)
     kept_own = shape((2, TOK, local_width), F32)
     all_streams = gather_narrow(turned_stream)
-    gained, *kv_blocks = run(
+    gained, own_stats, *kv_blocks = run(
         "key_value",
         key_value_body(subs),
-        [shape((rows_all, slice_width), BF16), kept_own] + [sent] * (E - 1),
-        [at, *all_streams, gain_one_plane[None], *kv_parts],
+        [shape((rows_all, slice_width), BF16), shape((8, TOK), F32), kept_own]
+        + [shape((2 * TOK + 16, local_width), BF16)] * (E - 1),
+        [
+            at,
+            *all_streams,
+            gain_one_plane[None],
+            jnp.pad(router_one_plane, ((0, 4), (0, 0))),
+            *kv_parts,
+        ],
         [
             pltpu.VMEM((2, slice_width, local_width), BF16),
             pltpu.VMEM((2, rows_all, local_width), F32),
+            pltpu.VMEM((E, 8, TOK), F32),
         ],
     )
+    turned_grad = swap(after(out_grad, own_stats))
     kv_blocks = exchange_planes(kv_blocks)
     routed_scratch = [
         pltpu.VMEM((E, slice_width, local_width), BF16),
         pltpu.VMEM((TOPK, rows_all, local_width), F32),
     ]
-    gained_home = home_stream * gain_one_home
-    stats_one = jnp.concatenate(
-        [
-            jnp.sum(home_stream * home_stream, axis=-1)[None],
-            dot(router_one_home, gained_home, ((1,), (1,)), PRECISE),
-        ],
-        axis=0,
-    )
-    stats_one = sum_narrow(stats_one)
     query_blocks = run(
         "query",
         routed_body(subs, True),
         [kept_own] + [sent] * (E - 1),
-        [at, after(gained, *kv_blocks[1:], stats_one), hot_cols, *query_parts],
+        [at, after(gained, *kv_blocks[1:]), hot_cols, *query_parts],
         routed_scratch,
     )
     query_blocks = exchange_planes(query_blocks)
-
-    scale_one = lax.rsqrt(stats_one[0] / width + EPSILON)
-    logits_one = stats_one[1:] * scale_one
 
     def gates(logits, hots):
         picked = jnp.sum(hots * logits[None], axis=1)
         gap = picked[0] - picked[1]
         return jnp.stack([jax.nn.sigmoid(gap), jax.nn.sigmoid(-gap)])
-
-    prob_one = gates(logits_one, hot_one)
-    gate_one = prob_one * keep_one
 
     def share(full):
         size = full.shape[-1]
@@ -634,18 +674,19 @@
         return jnp.concatenate([full, by_narrow(full, 1)], axis=0).reshape(-1, size), got
 
     picked = jnp.einsum("kst,td->ksd", select, turned_grad, preferred_element_type=F32).astype(BF16)
-    token_rows = jnp.stack([scale_one, gate_one[0], gate_one[1]] + [scale_one] * 5)
-    low, probs, context, gated = run(
+    token_rows, low, probs, context, gated = run(
         "attention",
         attention_body,
         [
+            shape((16, TOK), F32),
             shape((4, TOK, local_width), BF16),
             shape((head_count, TOPK * TOK, TOK), F32),
             sent,
             sent,
         ],
-        [doc_lengths[0], *kv_blocks, *query_blocks, token_rows],
-    )
+        [doc_lengths[0], *kv_blocks, *query_blocks, own_stats, home_hot],
+    )
+    scale_one, prob_one, logits_one = token_rows[0], token_rows[3:5], token_rows[5:9]
 
     (full,) = run(
         "join",
@@ -811,11 +852,21 @@
         ],
     )
     grad_planes = gather_planes(grads_low)
+    dboth = jnp.stack(
+        [
+            (dgate_pre.astype(F32) * row_scale).astype(BF16),
+            (dup_pre.astype(F32) * row_scale).astype(BF16),
+        ],
+        axis=1,
+    )
+    up_grad = jnp.einsum(
+        "rd,rkf->dkf", expert_rows, after(dboth, grad_planes[E - 1]), preferred_element_type=F32
+    )
     dmixed, *query_grad_parts = run(
         "query_grad",
         query_grad_body,
         [shape((E, rows_all, local_width), BF16)] + weight_parts(E),
-        [at, gained, hot_cols, *after(grad_planes, output_got)],
+        [at, gained, hot_cols, *after(grad_planes, output_got, up_grad)],
         weight_scratch,
     )
     query_grad, query_got = weight_sum(query_grad_parts)
@@ -833,6 +884,10 @@
         ],
         [pltpu.VMEM((2 + E, slice_width, local_width), BF16)],
     )
+    home_rows = swap(after(near, own_stats))
+    gain_one_home = home_rows[0].astype(F32)
+    router_one_home = home_rows[1:5].astype(F32)
+    gained_home = home_stream * gain_one_home
     home_sums = sum_narrow(after(home_sums, gain_row))
     dprob_one = keep_one * home_sums[:2]
     dlogit_one = gate_back(prob_one, dprob_one, hot_one)
@@ -864,17 +919,6 @@
     mixture = from_planes(*mixture, 0, gain_row)
     mixture = jnp.einsum("kst,ksd->td", select, after(mixture, turned_out), preferred_element_type=F32)
     layer_out = swap((hidden + mixture).astype(BF16)).astype(F32)
-    dboth = jnp.stack(
-        [
-            (dgate_pre.astype(F32) * row_scale).astype(BF16),
-            (dup_pre.astype(F32) * row_scale).astype(BF16),
-        ],
-        axis=1,
-    )
-    up_grad = jnp.einsum(
-        "rd,rkf->dkf", expert_rows, after(dboth, turned_out), preferred_element_type=F32
-    )
-
     return (
         layer_out,
         stream_grad,

time: 430 us -> 433 us (level)
  waiting for transfers between devices: 173 us -> 178 us
  other arithmetic: 37.1 us -> 32.2 us
    ppermute x9 -> x8, waiting for transfers between devices: 2.4 us -> 13.2 us  [by_sub(): return lax.ppermute(values, 'wide', [(i, i ^ k) for i in range(wide_count)])]
    ppermute x8, waiting for transfers between devices: 35.7 us -> 25.6 us  [by_side(): return lax.ppermute(values, ('wide', 'narrow'), pairs)]
    ppermute x20 -> x18, waiting for transfers between devices: 18.9 us -> 25.4 us  [by_narrow(): lax.ppermute(values, 'narrow', [(i, i ^ k) for i in range(narrow_count)])]
    dot_general x8 -> x7, matrix products: 19.9 us -> 17.9 us  [dot(): lax.dot_general(left, right, ((contract[0], contract[1]), ((), ())), prec...]
    ppermute x9 -> x8, starting transfers between devices: 8.98 us -> 8 us  [by_sub(): return lax.ppermute(values, 'wide', [(i, i ^ k) for i in range(wide_count)])]
  transfers between devices with their start and end apart: 75 -> 72, of which waited for: 32 -> 35; matrix products, arithmetic and copies ran while one was open for 15% -> 13% of each run, Pallas kernels for 12% -> 12%
where the time goes in v2:
time: 433 us; the launch traced here: 429 us
  waiting for transfers between devices  178 us (41%)
  starting transfers between devices  95.4 us (22%)
  Pallas kernels  61.4 us (14%)
  matrix products  45.7 us (11%)
  other arithmetic  32.2 us (7%)
  local copies, waits for them, and re-layouts  14.6 us (3%)
    ppermute x32, waiting for transfers between devices, by_plane(): lax.ppermute(values, 'wide', [(i, i ^ k * subs) for i in range(wide_count)])  106 us
    pallas_call x16, Pallas kernels, run(): pl.pallas_call(body, out_shape=tuple(outs), in_specs=[pl.BlockSpec(memory...  61.4 us
    ppermute x32, starting transfers between devices, by_plane(): lax.ppermute(values, 'wide', [(i, i ^ k * subs) for i in range(wide_count)])  56.7 us
    ppermute x8, waiting for transfers between devices, by_side(): return lax.ppermute(values, ('wide', 'narrow'), pairs)  25.6 us
    ppermute x18, waiting for transfers between devices, by_narrow(): lax.ppermute(values, 'narrow', [(i, i ^ k) for i in range(narrow_count)])  25.4 us
    ppermute x6, starting transfers between devices, swap(): return lax.ppermute(values, ('wide', 'narrow'), pairs)  23.1 us
    dot_general x7, matrix products, dot(): lax.dot_general(left, right, ((contract[0], contract[1]), ((), ())), prec...  17.9 us
    dot_general x1, matrix products, local(): jnp.einsum('krf,dkf->rd', jnp.stack([dgate_pre, dup_pre]), weight_in, pre...  14.5 us
  transfers between devices with their start and end apart: 72, of which 35 were waited for; matrix products, arithmetic and copies ran while one was open for 13% of the time, Pallas kernels for 12%

profile of v2, /device:TPU:2, one launch (start us, length us, event | category | flops | bytes accessed | tf_op | source)
XLA Modules:
  0.0 429.5 jit_solution(17851988410843572441)
XLA Ops:
  38.2 14.8 %collective-permute-done.11.refs_3_ = bf16[2,8,128]{2,1,0:T(8,128)(2,1)S(1)} collective-permute-done((bf16[2,8,128]{2,1,0:T(8,128)(2,1)S(1)}, bf16[2,8,128]{2,1,0:T(8,128)(2,1)S(1)}, u32[]{:S(2)}, u32[]{:S(2)}) %collective-permute-start.11) | collective-permute-done | bytes 4128 | tf_op jit(solution)/shard_map/ppermute | solution.py:506
  53.0 7.7 %collective-permute-start.10 = (bf16[2,8,128]{2,1,0:T(8,128)(2,1)S(1)}, bf16[2,8,128]{2,1,0:T(8,128)(2,1)S(1)}, u32[]{:S(2)}, u32[]{:S(2)}) collective-permute-start(bf16[2,8,128]{2,1,0:T(8,128)(2,1)S(1)} %pad_maximum_fusion.13.refs_0_), channel_id=1, source_target_pairs={{0,16},{4,20},{8,24},{12,28},{16,0},{20,4},{24,8},{28,12},{1,17},{... | collective-permute-start | bytes 12296 | tf_op jit(solution)/shard_map/ppermute | solution.py:506
  83.5 6.5 %collective-permute-done.13.refs_4_ = bf16[2,128,512]{2,1,0:T(8,128)(2,1)} collective-permute-done((bf16[2,128,512]{2,1,0:T(8,128)(2,1)}, bf16[2,128,512]{2,1,0:T(8,128)(2,1)}, u32[]{:S(2)}, u32[]{:S(2)}) %collective-permute-start.13) | collective-permute-done | bytes 262176 | tf_op jit(solution)/shard_map/ppermute | solution.py:506
  90.0 13.2 %collective-permute-done.14.refs_5_ = bf16[2,128,512]{2,1,0:T(8,128)(2,1)} collective-permute-done((bf16[2,128,512]{2,1,0:T(8,128)(2,1)}, bf16[2,128,512]{2,1,0:T(8,128)(2,1)}, u32[]{:S(2)}, u32[]{:S(2)}) %collective-permute-start.14) | collective-permute-done | bytes 262176 | tf_op jit(solution)/shard_map/ppermute | solution.py:506
  103.9 5.4 %attention.1 = (f32[16,128]{1,0:T(8,128)}, bf16[4,128,512]{2,1,0:T(8,128)(2,1)}, f32[4,256,128]{2,1,0:T(8,128)}, bf16[2,128,512]{2,1,0:T(8,128)(2,1)}, bf16[2,128,512]{2,1,0:T(8,128)(2,1)}) custom-call(s32[4]{0:T(128)} %bitcast.190, f32[2,128,512]{2,1,0:T(8,128)} %get-tuple-element.105.own_kv, bf16[272,512]{1,0:T(8,128)(2,1)} %copy-done.33, ...), custom_call_target="tpu_custom_call" | custom-call | flops 1 | bytes 1 | tf_op jit(solution)/shard_map/attention/pallas_call | solution.py:52
  123.8 15.3 %collective-permute-done.17.refs_2_ = bf16[2,128,512]{2,1,0:T(8,128)(2,1)} collective-permute-done((bf16[2,128,512]{2,1,0:T(8,128)(2,1)}, bf16[2,128,512]{2,1,0:T(8,128)(2,1)}, u32[]{:S(2)}, u32[]{:S(2)}) %collective-permute-start.17) | collective-permute-done | bytes 262176 | tf_op jit(solution)/shard_map/ppermute | solution.py:506
  162.2 5.9 %collective-permute-done.29.refs_2_ = bf16[80,640]{1,0:T(8,128)(2,1)} collective-permute-done((bf16[80,640]{1,0:T(8,128)(2,1)}, bf16[80,640]{1,0:T(8,128)(2,1)}, u32[]{:S(2)}, u32[]{:S(2)}) %collective-permute-start.29) | collective-permute-done | bytes 102432 | tf_op jit(solution)/shard_map/ppermute | solution.py:506
  171.0 7.0 %collective-permute-done.31 = bf16[80,2176]{1,0:T(8,128)(2,1)S(1)} collective-permute-done((bf16[80,2176]{1,0:T(8,128)(2,1)}, bf16[80,2176]{1,0:T(8,128)(2,1)S(1)}, u32[]{:S(2)}, u32[]{:S(2)}) %collective-permute-start.31) | collective-permute-done | bytes 348192 | tf_op jit(solution)/shard_map/ppermute | solution.py:528
  180.8 9.4 %collective-permute-done.32 = bf16[160,2176]{1,0:T(8,128)(2,1)S(1)} collective-permute-done((bf16[160,2176]{1,0:T(8,128)(2,1)S(1)}, bf16[160,2176]{1,0:T(8,128)(2,1)S(1)}, u32[]{:S(2)}, u32[]{:S(2)}) %collective-permute-start.32) | collective-permute-done | bytes 696352 | tf_op jit(solution)/shard_map/ppermute | solution.py:528
  203.4 4.8 %fusion.18 = f32[2,640,704]{1,2,0:T(8,128)S(1)} fusion(bf16[1,2048,2,704]{1,3,2,0:T(8,128)(2,1)S(1)} %bitcast.192, bf16[640,2176]{1,0:T(8,128)(2,1)S(1)} %pad_maximum_fusion.1), kind=kOutput, calls=%fused_computation.32 | convolution fusion | flops 3690987520 | bytes 11993088 | tf_op jit(solution)/shard_map/rd,dkf->krf/dot_general | solution.py:742
  212.0 14.5 %fusion.4 = f32[640,2048]{1,0:T(8,128)S(1)} fusion(bf16[1,2048,2,704]{1,3,2,0:T(8,128)(2,1)S(1)} %bitcast.192, bf16[1,640,704]{1,2,0:T(8,128)(2,1)S(1)} %bitcast.159, bf16[1,640,704]{1,2,0:T(8,128)(2,1)S(1)} %bitcast.160), kind=kOutput, calls=%fused_computation.7 | convolution fusion | flops 3691888640 | bytes 12812288 | tf_op jit(solution)/shard_map/krf,dkf->rd/dot_general | solution.py:753
  233.4 5.7 %collective-permute-start.64 = (bf16[16,512]{1,0:T(8,128)(2,1)S(1)}, bf16[16,512]{1,0:T(8,128)(2,1)S(1)}, u32[]{:S(2)}, u32[]{:S(2)}) collective-permute-start(bf16[16,512]{1,0:T(8,128)(2,1)S(1)} %bitcast.182), channel_id=1, source_target_pairs={{0,0},{1,8},{2,16},{3,24},{4,4},{5,12},{6,20},{7,28},{8,1},{9,9},{... | collective-permute-start | bytes 49160 | tf_op jit(solution)/shard_map/ppermute | solution.py:520
  247.9 6.0 %collective-permute-done.41.got = bf16[80,2176]{1,0:T(8,128)(2,1)} collective-permute-done((bf16[80,2176]{1,0:T(8,128)(2,1)S(1)}, bf16[80,2176]{1,0:T(8,128)(2,1)}, u32[]{:S(2)}, u32[]{:S(2)}) %collective-permute-start.41) | collective-permute-done | bytes 348192 | tf_op jit(solution)/shard_map/ppermute | solution.py:528
  290.3 6.8 %fusion.39 = f32[704,2048]{1,0:T(8,128)} fusion(bf16[640,704]{0,1:T(8,128)(2,1)} %get-tuple-element.154, bf16[320,2048]{1,0:T(8,128)(2,1)} %copy-done.60, bf16[160,2048]{1,0:T(8,128)(2,1)} %collective-permute-done.27, bf16[80,2048]{1,0:T(8,128)(2,1)} %copy-done.20, bf16[80,2048]{1,0:T(8,128)(2,1)S(1)} %copy-done.10), kind=kOutput, calls=%fused_computation.73 | convolution fusion | flops 1855979520 | bytes 9289728 | tf_op jit(solution)/shard_map/dot_general | solution.py:22
  297.1 6.9 %collective-permute-done.49.refs_1_ = bf16[2,128,512]{2,1,0:T(8,128)(2,1)} collective-permute-done((bf16[2,128,512]{2,1,0:T(8,128)(2,1)}, bf16[2,128,512]{2,1,0:T(8,128)(2,1)}, u32[]{:S(2)}, u32[]{:S(2)}) %collective-permute-start.49) | collective-permute-done | bytes 262176 | tf_op jit(solution)/shard_map/ppermute | solution.py:506
  304.0 5.1 %attention_back.1 = (bf16[4,128,512]{2,1,0:T(8,128)(2,1)}, f32[8,128]{1,0:T(8,128)}) custom-call(s32[4]{0:T(128)} %pad_add_fusion.at, f32[2,128,512]{2,1,0:T(8,128)} %get-tuple-element.155.own, bf16[2,128,512]{2,1,0:T(8,128)(2,1)} %collective-permute-done.48.refs_0_, bf16[2,128,512]{2,1,0:T(8,128)(2,1)} %collective-permute-done.49.refs_1_, ...), custom_call_target="tpu_custom_call" | custom-call | flops 1 | bytes 1 | tf_op jit(solution)/shard_map/attention_back/pallas_call | solution.py:52
  319.7 6.4 %collective-permute-done.53.refs_3_ = bf16[4,128,512]{2,1,0:T(8,128)(2,1)} collective-permute-done((bf16[4,128,512]{2,1,0:T(8,128)(2,1)}, bf16[4,128,512]{2,1,0:T(8,128)(2,1)}, u32[]{:S(2)}, u32[]{:S(2)}) %collective-permute-start.53) | collective-permute-done | bytes 524320 | tf_op jit(solution)/shard_map/ppermute | solution.py:506
  326.2 7.6 %fusion.13 = f32[2048,2,704]{0,2,1:T(8,128)} fusion(bf16[640,2,704]{0,2,1:T(8,128)(2,1)S(1)} %copy-done.17, bf16[640,2176]{1,0:T(8,128)(2,1)S(1)} %copy-done.9), kind=kOutput, calls=%fused_computation.19 | convolution fusion | flops 3690987520 | bytes 15958016 | tf_op jit(solution)/shard_map/rd,rkf->dkf/dot_general | solution.py:862
  333.8 23.6 %collective-permute-done.52.refs_2_ = bf16[4,128,512]{2,1,0:T(8,128)(2,1)S(1)} collective-permute-done((bf16[4,128,512]{2,1,0:T(8,128)(2,1)S(1)}, bf16[4,128,512]{2,1,0:T(8,128)(2,1)S(1)}, u32[]{:S(2)}, u32[]{:S(2)}) %collective-permute-start.52) | collective-permute-done | bytes 524320 | tf_op jit(solution)/shard_map/ppermute | solution.py:506
  358.4 5.3 %query_grad.1 = (bf16[4,512,512]{2,1,0:T(8,128)(2,1)}, f32[4,256,512]{2,1,0:T(8,128)}, bf16[4,256,512]{2,1,0:T(8,128)(2,1)}) custom-call(s32[4]{0:T(128)} %pad_add_fusion.at, bf16[512,512]{1,0:T(8,128)(2,1)} %get-tuple-element.110.refs_0_.rows, f32[512,8]{1,0:T(8,128)} %get-tuple-element.111.refs_1_.refs_4_.hot, ...), custom_call_target="tpu_custom_call" | custom-call | flops 1 | bytes 1 | tf_op jit(solution)/shard_map/query_grad/pallas_call | solution.py:52
  363.6 6.2 %input.1 = (bf16[2,512,512]{2,1,0:T(8,128)(2,1)}, f32[1,512]{1,0:T(1,128)}, f32[128,512]{1,0:T(8,128)}, f32[128,512]{1,0:T(8,128)}, bf16[2,128,512]{2,1,0:T(8,128)(2,1)}) custom-call(s32[4]{0:T(128)} %pad_add_fusion.at, bf16[4,128,512]{2,1,0:T(8,128)(2,1)} %get-tuple-element.170.refs_0_, bf16[4,128,512]{2,1,0:T(8,128)(2,1)} %copy-done.16, ...), custom_call_target="tpu_custom_call" | custom-call | flops 1 | bytes 1 | tf_op jit(solution)/shard_map/input/pallas_call | solution.py:52
  389.9 5.4 %collective-permute-done.67 = f32[4,512]{1,0:T(4,128)S(1)} collective-permute-done((f32[4,512]{1,0:T(4,128)S(1)}, f32[4,512]{1,0:T(4,128)S(1)}, u32[]{:S(2)}, u32[]{:S(2)}) %collective-permute-start.67) | collective-permute-done | bytes 8224 | tf_op jit(solution)/shard_map/ppermute | solution.py:520
  396.3 4.9 %collective-permute-done.60 = bf16[128,512]{1,0:T(8,128)(2,1)S(1)} collective-permute-done((bf16[128,512]{1,0:T(8,128)(2,1)S(1)}, bf16[128,512]{1,0:T(8,128)(2,1)S(1)}, u32[]{:S(2)}, u32[]{:S(2)}) %collective-permute-start.60) | collective-permute-done | bytes 131104 | tf_op jit(solution)/shard_map/ppermute | solution.py:512
  414.8 9.8 %collective-permute-done.70 = f32[10,512]{1,0:T(8,128)S(1)} collective-permute-done((f32[10,512]{1,0:T(8,128)S(1)}, f32[10,512]{1,0:T(8,128)S(1)}, u32[]{:S(2)}, u32[]{:S(2)}) %collective-permute-start.70) | collective-permute-done | bytes 20512 | tf_op jit(solution)/shard_map/ppermute | solution.py:509
  (359 shorter events, 223.4 us)
Async XLA Ops:
  15.7 57.0 %collective-permute-start.12 = (bf16[4,256,512]{2,1,0:T(8,128)(2,1)}, bf16[4,256,512]{2,1,0:T(8,128)(2,1)}, u32[]{:S(2)}, u32[]{:S(2)}) collective-permute-start(bf16[4,256,512]{2,1,0:T(8,128)(2,1)} %refs_7_.1), channel_id=1, source_target_pairs={{0,4},{4,0},{8,12},{12,8},{16,20},{20,16},{24,28},{28,24},{1,5},{5... | collective-permute-start | bytes 3145736 | tf_op jit(solution)/shard_map/ppermute | solution.py:509
  30.4 42.2 %collective-permute-start.6 = (bf16[272,512]{1,0:T(8,128)(2,1)}, bf16[272,512]{1,0:T(8,128)(2,1)S(1)}, u32[]{:S(2)}, u32[]{:S(2)}) collective-permute-start(bf16[272,512]{1,0:T(8,128)(2,1)} %get-tuple-element.106), channel_id=1, source_target_pairs={{0,8},{4,12},{8,0},{12,4},{16,24},{20,28},{24,16},{28,20},{1,9},{5... | collective-permute-start | bytes 835592 | tf_op jit(solution)/shard_map/ppermute | solution.py:506
  31.2 41.5 %collective-permute-start.7 = (bf16[272,512]{1,0:T(8,128)(2,1)}, bf16[272,512]{1,0:T(8,128)(2,1)}, u32[]{:S(2)}, u32[]{:S(2)}) collective-permute-start(bf16[272,512]{1,0:T(8,128)(2,1)} %get-tuple-element.107), channel_id=1, source_target_pairs={{0,16},{4,20},{8,24},{12,28},{16,0},{20,4},{24,8},{28,12},{1,17},{... | collective-permute-start | bytes 835592 | tf_op jit(solution)/shard_map/ppermute | solution.py:506
  33.8 38.9 %collective-permute-start.8 = (bf16[272,512]{1,0:T(8,128)(2,1)}, bf16[272,512]{1,0:T(8,128)(2,1)}, u32[]{:S(2)}, u32[]{:S(2)}) collective-permute-start(bf16[272,512]{1,0:T(8,128)(2,1)} %get-tuple-element.108), channel_id=1, source_target_pairs={{0,24},{4,28},{8,16},{12,20},{16,8},{20,12},{24,0},{28,4},{1,25},{... | collective-permute-start | bytes 835592 | tf_op jit(solution)/shard_map/ppermute | solution.py:506
  72.7 66.4 %collective-permute-start.19 = (bf16[4,256,512]{2,1,0:T(8,128)(2,1)}, bf16[4,256,512]{2,1,0:T(8,128)(2,1)}, u32[]{:S(2)}, u32[]{:S(2)}) collective-permute-start(bf16[4,256,512]{2,1,0:T(8,128)(2,1)} %refs_5_.4), channel_id=1, source_target_pairs={{0,4},{4,0},{8,12},{12,8},{16,20},{20,16},{24,28},{28,24},{1,5},{5... | collective-permute-start | bytes 3145736 | tf_op jit(solution)/shard_map/ppermute | solution.py:509
  78.0 25.2 %collective-permute-start.14 = (bf16[2,128,512]{2,1,0:T(8,128)(2,1)}, bf16[2,128,512]{2,1,0:T(8,128)(2,1)}, u32[]{:S(2)}, u32[]{:S(2)}) collective-permute-start(bf16[2,128,512]{2,1,0:T(8,128)(2,1)} %get-tuple-element.115), channel_id=1, source_target_pairs={{0,16},{4,20},{8,24},{12,28},{16,0},{20,4},{24,8},{28,12},{1,17},{... | collective-permute-start | bytes 786440 | tf_op jit(solution)/shard_map/ppermute | solution.py:506
  78.3 24.9 %collective-permute-start.15 = (bf16[2,128,512]{2,1,0:T(8,128)(2,1)}, bf16[2,128,512]{2,1,0:T(8,128)(2,1)S(1)}, u32[]{:S(2)}, u32[]{:S(2)}) collective-permute-start(bf16[2,128,512]{2,1,0:T(8,128)(2,1)} %get-tuple-element.116), channel_id=1, source_target_pairs={{0,24},{4,28},{8,16},{12,20},{16,8},{20,12},{24,0},{28,4},{1,25},{... | collective-permute-start | bytes 786440 | tf_op jit(solution)/shard_map/ppermute | solution.py:506
  83.5 25.9 %collective-permute-start.25 = (bf16[80,512]{1,0:T(8,128)(2,1)}, bf16[80,512]{1,0:T(8,128)(2,1)}, u32[]{:S(2)}, u32[]{:S(2)}) collective-permute-start(bf16[80,512]{1,0:T(8,128)(2,1)} %get-tuple-element.217), channel_id=1, source_target_pairs={{0,24},{4,28},{8,16},{12,20},{16,8},{20,12},{24,0},{28,4},{1,25},{... | collective-permute-start | bytes 245768 | tf_op jit(solution)/shard_map/ppermute | solution.py:506
  90.0 20.7 %collective-permute-start.24 = (bf16[80,512]{1,0:T(8,128)(2,1)}, bf16[80,512]{1,0:T(8,128)(2,1)}, u32[]{:S(2)}, u32[]{:S(2)}) collective-permute-start(bf16[80,512]{1,0:T(8,128)(2,1)} %get-tuple-element.218), channel_id=1, source_target_pairs={{0,16},{4,20},{8,24},{12,28},{16,0},{20,4},{24,8},{28,12},{1,17},{... | collective-permute-start | bytes 245768 | tf_op jit(solution)/shard_map/ppermute | solution.py:506
  115.5 23.6 %collective-permute-start.17 = (bf16[2,128,512]{2,1,0:T(8,128)(2,1)}, bf16[2,128,512]{2,1,0:T(8,128)(2,1)}, u32[]{:S(2)}, u32[]{:S(2)}) collective-permute-start(bf16[2,128,512]{2,1,0:T(8,128)(2,1)} %get-tuple-element.119.refs_0_), channel_id=1, source_target_pairs={{0,16},{4,20},{8,24},{12,28},{16,0},{20,4},{24,8},{28,12},{1,17},{... | collective-permute-start | bytes 786440 | tf_op jit(solution)/shard_map/ppermute | solution.py:506
  119.9 19.1 %collective-permute-start.16 = (bf16[2,128,512]{2,1,0:T(8,128)(2,1)}, bf16[2,128,512]{2,1,0:T(8,128)(2,1)}, u32[]{:S(2)}, u32[]{:S(2)}) collective-permute-start(bf16[2,128,512]{2,1,0:T(8,128)(2,1)} %get-tuple-element.119.refs_0_), channel_id=1, source_target_pairs={{0,8},{4,12},{8,0},{12,4},{16,24},{20,28},{24,16},{28,20},{1,9},{5... | collective-permute-start | bytes 786440 | tf_op jit(solution)/shard_map/ppermute | solution.py:506
  121.9 26.5 %collective-permute-start.27 = (bf16[160,2048]{1,0:T(8,128)(2,1)}, bf16[160,2048]{1,0:T(8,128)(2,1)}, u32[]{:S(2)}, u32[]{:S(2)}) collective-permute-start(bf16[160,2048]{1,0:T(8,128)(2,1)} %pad_maximum_fusion.7), channel_id=1, source_target_pairs={{0,2},{1,5},{2,0},{3,7},{4,6},{5,1},{6,4},{7,3},{8,10},{9,13},{10,... | collective-permute-start | bytes 1966088 | tf_op jit(solution)/shard_map/ppermute | solution.py:528
  180.7 17.9 %collective-permute-start.38 = (bf16[320,2048]{1,0:T(8,128)(2,1)S(1)}, bf16[320,2048]{1,0:T(8,128)(2,1)S(1)}, u32[]{:S(2)}, u32[]{:S(2)}) collective-permute-start(bf16[320,2048]{1,0:T(8,128)(2,1)S(1)} %pad_maximum_fusion.5), channel_id=1, source_target_pairs={{0,1},{1,0},{2,3},{3,2},{4,5},{5,4},{6,7},{7,6},{8,9},{9,8},{10,11... | collective-permute-start | bytes 3932168 | tf_op jit(solution)/shard_map/ppermute | solution.py:512
  271.0 40.6 %collective-permute-start.37 = (bf16[160,2048]{1,0:T(8,128)(2,1)}, bf16[160,2048]{1,0:T(8,128)(2,1)}, u32[]{:S(2)}, u32[]{:S(2)}) collective-permute-start(bf16[160,2048]{1,0:T(8,128)(2,1)} %slice.402), channel_id=1, source_target_pairs={{0,2},{1,5},{2,0},{3,7},{4,6},{5,1},{6,4},{7,3},{8,10},{9,13},{10,... | collective-permute-start | bytes 1966088 | tf_op jit(solution)/shard_map/ppermute | solution.py:528
  282.3 21.7 %collective-permute-start.49 = (bf16[2,128,512]{2,1,0:T(8,128)(2,1)}, bf16[2,128,512]{2,1,0:T(8,128)(2,1)}, u32[]{:S(2)}, u32[]{:S(2)}) collective-permute-start(bf16[2,128,512]{2,1,0:T(8,128)(2,1)} %get-tuple-element.149), channel_id=1, source_target_pairs={{0,16},{4,20},{8,24},{12,28},{16,0},{20,4},{24,8},{28,12},{1,17},{... | collective-permute-start | bytes 786440 | tf_op jit(solution)/shard_map/ppermute | solution.py:506
  283.9 20.1 %collective-permute-start.50 = (bf16[2,128,512]{2,1,0:T(8,128)(2,1)}, bf16[2,128,512]{2,1,0:T(8,128)(2,1)}, u32[]{:S(2)}, u32[]{:S(2)}) collective-permute-start(bf16[2,128,512]{2,1,0:T(8,128)(2,1)} %get-tuple-element.150), channel_id=1, source_target_pairs={{0,24},{4,28},{8,16},{12,20},{16,8},{20,12},{24,0},{28,4},{1,25},{... | collective-permute-start | bytes 786440 | tf_op jit(solution)/shard_map/ppermute | solution.py:506
  289.8 67.6 %collective-permute-start.54 = (bf16[4,256,512]{2,1,0:T(8,128)(2,1)}, bf16[4,256,512]{2,1,0:T(8,128)(2,1)}, u32[]{:S(2)}, u32[]{:S(2)}) collective-permute-start(bf16[4,256,512]{2,1,0:T(8,128)(2,1)} %get-tuple-element.153), channel_id=1, source_target_pairs={{0,4},{4,0},{8,12},{12,8},{16,20},{20,16},{24,28},{28,24},{1,5},{5... | collective-permute-start | bytes 3145736 | tf_op jit(solution)/shard_map/ppermute | solution.py:509
  314.5 65.4 %collective-permute-start.55 = (bf16[80,2048]{1,0:T(8,128)(2,1)}, bf16[80,2048]{1,0:T(8,128)(2,1)}, u32[]{:S(2)}, u32[]{:S(2)}) collective-permute-start(bf16[80,2048]{1,0:T(8,128)(2,1)} %slice.404), channel_id=1, source_target_pairs={{0,4},{1,3},{2,6},{3,1},{4,0},{5,7},{6,2},{7,5},{8,12},{9,11},{10,... | collective-permute-start | bytes 983048 | tf_op jit(solution)/shard_map/ppermute | solution.py:528
  315.0 42.4 %collective-permute-start.52 = (bf16[4,128,512]{2,1,0:T(8,128)(2,1)S(1)}, bf16[4,128,512]{2,1,0:T(8,128)(2,1)S(1)}, u32[]{:S(2)}, u32[]{:S(2)}) collective-permute-start(bf16[4,128,512]{2,1,0:T(8,128)(2,1)S(1)} %copy-done.14), channel_id=1, source_target_pairs={{0,16},{4,20},{8,24},{12,28},{16,0},{20,4},{24,8},{28,12},{1,17},{... | collective-permute-start | bytes 1572872 | tf_op jit(solution)/shard_map/ppermute | solution.py:506
  319.7 37.7 %collective-permute-start.51 = (bf16[4,128,512]{2,1,0:T(8,128)(2,1)S(1)}, bf16[4,128,512]{2,1,0:T(8,128)(2,1)S(1)}, u32[]{:S(2)}, u32[]{:S(2)}) collective-permute-start(bf16[4,128,512]{2,1,0:T(8,128)(2,1)S(1)} %copy-done.14), channel_id=1, source_target_pairs={{0,8},{4,12},{8,0},{12,4},{16,24},{20,28},{24,16},{28,20},{1,9},{5... | collective-permute-start | bytes 1572872 | tf_op jit(solution)/shard_map/ppermute | solution.py:506
  370.5 25.7 %collective-permute-start.61 = (bf16[4,256,512]{2,1,0:T(8,128)(2,1)}, bf16[4,256,512]{2,1,0:T(8,128)(2,1)}, u32[]{:S(2)}, u32[]{:S(2)}) collective-permute-start(bf16[4,256,512]{2,1,0:T(8,128)(2,1)} %get-tuple-element.169), channel_id=1, source_target_pairs={{0,4},{4,0},{8,12},{12,8},{16,20},{20,16},{24,28},{28,24},{1,5},{5... | collective-permute-start | bytes 3145736 | tf_op jit(solution)/shard_map/ppermute | solution.py:509
  401.6 25.5 %collective-permute-start.63 = (bf16[128,512]{1,0:T(8,128)(2,1)S(1)}, bf16[128,512]{1,0:T(8,128)(2,1)S(1)}, u32[]{:S(2)}, u32[]{:S(2)}) collective-permute-start(bf16[128,512]{1,0:T(8,128)(2,1)S(1)} %fusion.54), channel_id=1, source_target_pairs={{0,0},{1,8},{2,16},{3,24},{4,4},{5,12},{6,20},{7,28},{8,1},{9,9},{... | collective-permute-start | bytes 393224 | tf_op jit(solution)/shard_map/ppermute | solution.py:520
  405.3 21.1 %collective-permute-start.62 = (bf16[128,512]{1,0:T(8,128)(2,1)S(1)}, bf16[128,512]{1,0:T(8,128)(2,1)S(1)}, u32[]{:S(2)}, u32[]{:S(2)}) collective-permute-start(bf16[128,512]{1,0:T(8,128)(2,1)S(1)} %fusion.34), channel_id=1, source_target_pairs={{0,0},{1,8},{2,16},{3,24},{4,4},{5,12},{6,20},{7,28},{8,1},{9,9},{... | collective-permute-start | bytes 393224 | tf_op jit(solution)/shard_map/ppermute | solution.py:520
  409.6 18.6 %collective-permute-start.71 = (bf16[2,256,512]{2,1,0:T(8,128)(2,1)}, bf16[2,256,512]{2,1,0:T(8,128)(2,1)S(1)}, u32[]{:S(2)}, u32[]{:S(2)}) collective-permute-start(bf16[2,256,512]{2,1,0:T(8,128)(2,1)} %get-tuple-element.196), channel_id=1, source_target_pairs={{0,4},{4,0},{8,12},{12,8},{16,20},{20,16},{24,28},{28,24},{1,5},{5... | collective-permute-start | bytes 1572872 | tf_op jit(solution)/shard_map/ppermute | solution.py:509
  (112 other events, 1366.2 us)

commit v3 on v2

--- a/solution.py
+++ b/solution.py
@@ -88,9 +88,10 @@
 
 def key_value_body(subs):
     def body(at, *refs):
-        rows, gain, router, parts = refs[:E], refs[E], refs[E + 1], refs[E + 2 : E + 2 + subs]
-        gained, own_stats, *outs = refs[E + 2 + subs : E + 4 + subs + E]
-        weights, total, stats = refs[E + 4 + subs + E :]
+        rows, gain, router, routes = refs[:E], refs[E], refs[E + 1], refs[E + 2]
+        parts = refs[E + 3 : E + 3 + subs]
+        gained, own_stats, *outs = refs[E + 3 + subs : E + 5 + subs + E]
+        weights, total, stats = refs[E + 5 + subs + E :]
         place(weights, parts, at[1])
         for q in range(E):
             wide = rows[q][...].astype(F32)
@@ -117,6 +118,13 @@
                 pair = jnp.concatenate([high, mine - high], axis=0).astype(BF16)
                 outs[k][2 * TOK :, :] = jnp.zeros((16, outs[k].shape[1]), BF16)
                 outs[k][2 * TOK :, 0:TOK] = pair
+                for first in range(0, subs, 4):
+                    lines = [
+                        routes[j][0:4].astype(F32) if j < subs else jnp.zeros((4, TOK), F32)
+                        for j in range(first, first + 4)
+                    ]
+                    start = (1 + first // 4) * TOK
+                    outs[k][2 * TOK :, start : start + TOK] = jnp.concatenate(lines, axis=0).astype(BF16)
 
     return body
 
@@ -338,7 +346,12 @@
         expert = lax.broadcasted_iota(jnp.int32, (E, TOK), 0).astype(F32)
         for k in range(E):
             for j in range(subs):
-                line = tables[k][j].astype(F32)
+                if k == 0:
+                    line = tables[0][j].astype(F32)
+                else:
+                    first = (1 + j // 4) * TOK
+                    lines = tables[k][2 * TOK :, first : first + TOK].astype(F32)
+                    line = lines[(j % 4) * 4 : (j % 4) * 4 + 4]
                 ones = [(line[r : r + 1] == expert).astype(F32) for r in range(4)]
                 start = (k * subs + j) * 8
                 both[start : start + 4, :] = ones[0] + ones[1]
@@ -595,26 +608,8 @@
     gain_two_plane = near[5].astype(F32)
     router_two_plane = near[6:10].astype(F32)
 
+    route_parts = parts[:, :8, :TOK]
     at = jnp.stack([narrow ^ plane, sub, plane, narrow]).astype(jnp.int32)
-    line_count = wide_count * 8
-    hot_cols, home_hot, turned_hot, mlp_cols, expert_hot, select = run(
-        "route",
-        route_body(subs, capacity),
-        [
-            shape((E * TOK, 8), F32),
-            shape((16, TOK), F32),
-            shape((16, TOK), F32),
-            shape((TOK, 8), F32),
-            shape((8, TOK), F32),
-            shape((E, SLOTS, TOK), BF16),
-        ],
-        [at, *gather_planes(parts[:, :8, :TOK])],
-        [pltpu.VMEM((line_count, TOK), F32)] * 3 + [pltpu.VMEM((E, 8, TOK), F32)] * 2,
-    )
-    hot_one, keep_one = home_hot[0:8].reshape(TOPK, E, TOK), home_hot[8:10]
-    hot_two, keep_two = turned_hot[0:8].reshape(TOPK, E, TOK), turned_hot[8:10]
-    hot_two_k = expert_hot.reshape(E, TOPK, TOK)
-
     kv_parts = gather_subs(key_value)
     query_parts = gather_subs(query_proj, kv_parts[-1])
     out_parts = gather_subs(output_proj, query_parts[-1])
@@ -634,6 +629,7 @@
             *all_streams,
             gain_one_plane[None],
             jnp.pad(router_one_plane, ((0, 4), (0, 0))),
+            route_parts,
             *kv_parts,
         ],
         [
@@ -644,6 +640,25 @@
     )
     turned_grad = swap(after(out_grad, own_stats))
     kv_blocks = exchange_planes(kv_blocks)
+    line_count = wide_count * 8
+    hot_cols, home_hot, turned_hot, mlp_cols, expert_hot, select = run(
+        "route",
+        route_body(subs, capacity),
+        [
+            shape((E * TOK, 8), F32),
+            shape((16, TOK), F32),
+            shape((16, TOK), F32),
+            shape((TOK, 8), F32),
+            shape((8, TOK), F32),
+            shape((E, SLOTS, TOK), BF16),
+        ],
+        [at, route_parts, *kv_blocks[1:]],
+        [pltpu.VMEM((line_count, TOK), F32)] * 3 + [pltpu.VMEM((E, 8, TOK), F32)] * 2,
+    )
+    hot_one, keep_one = home_hot[0:8].reshape(TOPK, E, TOK), home_hot[8:10]
+    hot_two, keep_two = turned_hot[0:8].reshape(TOPK, E, TOK), turned_hot[8:10]
+    hot_two_k = expert_hot.reshape(E, TOPK, TOK)
+
     routed_scratch = [
         pltpu.VMEM((E, slice_width, local_width), BF16),
         pltpu.VMEM((TOPK, rows_all, local_width), F32),
@@ -652,7 +667,7 @@
         "query",
         routed_body(subs, True),
         [kept_own] + [sent] * (E - 1),
-        [at, after(gained, *kv_blocks[1:]), hot_cols, *query_parts],
+        [at, gained, hot_cols, *query_parts],
         routed_scratch,
     )
     query_blocks = exchange_planes(query_blocks)
@@ -897,7 +912,7 @@
     kv_grad_parts = run(
         "key_value_grad", weight_grad_body, weight_parts(2), [at, gained, dkv_all], weight_scratch
     )
-    kv_grad, _ = weight_sum(after(kv_grad_parts, query_got))
+    kv_grad, kv_got = weight_sum(after(kv_grad_parts, query_got))
     keep, got, other = after(reduce_narrow(*dnormed_one), kv_grad_parts[-1], query_got)
     dnormed_one = keep + got[0].astype(F32) + other.astype(F32)
     turned_out = dhidden + dnormed_one * gain_one_plane
@@ -909,7 +924,7 @@
     )
 
     small = jnp.concatenate([mlp_terms, gain_row, router_term], axis=0)
-    small = sum_subs(sum_narrow(after(small, query_got)))
+    small = sum_subs(after(sum_narrow(small), kv_got))
     mine = lax.dynamic_slice_in_dim(small, sub * shard_rows, shard_rows, 1)
     router_one_grad = mine[6:10]
     gain_one_grad = mine[5] + jnp.sum(

time: 433 us -> 425 us (0.982)
  waiting for transfers between devices: 178 us -> 166 us
    ppermute x32 -> x29, waiting for transfers between devices: 106 us -> 97 us  [by_plane(): lax.ppermute(values, 'wide', [(i, i ^ k * subs) for i in range(wide_count)])]
    ppermute x32 -> x29, starting transfers between devices: 56.7 us -> 55.3 us  [by_plane(): lax.ppermute(values, 'wide', [(i, i ^ k * subs) for i in range(wide_count)])]
  transfers between devices with their start and end apart: 72 -> 69, of which waited for: 35 -> 35; matrix products, arithmetic and copies ran while one was open for 13% -> 14% of each run, Pallas kernels for 12% -> 13%
where the time goes in v3:
time: 425 us; the launch traced here: 422 us
  waiting for transfers between devices  166 us (39%)
  starting transfers between devices  97.6 us (23%)
  Pallas kernels  61.8 us (15%)
  matrix products  47.1 us (11%)
  other arithmetic  32.6 us (8%)
  local copies, waits for them, and re-layouts  14.4 us (3%)
    ppermute x29, waiting for transfers between devices, by_plane(): lax.ppermute(values, 'wide', [(i, i ^ k * subs) for i in range(wide_count)])  97 us
    pallas_call x16, Pallas kernels, run(): pl.pallas_call(body, out_shape=tuple(outs), in_specs=[pl.BlockSpec(memory...  61.8 us
    ppermute x29, starting transfers between devices, by_plane(): lax.ppermute(values, 'wide', [(i, i ^ k * subs) for i in range(wide_count)])  55.3 us
    ppermute x8, waiting for transfers between devices, by_side(): return lax.ppermute(values, ('wide', 'narrow'), pairs)  25.6 us
    ppermute x18, waiting for transfers between devices, by_narrow(): lax.ppermute(values, 'narrow', [(i, i ^ k) for i in range(narrow_count)])  24.6 us
    ppermute x6, starting transfers between devices, swap(): return lax.ppermute(values, ('wide', 'narrow'), pairs)  22.4 us
    dot_general x7, matrix products, dot(): lax.dot_general(left, right, ((contract[0], contract[1]), ((), ())), prec...  17.9 us
    dot_general x1, matrix products, local(): jnp.einsum('krf,dkf->rd', jnp.stack([dgate_pre, dup_pre]), weight_in, pre...  14.5 us
  transfers between devices with their start and end apart: 69, of which 35 were waited for; matrix products, arithmetic and copies ran while one was open for 14% of the time, Pallas kernels for 13%

profile of v3, /device:TPU:2, one launch (start us, length us, event | category | flops | bytes accessed | tf_op | source)
XLA Modules:
  0.0 421.6 jit_solution(8375141034120965472)
XLA Ops:
  38.2 7.6 %collective-permute-done.6.refs_1_.refs_0_ = bf16[272,512]{1,0:T(8,128)(2,1)S(1)} collective-permute-done((bf16[272,512]{1,0:T(8,128)(2,1)}, bf16[272,512]{1,0:T(8,128)(2,1)S(1)}, u32[]{:S(2)}, u32[]{:S(2)}) %collective-permute-start.6) | collective-permute-done | bytes 278560 | tf_op jit(solution)/shard_map/ppermute | solution.py:519
  45.8 8.7 %collective-permute-done.7.refs_2_.refs_1_ = bf16[272,512]{1,0:T(8,128)(2,1)} collective-permute-done((bf16[272,512]{1,0:T(8,128)(2,1)}, bf16[272,512]{1,0:T(8,128)(2,1)}, u32[]{:S(2)}, u32[]{:S(2)}) %collective-permute-start.7) | collective-permute-done | bytes 278560 | tf_op jit(solution)/shard_map/ppermute | solution.py:519
  62.2 7.9 %collective-permute-start.10 = (bf16[2,128,512]{2,1,0:T(8,128)(2,1)}, bf16[2,128,512]{2,1,0:T(8,128)(2,1)S(1)}, u32[]{:S(2)}, u32[]{:S(2)}) collective-permute-start(bf16[2,128,512]{2,1,0:T(8,128)(2,1)} %get-tuple-element.112), channel_id=1, source_target_pairs={{0,8},{4,12},{8,0},{12,4},{16,24},{20,28},{24,16},{28,20},{1,9},{5... | collective-permute-start | bytes 786440 | tf_op jit(solution)/shard_map/ppermute | solution.py:519
  81.4 13.8 %collective-permute-done.11.refs_5_ = bf16[2,128,512]{2,1,0:T(8,128)(2,1)} collective-permute-done((bf16[2,128,512]{2,1,0:T(8,128)(2,1)}, bf16[2,128,512]{2,1,0:T(8,128)(2,1)}, u32[]{:S(2)}, u32[]{:S(2)}) %collective-permute-start.11) | collective-permute-done | bytes 262176 | tf_op jit(solution)/shard_map/ppermute | solution.py:519
  96.0 5.4 %attention.1 = (f32[16,128]{1,0:T(8,128)}, bf16[4,128,512]{2,1,0:T(8,128)(2,1)}, f32[4,256,128]{2,1,0:T(8,128)}, bf16[2,128,512]{2,1,0:T(8,128)(2,1)}, bf16[2,128,512]{2,1,0:T(8,128)(2,1)}) custom-call(s32[4]{0:T(128)} %bitcast.191, f32[2,128,512]{2,1,0:T(8,128)} %get-tuple-element.104.own_kv, bf16[272,512]{1,0:T(8,128)(2,1)} %copy-done.25, ...), custom_call_target="tpu_custom_call" | custom-call | flops 1 | bytes 1 | tf_op jit(solution)/shard_map/attention/pallas_call | solution.py:52
  116.2 14.2 %collective-permute-done.14.refs_2_ = bf16[2,128,512]{2,1,0:T(8,128)(2,1)} collective-permute-done((bf16[2,128,512]{2,1,0:T(8,128)(2,1)}, bf16[2,128,512]{2,1,0:T(8,128)(2,1)}, u32[]{:S(2)}, u32[]{:S(2)}) %collective-permute-start.14) | collective-permute-done | bytes 262176 | tf_op jit(solution)/shard_map/ppermute | solution.py:519
  139.5 4.7 %collective-permute-done.18.other = bf16[128,512]{1,0:T(8,128)(2,1)} collective-permute-done((bf16[128,512]{1,0:T(8,128)(2,1)S(1)}, bf16[128,512]{1,0:T(8,128)(2,1)}, u32[]{:S(2)}, u32[]{:S(2)}) %collective-permute-start.18) | collective-permute-done | bytes 131104 | tf_op jit(solution)/shard_map/ppermute | solution.py:525
  153.0 5.4 %collective-permute-done.26.refs_2_ = bf16[80,640]{1,0:T(8,128)(2,1)} collective-permute-done((bf16[80,640]{1,0:T(8,128)(2,1)}, bf16[80,640]{1,0:T(8,128)(2,1)}, u32[]{:S(2)}, u32[]{:S(2)}) %collective-permute-start.26) | collective-permute-done | bytes 102432 | tf_op jit(solution)/shard_map/ppermute | solution.py:519
  161.6 6.9 %collective-permute-done.28 = bf16[80,2176]{1,0:T(8,128)(2,1)S(1)} collective-permute-done((bf16[80,2176]{1,0:T(8,128)(2,1)}, bf16[80,2176]{1,0:T(8,128)(2,1)S(1)}, u32[]{:S(2)}, u32[]{:S(2)}) %collective-permute-start.28) | collective-permute-done | bytes 348192 | tf_op jit(solution)/shard_map/ppermute | solution.py:541
  171.5 9.2 %collective-permute-done.29 = bf16[160,2176]{1,0:T(8,128)(2,1)S(1)} collective-permute-done((bf16[160,2176]{1,0:T(8,128)(2,1)S(1)}, bf16[160,2176]{1,0:T(8,128)(2,1)S(1)}, u32[]{:S(2)}, u32[]{:S(2)}) %collective-permute-start.29) | collective-permute-done | bytes 696352 | tf_op jit(solution)/shard_map/ppermute | solution.py:541
  193.9 4.8 %fusion.18 = f32[2,640,704]{1,2,0:T(8,128)S(1)} fusion(bf16[1,2048,2,704]{1,3,2,0:T(8,128)(2,1)S(1)} %bitcast.193, bf16[640,2176]{1,0:T(8,128)(2,1)S(1)} %pad_maximum_fusion.1), kind=kOutput, calls=%fused_computation.32 | convolution fusion | flops 3690987520 | bytes 11993088 | tf_op jit(solution)/shard_map/rd,dkf->krf/dot_general | solution.py:757
  202.5 14.5 %fusion.4 = f32[640,2048]{1,0:T(8,128)S(1)} fusion(bf16[1,2048,2,704]{1,3,2,0:T(8,128)(2,1)S(1)} %bitcast.193, bf16[1,640,704]{1,2,0:T(8,128)(2,1)S(1)} %bitcast.159, bf16[1,640,704]{1,2,0:T(8,128)(2,1)S(1)} %bitcast.160), kind=kOutput, calls=%fused_computation.7 | convolution fusion | flops 3691888640 | bytes 12812288 | tf_op jit(solution)/shard_map/krf,dkf->rd/dot_general | solution.py:768
  238.4 5.9 %collective-permute-done.38.got = bf16[80,2176]{1,0:T(8,128)(2,1)} collective-permute-done((bf16[80,2176]{1,0:T(8,128)(2,1)S(1)}, bf16[80,2176]{1,0:T(8,128)(2,1)}, u32[]{:S(2)}, u32[]{:S(2)}) %collective-permute-start.38) | collective-permute-done | bytes 348192 | tf_op jit(solution)/shard_map/ppermute | solution.py:541
  274.9 4.8 %output_grad.1 = (f32[4,256,512]{2,1,0:T(8,128)}, bf16[4,256,512]{2,1,0:T(8,128)(2,1)}) custom-call(s32[4]{0:T(128)} %pad_add_fusion.at, bf16[512,512]{1,0:T(8,128)(2,1)} %get-tuple-element.149.rows, bf16[4,512,512]{2,1,0:T(8,128)(2,1)} %get-tuple-element.150.other), custom_call_target="tpu_custom_call" | custom-call | flops 1 | bytes 1 | tf_op jit(solution)/shard_map/output_grad/pallas_call | solution.py:52
  280.7 6.8 %fusion.39 = f32[704,2048]{1,0:T(8,128)} fusion(bf16[640,704]{0,1:T(8,128)(2,1)} %get-tuple-element.152, bf16[320,2048]{1,0:T(8,128)(2,1)} %copy-done.58, bf16[160,2048]{1,0:T(8,128)(2,1)} %collective-permute-done.24, bf16[80,2048]{1,0:T(8,128)(2,1)} %copy-done.20, bf16[80,2048]{1,0:T(8,128)(2,1)S(1)} %copy-done.12), kind=kOutput, calls=%fused_computation.73 | convolution fusion | flops 1855979520 | bytes 9289728 | tf_op jit(solution)/shard_map/dot_general | solution.py:22
  287.4 6.4 %collective-permute-done.46.refs_1_ = bf16[2,128,512]{2,1,0:T(8,128)(2,1)} collective-permute-done((bf16[2,128,512]{2,1,0:T(8,128)(2,1)}, bf16[2,128,512]{2,1,0:T(8,128)(2,1)}, u32[]{:S(2)}, u32[]{:S(2)}) %collective-permute-start.46) | collective-permute-done | bytes 262176 | tf_op jit(solution)/shard_map/ppermute | solution.py:519
  293.8 5.1 %attention_back.1 = (bf16[4,128,512]{2,1,0:T(8,128)(2,1)}, f32[8,128]{1,0:T(8,128)}) custom-call(s32[4]{0:T(128)} %pad_add_fusion.at, f32[2,128,512]{2,1,0:T(8,128)} %get-tuple-element.153.own, bf16[2,128,512]{2,1,0:T(8,128)(2,1)} %collective-permute-done.45.refs_0_, bf16[2,128,512]{2,1,0:T(8,128)(2,1)} %collective-permute-done.46.refs_1_, ...), custom_call_target="tpu_custom_call" | custom-call | flops 1 | bytes 1 | tf_op jit(solution)/shard_map/attention_back/pallas_call | solution.py:52
  305.5 4.7 %collective-permute-start.49 = (bf16[4,128,512]{2,1,0:T(8,128)(2,1)S(1)}, bf16[4,128,512]{2,1,0:T(8,128)(2,1)S(1)}, u32[]{:S(2)}, u32[]{:S(2)}) collective-permute-start(bf16[4,128,512]{2,1,0:T(8,128)(2,1)S(1)} %copy-done.15), channel_id=1, source_target_pairs={{0,16},{4,20},{8,24},{12,28},{16,0},{20,4},{24,8},{28,12},{1,17},{... | collective-permute-start | bytes 1572872 | tf_op jit(solution)/shard_map/ppermute | solution.py:519
  310.2 5.2 %collective-permute-done.50.refs_3_ = bf16[4,128,512]{2,1,0:T(8,128)(2,1)} collective-permute-done((bf16[4,128,512]{2,1,0:T(8,128)(2,1)}, bf16[4,128,512]{2,1,0:T(8,128)(2,1)}, u32[]{:S(2)}, u32[]{:S(2)}) %collective-permute-start.50) | collective-permute-done | bytes 524320 | tf_op jit(solution)/shard_map/ppermute | solution.py:519
  315.4 9.0 %fusion.13 = f32[2048,2,704]{0,2,1:T(8,128)} fusion(bf16[640,2,704]{0,2,1:T(8,128)(2,1)} %pad_maximum_fusion.3, bf16[640,2176]{1,0:T(8,128)(2,1)S(1)} %copy-done.11), kind=kOutput, calls=%fused_computation.19 | convolution fusion | flops 3690987520 | bytes 15958016 | tf_op jit(solution)/shard_map/rd,rkf->dkf/dot_general | solution.py:877
  324.4 22.7 %collective-permute-done.49.refs_2_ = bf16[4,128,512]{2,1,0:T(8,128)(2,1)S(1)} collective-permute-done((bf16[4,128,512]{2,1,0:T(8,128)(2,1)S(1)}, bf16[4,128,512]{2,1,0:T(8,128)(2,1)S(1)}, u32[]{:S(2)}, u32[]{:S(2)}) %collective-permute-start.49) | collective-permute-done | bytes 524320 | tf_op jit(solution)/shard_map/ppermute | solution.py:519
  348.1 5.3 %query_grad.1 = (bf16[4,512,512]{2,1,0:T(8,128)(2,1)}, f32[4,256,512]{2,1,0:T(8,128)}, bf16[4,256,512]{2,1,0:T(8,128)(2,1)}) custom-call(s32[4]{0:T(128)} %pad_add_fusion.at, bf16[512,512]{1,0:T(8,128)(2,1)} %get-tuple-element.108.refs_0_.rows, f32[512,8]{1,0:T(8,128)} %get-tuple-element.109.refs_1_.refs_4_.hot, ...), custom_call_target="tpu_custom_call" | custom-call | flops 1 | bytes 1 | tf_op jit(solution)/shard_map/query_grad/pallas_call | solution.py:52
  353.4 6.2 %input.1 = (bf16[2,512,512]{2,1,0:T(8,128)(2,1)}, f32[1,512]{1,0:T(1,128)}, f32[128,512]{1,0:T(8,128)}, f32[128,512]{1,0:T(8,128)}, bf16[2,128,512]{2,1,0:T(8,128)(2,1)}) custom-call(s32[4]{0:T(128)} %pad_add_fusion.at, bf16[4,128,512]{2,1,0:T(8,128)(2,1)} %get-tuple-element.168.refs_0_, bf16[4,128,512]{2,1,0:T(8,128)(2,1)} %copy-done.17, ...), custom_call_target="tpu_custom_call" | custom-call | flops 1 | bytes 1 | tf_op jit(solution)/shard_map/input/pallas_call | solution.py:52
  404.8 4.9 %collective-permute-done.59 = bf16[128,512]{1,0:T(8,128)(2,1)S(1)} collective-permute-done((bf16[128,512]{1,0:T(8,128)(2,1)S(1)}, bf16[128,512]{1,0:T(8,128)(2,1)S(1)}, u32[]{:S(2)}, u32[]{:S(2)}) %collective-permute-start.59) | collective-permute-done | bytes 131104 | tf_op jit(solution)/shard_map/ppermute | solution.py:533
  (353 shorter events, 229.7 us)
Async XLA Ops:
  15.7 41.0 %collective-permute-start.9 = (bf16[4,256,512]{2,1,0:T(8,128)(2,1)}, bf16[4,256,512]{2,1,0:T(8,128)(2,1)}, u32[]{:S(2)}, u32[]{:S(2)}) collective-permute-start(bf16[4,256,512]{2,1,0:T(8,128)(2,1)} %refs_7_.3), channel_id=1, source_target_pairs={{0,4},{4,0},{8,12},{12,8},{16,20},{20,16},{24,28},{28,24},{1,5},{5... | collective-permute-start | bytes 3145736 | tf_op jit(solution)/shard_map/ppermute | solution.py:522
  31.8 22.7 %collective-permute-start.7 = (bf16[272,512]{1,0:T(8,128)(2,1)}, bf16[272,512]{1,0:T(8,128)(2,1)}, u32[]{:S(2)}, u32[]{:S(2)}) collective-permute-start(bf16[272,512]{1,0:T(8,128)(2,1)} %get-tuple-element.106), channel_id=1, source_target_pairs={{0,16},{4,20},{8,24},{12,28},{16,0},{20,4},{24,8},{28,12},{1,17},{... | collective-permute-start | bytes 835592 | tf_op jit(solution)/shard_map/ppermute | solution.py:519
  34.4 20.1 %collective-permute-start.8 = (bf16[272,512]{1,0:T(8,128)(2,1)}, bf16[272,512]{1,0:T(8,128)(2,1)}, u32[]{:S(2)}, u32[]{:S(2)}) collective-permute-start(bf16[272,512]{1,0:T(8,128)(2,1)} %get-tuple-element.107), channel_id=1, source_target_pairs={{0,24},{4,28},{8,16},{12,20},{16,8},{20,12},{24,0},{28,4},{1,25},{... | collective-permute-start | bytes 835592 | tf_op jit(solution)/shard_map/ppermute | solution.py:519
  35.4 36.7 %collective-permute-start.19 = (bf16[128,512]{1,0:T(8,128)(2,1)}, bf16[128,512]{1,0:T(8,128)(2,1)S(1)}, u32[]{:S(2)}, u32[]{:S(2)}) collective-permute-start(bf16[128,512]{1,0:T(8,128)(2,1)} %param.15), channel_id=1, source_target_pairs={{0,0},{1,8},{2,16},{3,24},{4,4},{5,12},{6,20},{7,28},{8,1},{9,9},{... | collective-permute-start | bytes 393224 | tf_op jit(solution)/shard_map/ppermute | solution.py:533
  56.7 73.7 %collective-permute-start.16 = (bf16[4,256,512]{2,1,0:T(8,128)(2,1)}, bf16[4,256,512]{2,1,0:T(8,128)(2,1)}, u32[]{:S(2)}, u32[]{:S(2)}) collective-permute-start(bf16[4,256,512]{2,1,0:T(8,128)(2,1)} %refs_5_.4), channel_id=1, source_target_pairs={{0,4},{4,0},{8,12},{12,8},{16,20},{20,16},{24,28},{28,24},{1,5},{5... | collective-permute-start | bytes 3145736 | tf_op jit(solution)/shard_map/ppermute | solution.py:522
  62.2 17.1 %collective-permute-start.10 = (bf16[2,128,512]{2,1,0:T(8,128)(2,1)}, bf16[2,128,512]{2,1,0:T(8,128)(2,1)S(1)}, u32[]{:S(2)}, u32[]{:S(2)}) collective-permute-start(bf16[2,128,512]{2,1,0:T(8,128)(2,1)} %get-tuple-element.112), channel_id=1, source_target_pairs={{0,8},{4,12},{8,0},{12,4},{16,24},{20,28},{24,16},{28,20},{1,9},{5... | collective-permute-start | bytes 786440 | tf_op jit(solution)/shard_map/ppermute | solution.py:519
  70.1 25.1 %collective-permute-start.11 = (bf16[2,128,512]{2,1,0:T(8,128)(2,1)}, bf16[2,128,512]{2,1,0:T(8,128)(2,1)}, u32[]{:S(2)}, u32[]{:S(2)}) collective-permute-start(bf16[2,128,512]{2,1,0:T(8,128)(2,1)} %get-tuple-element.113), channel_id=1, source_target_pairs={{0,16},{4,20},{8,24},{12,28},{16,0},{20,4},{24,8},{28,12},{1,17},{... | collective-permute-start | bytes 786440 | tf_op jit(solution)/shard_map/ppermute | solution.py:519
  72.3 23.0 %collective-permute-start.12 = (bf16[2,128,512]{2,1,0:T(8,128)(2,1)}, bf16[2,128,512]{2,1,0:T(8,128)(2,1)S(1)}, u32[]{:S(2)}, u32[]{:S(2)}) collective-permute-start(bf16[2,128,512]{2,1,0:T(8,128)(2,1)} %get-tuple-element.114), channel_id=1, source_target_pairs={{0,24},{4,28},{8,16},{12,20},{16,8},{20,12},{24,0},{28,4},{1,25},{... | collective-permute-start | bytes 786440 | tf_op jit(solution)/shard_map/ppermute | solution.py:519
  74.6 26.9 %collective-permute-start.22 = (bf16[80,512]{1,0:T(8,128)(2,1)}, bf16[80,512]{1,0:T(8,128)(2,1)}, u32[]{:S(2)}, u32[]{:S(2)}) collective-permute-start(bf16[80,512]{1,0:T(8,128)(2,1)} %get-tuple-element.215), channel_id=1, source_target_pairs={{0,24},{4,28},{8,16},{12,20},{16,8},{20,12},{24,0},{28,4},{1,25},{... | collective-permute-start | bytes 245768 | tf_op jit(solution)/shard_map/ppermute | solution.py:519
  79.3 22.2 %collective-permute-start.21 = (bf16[80,512]{1,0:T(8,128)(2,1)}, bf16[80,512]{1,0:T(8,128)(2,1)}, u32[]{:S(2)}, u32[]{:S(2)}) collective-permute-start(bf16[80,512]{1,0:T(8,128)(2,1)} %get-tuple-element.216), channel_id=1, source_target_pairs={{0,16},{4,20},{8,24},{12,28},{16,0},{20,4},{24,8},{28,12},{1,17},{... | collective-permute-start | bytes 245768 | tf_op jit(solution)/shard_map/ppermute | solution.py:519
  108.3 22.1 %collective-permute-start.14 = (bf16[2,128,512]{2,1,0:T(8,128)(2,1)}, bf16[2,128,512]{2,1,0:T(8,128)(2,1)}, u32[]{:S(2)}, u32[]{:S(2)}) collective-permute-start(bf16[2,128,512]{2,1,0:T(8,128)(2,1)} %get-tuple-element.117.refs_0_), channel_id=1, source_target_pairs={{0,16},{4,20},{8,24},{12,28},{16,0},{20,4},{24,8},{28,12},{1,17},{... | collective-permute-start | bytes 786440 | tf_op jit(solution)/shard_map/ppermute | solution.py:519
  111.7 18.7 %collective-permute-start.13 = (bf16[2,128,512]{2,1,0:T(8,128)(2,1)}, bf16[2,128,512]{2,1,0:T(8,128)(2,1)}, u32[]{:S(2)}, u32[]{:S(2)}) collective-permute-start(bf16[2,128,512]{2,1,0:T(8,128)(2,1)} %get-tuple-element.117.refs_0_), channel_id=1, source_target_pairs={{0,8},{4,12},{8,0},{12,4},{16,24},{20,28},{24,16},{28,20},{1,9},{5... | collective-permute-start | bytes 786440 | tf_op jit(solution)/shard_map/ppermute | solution.py:519
  114.2 25.2 %collective-permute-start.24 = (bf16[160,2048]{1,0:T(8,128)(2,1)}, bf16[160,2048]{1,0:T(8,128)(2,1)}, u32[]{:S(2)}, u32[]{:S(2)}) collective-permute-start(bf16[160,2048]{1,0:T(8,128)(2,1)} %pad_maximum_fusion.7), channel_id=1, source_target_pairs={{0,2},{1,5},{2,0},{3,7},{4,6},{5,1},{6,4},{7,3},{8,10},{9,13},{10,... | collective-permute-start | bytes 1966088 | tf_op jit(solution)/shard_map/ppermute | solution.py:541
  171.4 17.6 %collective-permute-start.35 = (bf16[320,2048]{1,0:T(8,128)(2,1)S(1)}, bf16[320,2048]{1,0:T(8,128)(2,1)S(1)}, u32[]{:S(2)}, u32[]{:S(2)}) collective-permute-start(bf16[320,2048]{1,0:T(8,128)(2,1)S(1)} %pad_maximum_fusion.5), channel_id=1, source_target_pairs={{0,1},{1,0},{2,3},{3,2},{4,5},{5,4},{6,7},{7,6},{8,9},{9,8},{10,11... | collective-permute-start | bytes 3932168 | tf_op jit(solution)/shard_map/ppermute | solution.py:525
  261.2 39.5 %collective-permute-start.34 = (bf16[160,2048]{1,0:T(8,128)(2,1)}, bf16[160,2048]{1,0:T(8,128)(2,1)}, u32[]{:S(2)}, u32[]{:S(2)}) collective-permute-start(bf16[160,2048]{1,0:T(8,128)(2,1)} %slice.402), channel_id=1, source_target_pairs={{0,2},{1,5},{2,0},{3,7},{4,6},{5,1},{6,4},{7,3},{8,10},{9,13},{10,... | collective-permute-start | bytes 1966088 | tf_op jit(solution)/shard_map/ppermute | solution.py:541
  272.2 21.7 %collective-permute-start.46 = (bf16[2,128,512]{2,1,0:T(8,128)(2,1)}, bf16[2,128,512]{2,1,0:T(8,128)(2,1)}, u32[]{:S(2)}, u32[]{:S(2)}) collective-permute-start(bf16[2,128,512]{2,1,0:T(8,128)(2,1)} %get-tuple-element.147), channel_id=1, source_target_pairs={{0,16},{4,20},{8,24},{12,28},{16,0},{20,4},{24,8},{28,12},{1,17},{... | collective-permute-start | bytes 786440 | tf_op jit(solution)/shard_map/ppermute | solution.py:519
  273.0 20.8 %collective-permute-start.47 = (bf16[2,128,512]{2,1,0:T(8,128)(2,1)}, bf16[2,128,512]{2,1,0:T(8,128)(2,1)}, u32[]{:S(2)}, u32[]{:S(2)}) collective-permute-start(bf16[2,128,512]{2,1,0:T(8,128)(2,1)} %get-tuple-element.148), channel_id=1, source_target_pairs={{0,24},{4,28},{8,16},{12,20},{16,8},{20,12},{24,0},{28,4},{1,25},{... | collective-permute-start | bytes 786440 | tf_op jit(solution)/shard_map/ppermute | solution.py:519
  279.7 67.5 %collective-permute-start.51 = (bf16[4,256,512]{2,1,0:T(8,128)(2,1)}, bf16[4,256,512]{2,1,0:T(8,128)(2,1)}, u32[]{:S(2)}, u32[]{:S(2)}) collective-permute-start(bf16[4,256,512]{2,1,0:T(8,128)(2,1)} %get-tuple-element.151), channel_id=1, source_target_pairs={{0,4},{4,0},{8,12},{12,8},{16,20},{20,16},{24,28},{28,24},{1,5},{5... | collective-permute-start | bytes 3145736 | tf_op jit(solution)/shard_map/ppermute | solution.py:522
  303.7 60.9 %collective-permute-start.52 = (bf16[80,2048]{1,0:T(8,128)(2,1)}, bf16[80,2048]{1,0:T(8,128)(2,1)}, u32[]{:S(2)}, u32[]{:S(2)}) collective-permute-start(bf16[80,2048]{1,0:T(8,128)(2,1)} %slice.404), channel_id=1, source_target_pairs={{0,4},{1,3},{2,6},{3,1},{4,0},{5,7},{6,2},{7,5},{8,12},{9,11},{10,... | collective-permute-start | bytes 983048 | tf_op jit(solution)/shard_map/ppermute | solution.py:541
  305.5 41.6 %collective-permute-start.49 = (bf16[4,128,512]{2,1,0:T(8,128)(2,1)S(1)}, bf16[4,128,512]{2,1,0:T(8,128)(2,1)S(1)}, u32[]{:S(2)}, u32[]{:S(2)}) collective-permute-start(bf16[4,128,512]{2,1,0:T(8,128)(2,1)S(1)} %copy-done.15), channel_id=1, source_target_pairs={{0,16},{4,20},{8,24},{12,28},{16,0},{20,4},{24,8},{28,12},{1,17},{... | collective-permute-start | bytes 1572872 | tf_op jit(solution)/shard_map/ppermute | solution.py:519
  310.2 36.9 %collective-permute-start.48 = (bf16[4,128,512]{2,1,0:T(8,128)(2,1)S(1)}, bf16[4,128,512]{2,1,0:T(8,128)(2,1)S(1)}, u32[]{:S(2)}, u32[]{:S(2)}) collective-permute-start(bf16[4,128,512]{2,1,0:T(8,128)(2,1)S(1)} %copy-done.15), channel_id=1, source_target_pairs={{0,8},{4,12},{8,0},{12,4},{16,24},{20,28},{24,16},{28,20},{1,9},{5... | collective-permute-start | bytes 1572872 | tf_op jit(solution)/shard_map/ppermute | solution.py:519
  363.6 27.6 %collective-permute-start.58 = (bf16[4,256,512]{2,1,0:T(8,128)(2,1)}, bf16[4,256,512]{2,1,0:T(8,128)(2,1)S(1)}, u32[]{:S(2)}, u32[]{:S(2)}) collective-permute-start(bf16[4,256,512]{2,1,0:T(8,128)(2,1)} %get-tuple-element.167), channel_id=1, source_target_pairs={{0,4},{4,0},{8,12},{12,8},{16,20},{20,16},{24,28},{28,24},{1,5},{5... | collective-permute-start | bytes 3145736 | tf_op jit(solution)/shard_map/ppermute | solution.py:522
  366.8 23.0 %collective-permute-start.53 = (bf16[80,512]{1,0:T(8,128)(2,1)}, bf16[80,512]{1,0:T(8,128)(2,1)S(1)}, u32[]{:S(2)}, u32[]{:S(2)}) collective-permute-start(bf16[80,512]{1,0:T(8,128)(2,1)} %get-tuple-element.176), channel_id=1, source_target_pairs={{0,8},{4,12},{8,0},{12,4},{16,24},{20,28},{24,16},{28,20},{1,9},{5... | collective-permute-start | bytes 245768 | tf_op jit(solution)/shard_map/ppermute | solution.py:519
  366.8 23.0 %collective-permute-start.54 = (bf16[80,512]{1,0:T(8,128)(2,1)}, bf16[80,512]{1,0:T(8,128)(2,1)S(1)}, u32[]{:S(2)}, u32[]{:S(2)}) collective-permute-start(bf16[80,512]{1,0:T(8,128)(2,1)} %get-tuple-element.177), channel_id=1, source_target_pairs={{0,16},{4,20},{8,24},{12,28},{16,0},{20,4},{24,8},{28,12},{1,17},{... | collective-permute-start | bytes 245768 | tf_op jit(solution)/shard_map/ppermute | solution.py:519
  (109 other events, 1215.1 us)

commit v4 on v3

--- a/solution.py
+++ b/solution.py
@@ -60,12 +60,35 @@
     )(*args)
 
 
+def loop(count, step):
+    def one(i, carry):
+        step(i)
+        return carry
+
+    lax.fori_loop(0, count, one, 0)
+
+
+def clear(total):
+    def one(i):
+        total[i // E, block(i % E), :] = jnp.zeros((TOK, total.shape[2]), F32)
+
+    loop(total.shape[0] * E, one)
+
+
+def column(values, index):
+    lane = lax.broadcasted_iota(jnp.int32, values.shape, 1)
+    return jnp.sum(jnp.where(lane == index, values, 0.0), axis=-1, keepdims=True)
+
+
 def place(store, parts, sub, first=0):
     for j, part in enumerate(parts):
         rows = part.shape[1]
         start = pl.multiple_of((sub ^ j) * rows, rows)
-        for a in range(part.shape[0]):
+
+        def one(a, part=part, start=start, rows=rows):
             store[first + a, pl.ds(start, rows), :] = part[a]
+
+        loop(part.shape[0], one)
 
 
 def block(index):
@@ -74,8 +97,11 @@
 
 def send_blocks(total, outs, order):
     for k in range(E):
-        for a in range(total.shape[0]):
+
+        def one(a, k=k):
             outs[k][a] = total[a, block(order ^ k), :].astype(outs[k].dtype)
+
+        loop(total.shape[0], one)
 
 
 def stat_rows(square, logits):
@@ -101,8 +127,11 @@
                 scaled, router[...], NT, precision=lax.Precision.HIGHEST, preferred_element_type=F32
             )
             stats[q] = stat_rows(jnp.sum(wide * wide, axis=-1, keepdims=True), logits)
-        for a in range(2):
+
+        def project(a):
             total[a] = mul(gained[...], weights[a], NN)
+
+        loop(2, project)
         own_stats[...] = stats[at[0]]
         for k in range(E):
             where = block(at[0] ^ k)
@@ -143,11 +172,14 @@
                 wide[q * TOK : (q + 1) * TOK, :] = rows[q][...]
         outs, weights, total = rest[:E], rest[E], rest[E + 1]
         place(weights, parts, at[1])
-        for e in range(E):
+        clear(total)
+
+        def project(e):
             every = mul(wide[...], weights[e], NN)
             for i in range(TOPK):
-                mine = every * hot[:, i * E + e : i * E + e + 1]
-                total[i] = mine if e == 0 else total[i] + mine
+                total[i] = total[i] + every * column(hot[...], i * E + e)
+
+        loop(E, project)
         send_blocks(total, outs, at[0])
 
     return body
@@ -156,12 +188,14 @@
 def spread_pairs(at, rows, hot, out, first=0):
     for k in range(E):
         where = block(at[0] ^ k)
-        mask = hot[where, :].astype(BF16)
-        for e in range(E):
-            out[e, where, :] = (
-                rows[k][first] * mask[:, e : e + 1]
-                + rows[k][first + 1] * mask[:, E + e : E + e + 1]
-            )
+        mask = hot[where, :]
+
+        def one(e, k=k, where=where, mask=mask):
+            out[e, where, :] = rows[k][first] * column(mask, e).astype(BF16) + rows[k][
+                first + 1
+            ] * column(mask, E + e).astype(BF16)
+
+        loop(E, one)
 
 
 def fold_out(total, keep_0, keep_2, send):
@@ -174,13 +208,16 @@
 def output_body(subs):
     def body(at, *refs):
         rows, hot, parts = refs[:E], refs[E], refs[E + 1 : E + 1 + subs]
-        mixed, keep_0, keep_2, send, weights = refs[E + 1 + subs :]
+        mixed, keep_0, keep_2, send, weights, total = refs[E + 1 + subs :]
         place(weights, parts, at[1])
         spread_pairs(at, rows, hot, mixed)
-        total = mul(mixed[0], weights[0], NT)
-        for e in range(1, E):
-            total = total + mul(mixed[e], weights[e], NT)
-        fold_out(total, keep_0, keep_2, send)
+        clear(total)
+
+        def project(e):
+            total[0] = total[0] + mul(mixed[e], weights[e], NT)
+
+        loop(E, project)
+        fold_out(total[0], keep_0, keep_2, send)
 
     return body
 
@@ -191,15 +228,23 @@
         kv_parts = refs[E + 1 : E + 1 + subs]
         query_parts = refs[E + 1 + subs : E + 1 + 2 * subs]
         streams = refs[E + 1 + 2 * subs : 2 * E + 1 + 2 * subs]
-        dkv_all, gain_row, keep_0, keep_2, send, weights = refs[2 * E + 1 + 2 * subs :]
+        dkv_all, gain_row, keep_0, keep_2, send, weights, store = refs[2 * E + 1 + 2 * subs :]
         place(weights, kv_parts, at[1])
         place(weights, query_parts, at[1], 2)
         for k in range(E):
             for a in range(2):
                 dkv_all[a, block(at[0] ^ k), :] = rows[k][a]
-        total = mul(dkv_all[0], weights[0], NT) + mul(dkv_all[1], weights[1], NT)
-        for e in range(E):
-            total = total + mul(dmixed[e], weights[2 + e], NT)
+        clear(store)
+
+        def project_kv(a):
+            store[0] = store[0] + mul(dkv_all[a], weights[a], NT)
+
+        def project(e):
+            store[0] = store[0] + mul(dmixed[e], weights[2 + e], NT)
+
+        loop(2, project_kv)
+        loop(E, project)
+        total = store[0]
         gain = jnp.zeros((1, total.shape[1]), F32)
         for q in range(E):
             part = total[q * TOK : (q + 1) * TOK] * streams[q][...].astype(F32)
@@ -211,12 +256,14 @@
 
 
 def split_rows(at, rows, other, parts, total):
-    for a in range(other.shape[0]):
+    def one(a):
         total[...] = mul(rows[...], other[a], TN)
         for j, part in enumerate(parts):
             count = part.shape[1]
             start = pl.multiple_of((at[1] ^ j) * count, count)
             part[a] = total[pl.ds(start, count), :].astype(part.dtype)
+
+    loop(other.shape[0], one)
 
 
 def weight_grad_body(at, rows, other, *refs):
@@ -272,8 +319,9 @@
         low[a] = (total * scale).astype(BF16)
         low[2 + a] = (query * scale).astype(BF16)
     allowed = attention_mask(at)
-    for h in range(low.shape[2] // HS):
-        head = slice(h * HS, (h + 1) * HS)
+
+    def attend(h):
+        head = pl.ds(pl.multiple_of(h * HS, HS), HS)
         for i in range(TOPK):
             scores = mul(low[2 + i, :, head], low[0, :, head], NT) * HS ** (-0.5)
             scores = jnp.where(allowed, scores, NEGATIVE)
@@ -284,29 +332,31 @@
             context[i, :, head] = mixed
             gated[i, :, head] = (mixed.astype(F32) * cols[:, 1 + i : 2 + i]).astype(BF16)
 
+    loop(low.shape[2] // HS, attend)
+
 
 def attention_back_body(at, own, *refs):
     got = refs[: E - 1]
-    rows, low, probs, context, grads, sums = refs[E - 1 :]
+    rows, low, probs, context, grads, sums, dcontext, inner = refs[E - 1 :]
     cols = columns(rows[...])
     scale = cols[:, 0:1]
-    inner = jnp.zeros((TOK, 1), F32)
+    inner[...] = jnp.zeros((TOK, HS), F32)
     dprob = []
-    dcontext = []
     for i in range(TOPK):
         raw = own[i]
         for one in got:
             raw = raw + one[i].astype(F32)
         dprob.append(jnp.sum(context[i].astype(F32) * raw, axis=-1, keepdims=True))
-        dcontext.append((raw * cols[:, 1 + i : 2 + i]).astype(BF16))
-    for h in range(low.shape[2] // HS):
-        head = slice(h * HS, (h + 1) * HS)
+        dcontext[i] = (raw * cols[:, 1 + i : 2 + i]).astype(BF16)
+
+    def attend(h):
+        head = pl.ds(pl.multiple_of(h * HS, HS), HS)
         key, value = low[0, :, head], low[1, :, head]
         dkey = jnp.zeros((TOK, HS), F32)
         dvalue = jnp.zeros((TOK, HS), F32)
         for i in range(TOPK):
             query = low[2 + i, :, head]
-            grad = dcontext[i][:, head]
+            grad = dcontext[i, :, head]
             prob = probs[h, i * TOK : (i + 1) * TOK, :]
             dweight = mul(grad, value, NT)
             dscore = prob * (dweight - jnp.sum(prob * dweight, axis=-1, keepdims=True))
@@ -314,17 +364,45 @@
             done = mul(dscore, key, NN) * HS ** (-0.5)
             dkey = dkey + mul(dscore, query, TN)
             dvalue = dvalue + mul(prob.astype(BF16), grad, TN)
-            inner = inner + jnp.sum(done * query.astype(F32), axis=-1, keepdims=True)
+            inner[...] = inner[...] + done * query.astype(F32)
             grads[2 + i, :, head] = (done * scale).astype(BF16)
         dkey = dkey * HS ** (-0.5)
-        inner = inner + jnp.sum(
-            dkey * key.astype(F32) + dvalue * value.astype(F32), axis=-1, keepdims=True
-        )
+        inner[...] = inner[...] + dkey * key.astype(F32) + dvalue * value.astype(F32)
         grads[0, :, head] = (dkey * scale).astype(BF16)
         grads[1, :, head] = (dvalue * scale).astype(BF16)
+
+    loop(low.shape[2] // HS, attend)
+    total = jnp.sum(inner[...], axis=-1, keepdims=True)
     lane = lax.broadcasted_iota(jnp.int32, (TOK, TOK), 1)
-    table = jnp.where(lane == 0, dprob[0], jnp.where(lane == 1, dprob[1], jnp.where(lane == 2, inner, 0.0)))
+    table = jnp.where(lane == 0, dprob[0], jnp.where(lane == 1, dprob[1], jnp.where(lane == 2, total, 0.0)))
     sums[...] = jnp.transpose(table)[0:8]
+
+
+def expert_grad_body(at, dgate, dup, weights, stats, own, send):
+    half, size = own.shape[0], weights.shape[2]
+
+    def one(n):
+        where = pl.ds(pl.multiple_of(n * 256, 256), 256)
+        total = mul(dgate[...], weights[0, :, where], NN) + mul(dup[...], weights[1, :, where], NN)
+        own[:, where] = total[:half]
+        send[:, where] = total[half:].astype(BF16)
+
+    loop(size // 256, one)
+    own[:, size:] = stats[:half, :]
+    send[:, size:] = stats[half:, :].astype(BF16)
+
+
+def expert_out_body(at, rows, weights, pairs, own, send):
+    half, size = own.shape[0], weights.shape[1]
+    gate = pairs[:, 2:3].astype(F32) + pairs[:, 3:4].astype(F32)
+
+    def one(n):
+        where = pl.ds(pl.multiple_of(n * 256, 256), 256)
+        total = mul(rows[...], weights[:, where], NN) * gate
+        own[:, where] = total[:half]
+        send[:, where] = total[half:].astype(BF16)
+
+    loop(size // 256, one)
 
 
 def columns(rows):
@@ -716,7 +794,10 @@
         output_body(subs),
         [shape((E, rows_all, local_width), BF16)] + folded,
         [at, *gather_planes(gated), hot_cols, *out_parts],
-        [pltpu.VMEM((E, slice_width, local_width), BF16)],
+        [
+            pltpu.VMEM((E, slice_width, local_width), BF16),
+            pltpu.VMEM((1, rows_all, slice_width), F32),
+        ],
     )
     weight_in = expert_in[0]
     weight_down = expert_down[0]
@@ -765,17 +846,13 @@
     dup_pre = (dactiv * silu_gate).astype(BF16)
     dprob_rows = jnp.sum(activation.astype(F32) * dact_raw, axis=-1)
     inner_rows = jnp.sum(dgate_pre.astype(F32) * gate_pre + dup_pre.astype(F32) * up_pre, axis=-1)
-    drows = jnp.einsum(
-        "krf,dkf->rd", jnp.stack([dgate_pre, dup_pre]), weight_in, preferred_element_type=F32
-    )
     lanes = jnp.arange(128)
     row_stats = jnp.where(
         lanes[None, :] == 0, dprob_rows[:, None], jnp.where(lanes[None, :] == 1, inner_rows[:, None], 0.0)
     )
 
-    def give_back(rows):
-        half = rows.shape[0] // 2
-        rows = rows[:half] + by_narrow(rows[half:].astype(BF16), 1).astype(F32)
+    def give_back(own, send):
+        rows = own + by_narrow(send, 1).astype(F32)
         bit = subs // 2
         while bit > 1:
             half = rows.shape[0] // 2
@@ -797,7 +874,14 @@
         )
         return jnp.stack(exchange_planes(pieces))
 
-    returned = give_back(jnp.concatenate([drows, row_stats], axis=1))
+    half = expert_rows.shape[0] // 2
+    returned = run(
+        "expert_grad",
+        expert_grad_body,
+        [shape((half, width + 128), F32), shape((half, width + 128), BF16)],
+        [at, dgate_pre, dup_pre, jnp.transpose(weight_in, (1, 2, 0)), row_stats],
+    )
+    returned = give_back(*returned)
     returned = from_planes(*returned, row_stats.shape[1])
     combined = jnp.einsum("kst,ksd->ktd", select, returned, preferred_element_type=F32)
     per_expert = combined[:, :, slice_width : slice_width + 2]
@@ -848,8 +932,13 @@
     output_parts = run(
         "output_grad", weight_grad_body, weight_parts(E), [at, wide_grad, mixed], weight_scratch
     )
-    expert_out = dot(activation, weight_down, ((1,), (0,))) * row_gate
-    mixture = give_back(expert_out)
+    expert_out = run(
+        "expert_out",
+        expert_out_body,
+        [shape((half, width), F32), shape((half, width), BF16)],
+        [at, activation, weight_down, full[:, width:]],
+    )
+    mixture = give_back(*expert_out)
     output_grad, output_got = weight_sum(output_parts)
     gated_act = (activation.astype(F32) * row_gate).astype(BF16)
     down_grad = dot(after(gated_act, dcontext_blocks[0]), grad_rows, ((0,), (0,)))
@@ -865,6 +954,7 @@
             probs,
             context,
         ],
+        [pltpu.VMEM((TOPK, TOK, local_width), BF16), pltpu.VMEM((TOK, HS), F32)],
     )
     grad_planes = gather_planes(grads_low)
     dboth = jnp.stack(
@@ -897,7 +987,10 @@
             *query_parts,
             *all_streams,
         ],
-        [pltpu.VMEM((2 + E, slice_width, local_width), BF16)],
+        [
+            pltpu.VMEM((2 + E, slice_width, local_width), BF16),
+            pltpu.VMEM((1, rows_all, slice_width), F32),
+        ],
     )
     home_rows = swap(after(near, own_stats))
     gain_one_home = home_rows[0].astype(F32)

time: 425 us -> 434 us (1.021)
  Pallas kernels: 61.8 us -> 91.8 us
  matrix products: 47.1 us -> 25.9 us
  local copies, waits for them, and re-layouts: 14.4 us -> 20.3 us
    pallas_call x16 -> x18, Pallas kernels: 61.8 us -> 91.8 us  [run(): pl.pallas_call(body, out_shape=tuple(outs), in_specs=[pl.BlockSpec(memory...]
    dot_general x1 -> x0, matrix products: 14.5 us -> none  [local(): jnp.einsum('krf,dkf->rd', jnp.stack([dgate_pre, dup_pre]), weight_in, pre...]
    dot_general x7 -> x6, matrix products: 17.9 us -> 11.8 us  [dot(): lax.dot_general(left, right, ((contract[0], contract[1]), ((), ())), prec...]
    unnamed x128 -> x156, local copies, waits for them, and re-layouts: 7.13 us -> 11.6 us
  transfers between devices with their start and end apart: 69 -> 69, of which waited for: 35 -> 35; matrix products, arithmetic and copies ran while one was open for 14% -> 11% of each run, Pallas kernels for 13% -> 17%
where the time goes in v4:
time: 434 us; the launch traced here: 433 us
  waiting for transfers between devices  169 us (39%)
  starting transfers between devices  93.7 us (22%)
  Pallas kernels  91.8 us (21%)
  other arithmetic  31.1 us (7%)
  matrix products  25.9 us (6%)
  local copies, waits for them, and re-layouts  20.3 us (5%)
    ppermute x29, waiting for transfers between devices, by_plane(): lax.ppermute(values, 'wide', [(i, i ^ k * subs) for i in range(wide_count)])  93.9 us
    pallas_call x18, Pallas kernels, run(): pl.pallas_call(body, out_shape=tuple(outs), in_specs=[pl.BlockSpec(memory...  91.8 us
    ppermute x29, starting transfers between devices, by_plane(): lax.ppermute(values, 'wide', [(i, i ^ k * subs) for i in range(wide_count)])  52.1 us
    ppermute x18, waiting for transfers between devices, by_narrow(): lax.ppermute(values, 'narrow', [(i, i ^ k) for i in range(narrow_count)])  27.1 us
    ppermute x8, waiting for transfers between devices, by_side(): return lax.ppermute(values, ('wide', 'narrow'), pairs)  26 us
    ppermute x6, starting transfers between devices, swap(): return lax.ppermute(values, ('wide', 'narrow'), pairs)  20.8 us
    dot_general x6, matrix products, dot(): lax.dot_general(left, right, ((contract[0], contract[1]), ((), ())), prec...  11.8 us
    unnamed x156, local copies, waits for them, and re-layouts  11.6 us
  transfers between devices with their start and end apart: 69, of which 35 were waited for; matrix products, arithmetic and copies ran while one was open for 11% of the time, Pallas kernels for 17%

profile of v4, /device:TPU:2, one launch (start us, length us, event | category | flops | bytes accessed | tf_op | source)
XLA Modules:
  0.0 432.9 jit_solution(2681940638113212344)
XLA Ops:
  36.6 8.1 %collective-permute-done.6.refs_1_.refs_0_ = bf16[272,512]{1,0:T(8,128)(2,1)S(1)} collective-permute-done((bf16[272,512]{1,0:T(8,128)(2,1)}, bf16[272,512]{1,0:T(8,128)(2,1)S(1)}, u32[]{:S(2)}, u32[]{:S(2)}) %collective-permute-start.6) | collective-permute-done | bytes 278560 | tf_op jit(solution)/shard_map/ppermute | solution.py:597
  44.7 8.5 %collective-permute-done.7.refs_2_.refs_1_ = bf16[272,512]{1,0:T(8,128)(2,1)S(1)} collective-permute-done((bf16[272,512]{1,0:T(8,128)(2,1)}, bf16[272,512]{1,0:T(8,128)(2,1)S(1)}, u32[]{:S(2)}, u32[]{:S(2)}) %collective-permute-start.7) | collective-permute-done | bytes 278560 | tf_op jit(solution)/shard_map/ppermute | solution.py:597
  58.4 5.3 %query.1 = (f32[2,128,512]{2,1,0:T(8,128)}, bf16[2,128,512]{2,1,0:T(8,128)(2,1)}, bf16[2,128,512]{2,1,0:T(8,128)(2,1)}, bf16[2,128,512]{2,1,0:T(8,128)(2,1)}) custom-call(s32[4]{0:T(128)} %pad_add_fusion.at, bf16[512,512]{1,0:T(8,128)(2,1)} %get-tuple-element.112.refs_0_.rows, f32[512,8]{1,0:T(8,128)} %get-tuple-element.113.refs_1_.refs_4_.hot, ...), custom_call_target="tpu_custom_call" | custom-call | flops 1 | bytes 1 | tf_op jit(solution)/shard_map/query/pallas_call | solution.py:52
  63.7 6.9 %collective-permute-start.10 = (bf16[2,128,512]{2,1,0:T(8,128)(2,1)}, bf16[2,128,512]{2,1,0:T(8,128)(2,1)S(1)}, u32[]{:S(2)}, u32[]{:S(2)}) collective-permute-start(bf16[2,128,512]{2,1,0:T(8,128)(2,1)} %get-tuple-element.116), channel_id=1, source_target_pairs={{0,8},{4,12},{8,0},{12,4},{16,24},{20,28},{24,16},{28,20},{1,9},{5... | collective-permute-start | bytes 786440 | tf_op jit(solution)/shard_map/ppermute | solution.py:597
  81.8 13.8 %collective-permute-done.11.refs_5_ = bf16[2,128,512]{2,1,0:T(8,128)(2,1)S(1)} collective-permute-done((bf16[2,128,512]{2,1,0:T(8,128)(2,1)}, bf16[2,128,512]{2,1,0:T(8,128)(2,1)S(1)}, u32[]{:S(2)}, u32[]{:S(2)}) %collective-permute-start.11) | collective-permute-done | bytes 262176 | tf_op jit(solution)/shard_map/ppermute | solution.py:597
  96.4 6.2 %attention.1 = (f32[16,128]{1,0:T(8,128)}, bf16[4,128,512]{2,1,0:T(8,128)(2,1)}, f32[4,256,128]{2,1,0:T(8,128)}, bf16[2,128,512]{2,1,0:T(8,128)(2,1)}, bf16[2,128,512]{2,1,0:T(8,128)(2,1)}) custom-call(s32[4]{0:T(128)} %bitcast.188, f32[2,128,512]{2,1,0:T(8,128)} %get-tuple-element.108.own_kv, bf16[272,512]{1,0:T(8,128)(2,1)} %copy-done.28, ...), custom_call_target="tpu_custom_call" | custom-call | flops 1 | bytes 1 | tf_op jit(solution)/shard_map/attention/pallas_call | solution.py:52
  117.3 14.0 %collective-permute-done.14.refs_2_ = bf16[2,128,512]{2,1,0:T(8,128)(2,1)S(1)} collective-permute-done((bf16[2,128,512]{2,1,0:T(8,128)(2,1)}, bf16[2,128,512]{2,1,0:T(8,128)(2,1)S(1)}, u32[]{:S(2)}, u32[]{:S(2)}) %collective-permute-start.14) | collective-permute-done | bytes 262176 | tf_op jit(solution)/shard_map/ppermute | solution.py:597
  133.8 7.1 %output.1 = (bf16[4,512,512]{2,1,0:T(8,128)(2,1)}, f32[128,512]{1,0:T(8,128)}, f32[128,512]{1,0:T(8,128)}, bf16[2,128,512]{2,1,0:T(8,128)(2,1)}) custom-call(s32[4]{0:T(128)} %pad_add_fusion.at, bf16[2,128,512]{2,1,0:T(8,128)(2,1)} %get-tuple-element.121.refs_0_, bf16[2,128,512]{2,1,0:T(8,128)(2,1)} %copy-done.47, bf16[2,128,512]{2,1,0:T(8,128)(2,1)} %copy-done.46, ...), custom_call_target="tpu_custom_call" | custom-call | flops 1 | bytes 1 | tf_op jit(solution)/shard_map/output/pallas_call | solution.py:52
  158.6 5.4 %collective-permute-done.26.refs_2_ = bf16[80,640]{1,0:T(8,128)(2,1)S(1)} collective-permute-done((bf16[80,640]{1,0:T(8,128)(2,1)}, bf16[80,640]{1,0:T(8,128)(2,1)S(1)}, u32[]{:S(2)}, u32[]{:S(2)}) %collective-permute-start.26) | collective-permute-done | bytes 102432 | tf_op jit(solution)/shard_map/ppermute | solution.py:597
  168.2 7.4 %collective-permute-done.28 = bf16[80,2176]{1,0:T(8,128)(2,1)S(1)} collective-permute-done((bf16[80,2176]{1,0:T(8,128)(2,1)}, bf16[80,2176]{1,0:T(8,128)(2,1)S(1)}, u32[]{:S(2)}, u32[]{:S(2)}) %collective-permute-start.28) | collective-permute-done | bytes 348192 | tf_op jit(solution)/shard_map/ppermute | solution.py:619
  178.1 9.6 %collective-permute-done.29 = bf16[160,2176]{1,0:T(8,128)(2,1)S(1)} collective-permute-done((bf16[160,2176]{1,0:T(8,128)(2,1)S(1)}, bf16[160,2176]{1,0:T(8,128)(2,1)S(1)}, u32[]{:S(2)}, u32[]{:S(2)}) %collective-permute-start.29) | collective-permute-done | bytes 696352 | tf_op jit(solution)/shard_map/ppermute | solution.py:619
  209.2 10.7 %expert_grad.1 = (f32[320,2176]{1,0:T(8,128)}, bf16[320,2176]{1,0:T(8,128)(2,1)}) custom-call(s32[4]{0:T(128)} %pad_add_fusion.at, bf16[640,704]{1,0:T(8,128)(2,1)} %copy-done.2, bf16[640,704]{1,0:T(8,128)(2,1)} %copy-done.1, bf16[2,704,2048]{2,1,0:T(8,128)(2,1)} %bitcast.152, f32[640,128]{1,0:T(8,128)} %select_select_fusion.stats), custom_call_target="tpu_custom_call" | custom-call | flops 1 | bytes 1 | tf_op jit(solution)/shard_map/expert_grad/pallas_call | solution.py:52
  255.8 7.6 %expert_out.1 = (f32[320,2048]{1,0:T(8,128)}, bf16[320,2048]{1,0:T(8,128)(2,1)}) custom-call(s32[4]{0:T(128)} %pad_add_fusion.at, bf16[640,704]{1,0:T(8,128)(2,1)} %copy-done, bf16[704,2048]{1,0:T(8,128)(2,1)} %bitcast.155, bf16[640,128]{1,0:T(8,128)(2,1)} %slice.187.pairs), custom_call_target="tpu_custom_call" | custom-call | flops 1 | bytes 1 | tf_op jit(solution)/shard_map/expert_out/pallas_call | solution.py:52
  273.4 5.5 %dcontext.1 = (bf16[512,512]{1,0:T(8,128)(2,1)}, f32[2,128,512]{2,1,0:T(8,128)}, bf16[2,128,512]{2,1,0:T(8,128)(2,1)}, bf16[2,128,512]{2,1,0:T(8,128)(2,1)}, bf16[2,128,512]{2,1,0:T(8,128)(2,1)}) custom-call(s32[4]{0:T(128)} %pad_add_fusion.at, bf16[128,512]{1,0:T(8,128)(2,1)} %copy-done.39, bf16[128,512]{1,0:T(8,128)(2,1)} %copy-done.51, ...), custom_call_target="tpu_custom_call" | custom-call | flops 1 | bytes 1 | tf_op jit(solution)/shard_map/dcontext/pallas_call | solution.py:52
  283.4 5.5 %output_grad.1 = (f32[4,256,512]{2,1,0:T(8,128)}, bf16[4,256,512]{2,1,0:T(8,128)(2,1)}) custom-call(s32[4]{0:T(128)} %pad_add_fusion.at, bf16[512,512]{1,0:T(8,128)(2,1)} %get-tuple-element.157.rows, bf16[4,512,512]{2,1,0:T(8,128)(2,1)} %get-tuple-element.158.other), custom_call_target="tpu_custom_call" | custom-call | flops 1 | bytes 1 | tf_op jit(solution)/shard_map/output_grad/pallas_call | solution.py:52
  290.3 6.8 %fusion.25 = f32[704,2048]{1,0:T(8,128)} fusion(bf16[640,704]{1,0:T(8,128)(2,1)} %get-tuple-element.160, bf16[320,2048]{1,0:T(8,128)(2,1)} %copy-done.73, bf16[160,2048]{1,0:T(8,128)(2,1)} %copy-done.33, bf16[80,2048]{1,0:T(8,128)(2,1)} %copy-done.24, bf16[80,2048]{1,0:T(8,128)(2,1)S(1)} %copy-done.14), kind=kOutput, calls=%fused_computation.56 | convolution fusion | flops 1855979520 | bytes 9289728 | tf_op jit(solution)/shard_map/dot_general | solution.py:22
  300.7 5.5 %attention_back.1 = (bf16[4,128,512]{2,1,0:T(8,128)(2,1)}, f32[8,128]{1,0:T(8,128)}) custom-call(s32[4]{0:T(128)} %pad_add_fusion.at, f32[2,128,512]{2,1,0:T(8,128)} %get-tuple-element.161.own, bf16[2,128,512]{2,1,0:T(8,128)(2,1)} %collective-permute-done.45.refs_0_, bf16[2,128,512]{2,1,0:T(8,128)(2,1)} %collective-permute-done.46.refs_1_, ...), custom_call_target="tpu_custom_call" | custom-call | flops 1 | bytes 1 | tf_op jit(solution)/shard_map/attention_back/pallas_call | solution.py:52
  312.1 5.7 %collective-permute-start.49 = (bf16[4,128,512]{2,1,0:T(8,128)(2,1)S(1)}, bf16[4,128,512]{2,1,0:T(8,128)(2,1)S(1)}, u32[]{:S(2)}, u32[]{:S(2)}) collective-permute-start(bf16[4,128,512]{2,1,0:T(8,128)(2,1)S(1)} %copy-done.19), channel_id=1, source_target_pairs={{0,16},{4,20},{8,24},{12,28},{16,0},{20,4},{24,8},{28,12},{1,17},{... | collective-permute-start | bytes 1572872 | tf_op jit(solution)/shard_map/ppermute | solution.py:597
  317.8 5.4 %collective-permute-done.50.refs_3_ = bf16[4,128,512]{2,1,0:T(8,128)(2,1)} collective-permute-done((bf16[4,128,512]{2,1,0:T(8,128)(2,1)}, bf16[4,128,512]{2,1,0:T(8,128)(2,1)}, u32[]{:S(2)}, u32[]{:S(2)}) %collective-permute-start.50) | collective-permute-done | bytes 524320 | tf_op jit(solution)/shard_map/ppermute | solution.py:597
  323.2 9.0 %fusion.2 = f32[2048,2,704]{0,2,1:T(8,128)} fusion(bf16[640,2,704]{2,0,1:T(8,128)(2,1)} %pad_maximum_fusion.2, bf16[640,2176]{1,0:T(8,128)(2,1)S(1)} %copy-done.13), kind=kOutput, calls=%fused_computation.5 | convolution fusion | flops 3690987520 | bytes 15958016 | tf_op jit(solution)/shard_map/rd,rkf->dkf/dot_general | solution.py:967
  332.2 22.7 %collective-permute-done.49.refs_2_ = bf16[4,128,512]{2,1,0:T(8,128)(2,1)S(1)} collective-permute-done((bf16[4,128,512]{2,1,0:T(8,128)(2,1)S(1)}, bf16[4,128,512]{2,1,0:T(8,128)(2,1)S(1)}, u32[]{:S(2)}, u32[]{:S(2)}) %collective-permute-start.49) | collective-permute-done | bytes 524320 | tf_op jit(solution)/shard_map/ppermute | solution.py:597
  356.0 7.6 %query_grad.1 = (bf16[4,512,512]{2,1,0:T(8,128)(2,1)}, f32[4,256,512]{2,1,0:T(8,128)}, bf16[4,256,512]{2,1,0:T(8,128)(2,1)}) custom-call(s32[4]{0:T(128)} %pad_add_fusion.at, bf16[512,512]{1,0:T(8,128)(2,1)} %get-tuple-element.112.refs_0_.rows, f32[512,8]{1,0:T(8,128)} %get-tuple-element.113.refs_1_.refs_4_.hot, ...), custom_call_target="tpu_custom_call" | custom-call | flops 1 | bytes 1 | tf_op jit(solution)/shard_map/query_grad/pallas_call | solution.py:52
  363.6 7.5 %input.1 = (bf16[2,512,512]{2,1,0:T(8,128)(2,1)}, f32[1,512]{1,0:T(1,128)}, f32[128,512]{1,0:T(8,128)}, f32[128,512]{1,0:T(8,128)}, bf16[2,128,512]{2,1,0:T(8,128)(2,1)}) custom-call(s32[4]{0:T(128)} %pad_add_fusion.at, bf16[4,128,512]{2,1,0:T(8,128)(2,1)} %get-tuple-element.176.refs_0_, bf16[4,128,512]{2,1,0:T(8,128)(2,1)} %copy-done.21, ...), custom_call_target="tpu_custom_call" | custom-call | flops 1 | bytes 1 | tf_op jit(solution)/shard_map/input/pallas_call | solution.py:52
  415.5 5.7 %collective-permute-done.59 = bf16[128,512]{1,0:T(8,128)(2,1)S(1)} collective-permute-done((bf16[128,512]{1,0:T(8,128)(2,1)S(1)}, bf16[128,512]{1,0:T(8,128)(2,1)S(1)}, u32[]{:S(2)}, u32[]{:S(2)}) %collective-permute-start.59) | collective-permute-done | bytes 131104 | tf_op jit(solution)/shard_map/ppermute | solution.py:611
  (380 shorter events, 233.8 us)
Async XLA Ops:
  14.9 42.0 %collective-permute-start.9 = (bf16[4,256,512]{2,1,0:T(8,128)(2,1)}, bf16[4,256,512]{2,1,0:T(8,128)(2,1)S(1)}, u32[]{:S(2)}, u32[]{:S(2)}) collective-permute-start(bf16[4,256,512]{2,1,0:T(8,128)(2,1)} %refs_7_.3), channel_id=1, source_target_pairs={{0,4},{4,0},{8,12},{12,8},{16,20},{20,16},{24,28},{28,24},{1,5},{5... | collective-permute-start | bytes 3145736 | tf_op jit(solution)/shard_map/ppermute | solution.py:600
  30.6 22.6 %collective-permute-start.7 = (bf16[272,512]{1,0:T(8,128)(2,1)}, bf16[272,512]{1,0:T(8,128)(2,1)S(1)}, u32[]{:S(2)}, u32[]{:S(2)}) collective-permute-start(bf16[272,512]{1,0:T(8,128)(2,1)} %get-tuple-element.110), channel_id=1, source_target_pairs={{0,16},{4,20},{8,24},{12,28},{16,0},{20,4},{24,8},{28,12},{1,17},{... | collective-permute-start | bytes 835592 | tf_op jit(solution)/shard_map/ppermute | solution.py:597
  32.8 20.4 %collective-permute-start.8 = (bf16[272,512]{1,0:T(8,128)(2,1)}, bf16[272,512]{1,0:T(8,128)(2,1)S(1)}, u32[]{:S(2)}, u32[]{:S(2)}) collective-permute-start(bf16[272,512]{1,0:T(8,128)(2,1)} %get-tuple-element.111), channel_id=1, source_target_pairs={{0,24},{4,28},{8,16},{12,20},{16,8},{20,12},{24,0},{28,4},{1,25},{... | collective-permute-start | bytes 835592 | tf_op jit(solution)/shard_map/ppermute | solution.py:597
  34.5 37.8 %collective-permute-start.19 = (bf16[128,512]{1,0:T(8,128)(2,1)}, bf16[128,512]{1,0:T(8,128)(2,1)S(1)}, u32[]{:S(2)}, u32[]{:S(2)}) collective-permute-start(bf16[128,512]{1,0:T(8,128)(2,1)} %param.15), channel_id=1, source_target_pairs={{0,0},{1,8},{2,16},{3,24},{4,4},{5,12},{6,20},{7,28},{8,1},{9,9},{... | collective-permute-start | bytes 393224 | tf_op jit(solution)/shard_map/ppermute | solution.py:611
  56.9 75.9 %collective-permute-start.16 = (bf16[4,256,512]{2,1,0:T(8,128)(2,1)S(1)}, bf16[4,256,512]{2,1,0:T(8,128)(2,1)S(1)}, u32[]{:S(2)}, u32[]{:S(2)}) collective-permute-start(bf16[4,256,512]{2,1,0:T(8,128)(2,1)S(1)} %copy-done.5), channel_id=1, source_target_pairs={{0,4},{4,0},{8,12},{12,8},{16,20},{20,16},{24,28},{28,24},{1,5},{5... | collective-permute-start | bytes 3145736 | tf_op jit(solution)/shard_map/ppermute | solution.py:600
  70.6 25.0 %collective-permute-start.11 = (bf16[2,128,512]{2,1,0:T(8,128)(2,1)}, bf16[2,128,512]{2,1,0:T(8,128)(2,1)S(1)}, u32[]{:S(2)}, u32[]{:S(2)}) collective-permute-start(bf16[2,128,512]{2,1,0:T(8,128)(2,1)} %get-tuple-element.117), channel_id=1, source_target_pairs={{0,16},{4,20},{8,24},{12,28},{16,0},{20,4},{24,8},{28,12},{1,17},{... | collective-permute-start | bytes 786440 | tf_op jit(solution)/shard_map/ppermute | solution.py:597
  72.6 23.0 %collective-permute-start.12 = (bf16[2,128,512]{2,1,0:T(8,128)(2,1)}, bf16[2,128,512]{2,1,0:T(8,128)(2,1)S(1)}, u32[]{:S(2)}, u32[]{:S(2)}) collective-permute-start(bf16[2,128,512]{2,1,0:T(8,128)(2,1)} %get-tuple-element.118), channel_id=1, source_target_pairs={{0,24},{4,28},{8,16},{12,20},{16,8},{20,12},{24,0},{28,4},{1,25},{... | collective-permute-start | bytes 786440 | tf_op jit(solution)/shard_map/ppermute | solution.py:597
  74.8 27.8 %collective-permute-start.22 = (bf16[80,512]{1,0:T(8,128)(2,1)S(1)}, bf16[80,512]{1,0:T(8,128)(2,1)S(1)}, u32[]{:S(2)}, u32[]{:S(2)}) collective-permute-start(bf16[80,512]{1,0:T(8,128)(2,1)S(1)} %get-tuple-element.221), channel_id=1, source_target_pairs={{0,24},{4,28},{8,16},{12,20},{16,8},{20,12},{24,0},{28,4},{1,25},{... | collective-permute-start | bytes 245768 | tf_op jit(solution)/shard_map/ppermute | solution.py:597
  80.0 22.6 %collective-permute-start.21 = (bf16[80,512]{1,0:T(8,128)(2,1)S(1)}, bf16[80,512]{1,0:T(8,128)(2,1)S(1)}, u32[]{:S(2)}, u32[]{:S(2)}) collective-permute-start(bf16[80,512]{1,0:T(8,128)(2,1)S(1)} %get-tuple-element.222), channel_id=1, source_target_pairs={{0,16},{4,20},{8,24},{12,28},{16,0},{20,4},{24,8},{28,12},{1,17},{... | collective-permute-start | bytes 245768 | tf_op jit(solution)/shard_map/ppermute | solution.py:597
  108.6 22.7 %collective-permute-start.14 = (bf16[2,128,512]{2,1,0:T(8,128)(2,1)}, bf16[2,128,512]{2,1,0:T(8,128)(2,1)S(1)}, u32[]{:S(2)}, u32[]{:S(2)}) collective-permute-start(bf16[2,128,512]{2,1,0:T(8,128)(2,1)} %get-tuple-element.121.refs_0_), channel_id=1, source_target_pairs={{0,16},{4,20},{8,24},{12,28},{16,0},{20,4},{24,8},{28,12},{1,17},{... | collective-permute-start | bytes 786440 | tf_op jit(solution)/shard_map/ppermute | solution.py:597
  112.9 18.5 %collective-permute-start.13 = (bf16[2,128,512]{2,1,0:T(8,128)(2,1)}, bf16[2,128,512]{2,1,0:T(8,128)(2,1)S(1)}, u32[]{:S(2)}, u32[]{:S(2)}) collective-permute-start(bf16[2,128,512]{2,1,0:T(8,128)(2,1)} %get-tuple-element.121.refs_0_), channel_id=1, source_target_pairs={{0,8},{4,12},{8,0},{12,4},{16,24},{20,28},{24,16},{28,20},{1,9},{5... | collective-permute-start | bytes 786440 | tf_op jit(solution)/shard_map/ppermute | solution.py:597
  115.4 29.2 %collective-permute-start.24 = (bf16[160,2048]{1,0:T(8,128)(2,1)}, bf16[160,2048]{1,0:T(8,128)(2,1)S(1)}, u32[]{:S(2)}, u32[]{:S(2)}) collective-permute-start(bf16[160,2048]{1,0:T(8,128)(2,1)} %pad_maximum_fusion.6), channel_id=1, source_target_pairs={{0,2},{1,5},{2,0},{3,7},{4,6},{5,1},{6,4},{7,3},{8,10},{9,13},{10,... | collective-permute-start | bytes 1966088 | tf_op jit(solution)/shard_map/ppermute | solution.py:619
  178.1 18.0 %collective-permute-start.35 = (bf16[320,2048]{1,0:T(8,128)(2,1)S(1)}, bf16[320,2048]{1,0:T(8,128)(2,1)S(1)}, u32[]{:S(2)}, u32[]{:S(2)}) collective-permute-start(bf16[320,2048]{1,0:T(8,128)(2,1)S(1)} %pad_maximum_fusion.4), channel_id=1, source_target_pairs={{0,1},{1,0},{2,3},{3,2},{4,5},{5,4},{6,7},{7,6},{8,9},{9,8},{10,11... | collective-permute-start | bytes 3932168 | tf_op jit(solution)/shard_map/ppermute | solution.py:603
  268.0 39.7 %collective-permute-start.34 = (bf16[160,2048]{1,0:T(8,128)(2,1)}, bf16[160,2048]{1,0:T(8,128)(2,1)}, u32[]{:S(2)}, u32[]{:S(2)}) collective-permute-start(bf16[160,2048]{1,0:T(8,128)(2,1)} %slice.369), channel_id=1, source_target_pairs={{0,2},{1,5},{2,0},{3,7},{4,6},{5,1},{6,4},{7,3},{8,10},{9,13},{10,... | collective-permute-start | bytes 1966088 | tf_op jit(solution)/shard_map/ppermute | solution.py:619
  279.0 18.1 %collective-permute-start.45 = (bf16[2,128,512]{2,1,0:T(8,128)(2,1)}, bf16[2,128,512]{2,1,0:T(8,128)(2,1)}, u32[]{:S(2)}, u32[]{:S(2)}) collective-permute-start(bf16[2,128,512]{2,1,0:T(8,128)(2,1)} %get-tuple-element.154), channel_id=1, source_target_pairs={{0,8},{4,12},{8,0},{12,4},{16,24},{20,28},{24,16},{28,20},{1,9},{5... | collective-permute-start | bytes 786440 | tf_op jit(solution)/shard_map/ppermute | solution.py:597
  279.0 21.7 %collective-permute-start.46 = (bf16[2,128,512]{2,1,0:T(8,128)(2,1)}, bf16[2,128,512]{2,1,0:T(8,128)(2,1)}, u32[]{:S(2)}, u32[]{:S(2)}) collective-permute-start(bf16[2,128,512]{2,1,0:T(8,128)(2,1)} %get-tuple-element.155), channel_id=1, source_target_pairs={{0,16},{4,20},{8,24},{12,28},{16,0},{20,4},{24,8},{28,12},{1,17},{... | collective-permute-start | bytes 786440 | tf_op jit(solution)/shard_map/ppermute | solution.py:597
  280.9 19.8 %collective-permute-start.47 = (bf16[2,128,512]{2,1,0:T(8,128)(2,1)}, bf16[2,128,512]{2,1,0:T(8,128)(2,1)}, u32[]{:S(2)}, u32[]{:S(2)}) collective-permute-start(bf16[2,128,512]{2,1,0:T(8,128)(2,1)} %get-tuple-element.156), channel_id=1, source_target_pairs={{0,24},{4,28},{8,16},{12,20},{16,8},{20,12},{24,0},{28,4},{1,25},{... | collective-permute-start | bytes 786440 | tf_op jit(solution)/shard_map/ppermute | solution.py:597
  288.9 66.0 %collective-permute-start.51 = (bf16[4,256,512]{2,1,0:T(8,128)(2,1)}, bf16[4,256,512]{2,1,0:T(8,128)(2,1)}, u32[]{:S(2)}, u32[]{:S(2)}) collective-permute-start(bf16[4,256,512]{2,1,0:T(8,128)(2,1)} %get-tuple-element.159), channel_id=1, source_target_pairs={{0,4},{4,0},{8,12},{12,8},{16,20},{20,16},{24,28},{28,24},{1,5},{5... | collective-permute-start | bytes 3145736 | tf_op jit(solution)/shard_map/ppermute | solution.py:600
  310.8 65.8 %collective-permute-start.52 = (bf16[80,2048]{1,0:T(8,128)(2,1)}, bf16[80,2048]{1,0:T(8,128)(2,1)}, u32[]{:S(2)}, u32[]{:S(2)}) collective-permute-start(bf16[80,2048]{1,0:T(8,128)(2,1)} %slice.371), channel_id=1, source_target_pairs={{0,4},{1,3},{2,6},{3,1},{4,0},{5,7},{6,2},{7,5},{8,12},{9,11},{10,... | collective-permute-start | bytes 983048 | tf_op jit(solution)/shard_map/ppermute | solution.py:619
  312.1 42.8 %collective-permute-start.49 = (bf16[4,128,512]{2,1,0:T(8,128)(2,1)S(1)}, bf16[4,128,512]{2,1,0:T(8,128)(2,1)S(1)}, u32[]{:S(2)}, u32[]{:S(2)}) collective-permute-start(bf16[4,128,512]{2,1,0:T(8,128)(2,1)S(1)} %copy-done.19), channel_id=1, source_target_pairs={{0,16},{4,20},{8,24},{12,28},{16,0},{20,4},{24,8},{28,12},{1,17},{... | collective-permute-start | bytes 1572872 | tf_op jit(solution)/shard_map/ppermute | solution.py:597
  317.8 37.1 %collective-permute-start.48 = (bf16[4,128,512]{2,1,0:T(8,128)(2,1)S(1)}, bf16[4,128,512]{2,1,0:T(8,128)(2,1)S(1)}, u32[]{:S(2)}, u32[]{:S(2)}) collective-permute-start(bf16[4,128,512]{2,1,0:T(8,128)(2,1)S(1)} %copy-done.19), channel_id=1, source_target_pairs={{0,8},{4,12},{8,0},{12,4},{16,24},{20,28},{24,16},{28,20},{1,9},{5... | collective-permute-start | bytes 1572872 | tf_op jit(solution)/shard_map/ppermute | solution.py:597
  375.2 27.4 %collective-permute-start.58 = (bf16[4,256,512]{2,1,0:T(8,128)(2,1)}, bf16[4,256,512]{2,1,0:T(8,128)(2,1)S(1)}, u32[]{:S(2)}, u32[]{:S(2)}) collective-permute-start(bf16[4,256,512]{2,1,0:T(8,128)(2,1)} %get-tuple-element.175), channel_id=1, source_target_pairs={{0,4},{4,0},{8,12},{12,8},{16,20},{20,16},{24,28},{28,24},{1,5},{5... | collective-permute-start | bytes 3145736 | tf_op jit(solution)/shard_map/ppermute | solution.py:600
  378.9 22.3 %collective-permute-start.53 = (bf16[80,512]{1,0:T(8,128)(2,1)}, bf16[80,512]{1,0:T(8,128)(2,1)S(1)}, u32[]{:S(2)}, u32[]{:S(2)}) collective-permute-start(bf16[80,512]{1,0:T(8,128)(2,1)} %get-tuple-element.184), channel_id=1, source_target_pairs={{0,8},{4,12},{8,0},{12,4},{16,24},{20,28},{24,16},{28,20},{1,9},{5... | collective-permute-start | bytes 245768 | tf_op jit(solution)/shard_map/ppermute | solution.py:597
  378.9 22.3 %collective-permute-start.54 = (bf16[80,512]{1,0:T(8,128)(2,1)}, bf16[80,512]{1,0:T(8,128)(2,1)S(1)}, u32[]{:S(2)}, u32[]{:S(2)}) collective-permute-start(bf16[80,512]{1,0:T(8,128)(2,1)} %get-tuple-element.185), channel_id=1, source_target_pairs={{0,16},{4,20},{8,24},{12,28},{16,0},{20,4},{24,8},{28,12},{1,17},{... | collective-permute-start | bytes 245768 | tf_op jit(solution)/shard_map/ppermute | solution.py:597
  (123 other events, 1308.0 us)

commit v5 on v3

--- a/solution.py
+++ b/solution.py
@@ -47,7 +47,7 @@
     return jax.ShapeDtypeStruct(tuple(dims), dtype)
 
 
-def run(name, body, outs, args, scratch=()):
+def run(name, body, outs, args, scratch=(), flops=1):
     vector = pl.BlockSpec(memory_space=pltpu.VMEM)
     return pl.pallas_call(
         body,
@@ -55,9 +55,22 @@
         in_specs=[pl.BlockSpec(memory_space=pltpu.SMEM)] + [vector] * (len(args) - 1),
         out_specs=tuple(vector for _ in outs),
         scratch_shapes=list(scratch),
-        cost_estimate=pl.CostEstimate(flops=1, transcendentals=0, bytes_accessed=1),
+        cost_estimate=pl.CostEstimate(flops=flops, transcendentals=0, bytes_accessed=1),
         name=name,
     )(*args)
+
+
+def loop(count, step):
+    def one(i, carry):
+        step(i)
+        return carry
+
+    lax.fori_loop(0, count, one, 0)
+
+
+def column(values, index):
+    lane = lax.broadcasted_iota(jnp.int32, values.shape, 1)
+    return jnp.sum(jnp.where(lane == index, values, 0.0), axis=-1, keepdims=True)
 
 
 def place(store, parts, sub, first=0):
@@ -74,8 +87,11 @@
 
 def send_blocks(total, outs, order):
     for k in range(E):
-        for a in range(total.shape[0]):
+
+        def one(a, k=k):
             outs[k][a] = total[a, block(order ^ k), :].astype(outs[k].dtype)
+
+        loop(total.shape[0], one)
 
 
 def stat_rows(square, logits):
@@ -142,12 +158,36 @@
             for q in range(E):
                 wide[q * TOK : (q + 1) * TOK, :] = rows[q][...]
         outs, weights, total = rest[:E], rest[E], rest[E + 1]
-        place(weights, parts, at[1])
-        for e in range(E):
+        if joined:
+            place(weights, parts, at[1])
+            for e in range(E):
+                every = mul(wide[...], weights[e], NN)
+                for i in range(TOPK):
+                    mine = every * hot[:, i * E + e : i * E + e + 1]
+                    total[i] = mine if e == 0 else total[i] + mine
+            send_blocks(total, outs, at[0])
+            return
+
+        for j, part in enumerate(parts):
+            size = part.shape[1]
+            start = pl.multiple_of((at[1] ^ j) * size, size)
+
+            def move(e, part=part, start=start, size=size):
+                weights[e, pl.ds(start, size), :] = part[e]
+
+            loop(E, move)
+
+        def empty(n):
+            total[n // E, block(n % E), :] = jnp.zeros((TOK, total.shape[2]), F32)
+
+        loop(TOPK * E, empty)
+
+        def project(e):
             every = mul(wide[...], weights[e], NN)
             for i in range(TOPK):
-                mine = every * hot[:, i * E + e : i * E + e + 1]
-                total[i] = mine if e == 0 else total[i] + mine
+                total[i] = total[i] + every * column(hot[...], i * E + e)
+
+        loop(E, project)
         send_blocks(total, outs, at[0])
 
     return body
@@ -210,23 +250,23 @@
     return body
 
 
-def split_rows(at, rows, other, parts, total):
-    for a in range(other.shape[0]):
-        total[...] = mul(rows[...], other[a], TN)
-        for j, part in enumerate(parts):
-            count = part.shape[1]
-            start = pl.multiple_of((at[1] ^ j) * count, count)
-            part[a] = total[pl.ds(start, count), :].astype(part.dtype)
+def split_rows(at, rows, other, parts, total, a):
+    total[...] = mul(rows[...], other[a], TN)
+    for j, part in enumerate(parts):
+        count = part.shape[1]
+        start = pl.multiple_of((at[1] ^ j) * count, count)
+        part[a] = total[pl.ds(start, count), :].astype(part.dtype)
 
 
 def weight_grad_body(at, rows, other, *refs):
-    split_rows(at, rows, other, refs[:-1], refs[-1])
+    loop(other.shape[0], lambda a: split_rows(at, rows, other, refs[:-1], refs[-1], a))
 
 
 def query_grad_body(at, rows, hot, *refs):
     dmixed = refs[E]
     spread_pairs(at, refs[:E], hot, dmixed, 2)
-    split_rows(at, rows, dmixed, refs[E + 1 : -1], refs[-1])
+    for e in range(E):
+        split_rows(at, rows, dmixed, refs[E + 1 : -1], refs[-1], e)
 
 
 def attention_mask(at):
@@ -287,26 +327,26 @@
 
 def attention_back_body(at, own, *refs):
     got = refs[: E - 1]
-    rows, low, probs, context, grads, sums = refs[E - 1 :]
+    rows, low, probs, context, grads, sums, dcontext, inner = refs[E - 1 :]
     cols = columns(rows[...])
     scale = cols[:, 0:1]
-    inner = jnp.zeros((TOK, 1), F32)
+    inner[...] = jnp.zeros((TOK, HS), F32)
     dprob = []
-    dcontext = []
     for i in range(TOPK):
         raw = own[i]
         for one in got:
             raw = raw + one[i].astype(F32)
         dprob.append(jnp.sum(context[i].astype(F32) * raw, axis=-1, keepdims=True))
-        dcontext.append((raw * cols[:, 1 + i : 2 + i]).astype(BF16))
-    for h in range(low.shape[2] // HS):
-        head = slice(h * HS, (h + 1) * HS)
+        dcontext[i] = (raw * cols[:, 1 + i : 2 + i]).astype(BF16)
+
+    def attend(h):
+        head = pl.ds(pl.multiple_of(h * HS, HS), HS)
         key, value = low[0, :, head], low[1, :, head]
         dkey = jnp.zeros((TOK, HS), F32)
         dvalue = jnp.zeros((TOK, HS), F32)
         for i in range(TOPK):
             query = low[2 + i, :, head]
-            grad = dcontext[i][:, head]
+            grad = dcontext[i, :, head]
             prob = probs[h, i * TOK : (i + 1) * TOK, :]
             dweight = mul(grad, value, NT)
             dscore = prob * (dweight - jnp.sum(prob * dweight, axis=-1, keepdims=True))
@@ -314,17 +354,55 @@
             done = mul(dscore, key, NN) * HS ** (-0.5)
             dkey = dkey + mul(dscore, query, TN)
             dvalue = dvalue + mul(prob.astype(BF16), grad, TN)
-            inner = inner + jnp.sum(done * query.astype(F32), axis=-1, keepdims=True)
+            inner[...] = inner[...] + done * query.astype(F32)
             grads[2 + i, :, head] = (done * scale).astype(BF16)
         dkey = dkey * HS ** (-0.5)
-        inner = inner + jnp.sum(
-            dkey * key.astype(F32) + dvalue * value.astype(F32), axis=-1, keepdims=True
-        )
+        inner[...] = inner[...] + dkey * key.astype(F32) + dvalue * value.astype(F32)
         grads[0, :, head] = (dkey * scale).astype(BF16)
         grads[1, :, head] = (dvalue * scale).astype(BF16)
+
+    loop(low.shape[2] // HS, attend)
+    total = jnp.sum(inner[...], axis=-1, keepdims=True)
     lane = lax.broadcasted_iota(jnp.int32, (TOK, TOK), 1)
-    table = jnp.where(lane == 0, dprob[0], jnp.where(lane == 1, dprob[1], jnp.where(lane == 2, inner, 0.0)))
+    table = jnp.where(lane == 0, dprob[0], jnp.where(lane == 1, dprob[1], jnp.where(lane == 2, total, 0.0)))
     sums[...] = jnp.transpose(table)[0:8]
+
+
+def expert_body(at, gate_up, dact, full, act, gated, dpair, scaled, stats):
+    def one(n):
+        where = pl.ds(pl.multiple_of(n * SLOTS, SLOTS), SLOTS)
+        pairs = full[where, full.shape[1] - 128 :].astype(F32)
+        scale, gate = pairs[:, 0:1] + pairs[:, 1:2], pairs[:, 2:3] + pairs[:, 3:4]
+        gate_pre, up_pre = gate_up[0, where, :] * scale, gate_up[1, where, :] * scale
+        sig = 1.0 / (1.0 + jnp.exp(-gate_pre))
+        silu = gate_pre * sig
+        low = (silu * up_pre).astype(BF16)
+        raw = dact[where, :]
+        grad = raw * gate
+        dgate = (grad * up_pre * sig * (1.0 + gate_pre * (1.0 - sig))).astype(BF16)
+        dup = (grad * silu).astype(BF16)
+        wide, dgate_wide, dup_wide = low.astype(F32), dgate.astype(F32), dup.astype(F32)
+        act[where, :] = low
+        gated[where, :] = (wide * gate).astype(BF16)
+        dpair[0, where, :], dpair[1, where, :] = dgate, dup
+        scaled[0, where, :] = (dgate_wide * scale).astype(BF16)
+        scaled[1, where, :] = (dup_wide * scale).astype(BF16)
+        dprob = jnp.sum(wide * raw, axis=-1, keepdims=True)
+        inner = jnp.sum(dgate_wide * gate_pre + dup_wide * up_pre, axis=-1, keepdims=True)
+        lane = lax.broadcasted_iota(jnp.int32, (SLOTS, 128), 1)
+        stats[where, :] = jnp.where(lane == 0, dprob, jnp.where(lane == 1, inner, 0.0))
+
+    loop(dact.shape[0] // SLOTS, one)
+
+
+def rows_grad_body(at, left, right, out):
+    part = 512
+
+    def one(n):
+        a, where = n % left.shape[0], pl.ds(pl.multiple_of((n // left.shape[0]) * part, part), part)
+        out[a, :, where] = mul(left[a], right[:, where], TN)
+
+    loop(left.shape[0] * (out.shape[2] // part), one)
 
 
 def columns(rows):
@@ -450,13 +528,13 @@
     out[:, E * size :] = two_halves([scale, gate])
 
 
+def piece_of(plane, k, size):
+    return pl.ds(pl.multiple_of((plane ^ k) * size, size), size)
+
+
 def join_pieces(at, pieces, out, size):
     for k in range(E):
-        for p in range(E):
-
-            @pl.when((at[2] ^ k) == p)
-            def _(k=k, p=p):
-                out[:, p * size : (p + 1) * size] = pieces[k][:, :size]
+        out[:, piece_of(at[2], k, size)] = pieces[k][:, :size]
 
 
 def join_body(at, *refs):
@@ -469,12 +547,7 @@
         store[...] = (own[...] + got[...].astype(F32)).astype(BF16)
         size = outs[0].shape[1] - extra
         for k in range(E):
-            for p in range(E):
-
-                @pl.when((at[2] ^ k) == p)
-                def _(k=k, p=p):
-                    outs[k][:, :size] = store[:, p * size : (p + 1) * size]
-
+            outs[k][:, :size] = store[:, piece_of(at[2], k, size)]
             if extra:
                 outs[k][:, size:] = store[:, E * size :]
 
@@ -747,31 +820,22 @@
     full, _ = share(full)
     full = after(full, stats_two)
     expert_rows = full[:, :width]
-    row_pairs = full[:, width : width + 4].astype(F32)
-    row_scale = row_pairs[:, 0:1] + row_pairs[:, 1:2]
-    row_gate = row_pairs[:, 2:3] + row_pairs[:, 3:4]
+    row_gate = jnp.sum(full[:, width + 2 : width + 4].astype(F32), axis=-1, keepdims=True)
     scale_two = lax.rsqrt(stats_two[E] / width + EPSILON)
     logits_two = stats_two[:E] * scale_two
     prob_two = gates(logits_two, hot_two)
 
     gate_up = jnp.einsum("rd,dkf->krf", expert_rows, weight_in, preferred_element_type=F32)
-    gate_pre = gate_up[0] * row_scale
-    up_pre = gate_up[1] * row_scale
-    gate_sig = jax.nn.sigmoid(gate_pre)
-    silu_gate = gate_pre * gate_sig
-    activation = (silu_gate * up_pre).astype(BF16)
-    dactiv = dact_raw * row_gate
-    dgate_pre = (dactiv * up_pre * gate_sig * (1.0 + gate_pre * (1.0 - gate_sig))).astype(BF16)
-    dup_pre = (dactiv * silu_gate).astype(BF16)
-    dprob_rows = jnp.sum(activation.astype(F32) * dact_raw, axis=-1)
-    inner_rows = jnp.sum(dgate_pre.astype(F32) * gate_pre + dup_pre.astype(F32) * up_pre, axis=-1)
-    drows = jnp.einsum(
-        "krf,dkf->rd", jnp.stack([dgate_pre, dup_pre]), weight_in, preferred_element_type=F32
-    )
-    lanes = jnp.arange(128)
-    row_stats = jnp.where(
-        lanes[None, :] == 0, dprob_rows[:, None], jnp.where(lanes[None, :] == 1, inner_rows[:, None], 0.0)
-    )
+    row_count = expert_rows.shape[0]
+    activation, gated_act, dpair, dboth, row_stats = run(
+        "expert",
+        expert_body,
+        [shape((row_count, hidden_units), BF16)] * 2
+        + [shape((2, row_count, hidden_units), BF16)] * 2
+        + [shape((row_count, 128), F32)],
+        [at, gate_up, dact_raw, full],
+    )
+    drows = jnp.einsum("krf,dkf->rd", dpair, weight_in, preferred_element_type=F32)
 
     def give_back(rows):
         half = rows.shape[0] // 2
@@ -851,8 +915,13 @@
     expert_out = dot(activation, weight_down, ((1,), (0,))) * row_gate
     mixture = give_back(expert_out)
     output_grad, output_got = weight_sum(output_parts)
-    gated_act = (activation.astype(F32) * row_gate).astype(BF16)
-    down_grad = dot(after(gated_act, dcontext_blocks[0]), grad_rows, ((0,), (0,)))
+    (down_grad,) = run(
+        "down_grad",
+        rows_grad_body,
+        [shape((1, hidden_units, width), F32)],
+        [at, after(gated_act, dcontext_blocks[0])[None], grad_rows],
+        flops=4 * row_count * hidden_units * width,
+    )
     grads_low, home_sums = run(
         "attention_back",
         attention_back_body,
@@ -865,17 +934,15 @@
             probs,
             context,
         ],
+        [pltpu.VMEM((TOPK, TOK, local_width), BF16), pltpu.VMEM((TOK, HS), F32)],
     )
     grad_planes = gather_planes(grads_low)
-    dboth = jnp.stack(
-        [
-            (dgate_pre.astype(F32) * row_scale).astype(BF16),
-            (dup_pre.astype(F32) * row_scale).astype(BF16),
-        ],
-        axis=1,
-    )
-    up_grad = jnp.einsum(
-        "rd,rkf->dkf", expert_rows, after(dboth, grad_planes[E - 1]), preferred_element_type=F32
+    (up_grad,) = run(
+        "up_grad",
+        rows_grad_body,
+        [shape((2, hidden_units, width), F32)],
+        [at, after(dboth, grad_planes[E - 1]), expert_rows],
+        flops=4 * row_count * hidden_units * width,
     )
     dmixed, *query_grad_parts = run(
         "query_grad",
@@ -944,8 +1011,8 @@
         output_grad,
         mine[0],
         mine[1:5].T,
-        up_grad[None],
-        down_grad[None],
+        up_grad.transpose(2, 0, 1)[None],
+        down_grad,
     )
 
 

time: 425 us -> 436 us (1.026)
  Pallas kernels: 61.8 us -> 94.8 us
  matrix products: 47.1 us -> 24.6 us
  waiting for transfers between devices: 166 us -> 159 us
  other arithmetic: 32.6 us -> 38 us
    pallas_call x16 -> x19, Pallas kernels: 61.8 us -> 94.8 us  [run(): pl.pallas_call(body, out_shape=tuple(outs), in_specs=[pl.BlockSpec(memory...]
    dot_general x2 -> x1, matrix products: 23.5 us -> 6.89 us  [local(): jnp.einsum('krf,dkf->rd', dpair, weight_in, preferred_element_type=F32)]
    dot_general x7 -> x6, matrix products: 17.9 us -> 10.7 us  [dot(): lax.dot_general(left, right, ((contract[0], contract[1]), ((), ())), prec...]
    ppermute x6, waiting for transfers between devices: 8.91 us -> 3.95 us  [swap(): return lax.ppermute(values, ('wide', 'narrow'), pairs)]
    add x2, other arithmetic: 0.59 us -> 5.04 us  [give_back(): rows = rows[:half] + by_narrow(rows[half:].astype(BF16), 1).astype(F32)]
  transfers between devices with their start and end apart: 69 -> 69, of which waited for: 35 -> 33; matrix products, arithmetic and copies ran while one was open for 14% -> 12% of each run, Pallas kernels for 13% -> 18%
where the time goes in v5:
time: 436 us; the launch traced here: 434 us
  waiting for transfers between devices  159 us (36%)
  starting transfers between devices  100 us (23%)
  Pallas kernels  94.8 us (22%)
  other arithmetic  38 us (9%)
  matrix products  24.6 us (6%)
  local copies, waits for them, and re-layouts  16.4 us (4%)
    pallas_call x19, Pallas kernels, run(): pl.pallas_call(body, out_shape=tuple(outs), in_specs=[pl.BlockSpec(memory...  94.8 us
    ppermute x29, waiting for transfers between devices, by_plane(): lax.ppermute(values, 'wide', [(i, i ^ k * subs) for i in range(wide_count)])  92.9 us
    ppermute x29, starting transfers between devices, by_plane(): lax.ppermute(values, 'wide', [(i, i ^ k * subs) for i in range(wide_count)])  55.1 us
    ppermute x18, waiting for transfers between devices, by_narrow(): lax.ppermute(values, 'narrow', [(i, i ^ k) for i in range(narrow_count)])  26.9 us
    ppermute x8, waiting for transfers between devices, by_side(): return lax.ppermute(values, ('wide', 'narrow'), pairs)  25.6 us
    ppermute x6, starting transfers between devices, swap(): return lax.ppermute(values, ('wide', 'narrow'), pairs)  23.8 us
    dot_general x6, matrix products, dot(): lax.dot_general(left, right, ((contract[0], contract[1]), ((), ())), prec...  10.7 us
    ppermute x8, waiting for transfers between devices, by_sub(): return lax.ppermute(values, 'wide', [(i, i ^ k) for i in range(wide_count)])  9.77 us
  transfers between devices with their start and end apart: 69, of which 33 were waited for; matrix products, arithmetic and copies ran while one was open for 12% of the time, Pallas kernels for 18%

profile of v5, /device:TPU:2, one launch (start us, length us, event | category | flops | bytes accessed | tf_op | source)
XLA Modules:
  0.0 434.3 jit_solution(1074528523056399278)
XLA Ops:
  38.2 7.6 %collective-permute-done.6.refs_1_.refs_0_ = bf16[272,512]{1,0:T(8,128)(2,1)S(1)} collective-permute-done((bf16[272,512]{1,0:T(8,128)(2,1)}, bf16[272,512]{1,0:T(8,128)(2,1)S(1)}, u32[]{:S(2)}, u32[]{:S(2)}) %collective-permute-start.6) | collective-permute-done | bytes 278560 | tf_op jit(solution)/shard_map/ppermute | solution.py:592
  45.8 8.7 %collective-permute-done.7.refs_2_.refs_1_ = bf16[272,512]{1,0:T(8,128)(2,1)} collective-permute-done((bf16[272,512]{1,0:T(8,128)(2,1)}, bf16[272,512]{1,0:T(8,128)(2,1)}, u32[]{:S(2)}, u32[]{:S(2)}) %collective-permute-start.7) | collective-permute-done | bytes 278560 | tf_op jit(solution)/shard_map/ppermute | solution.py:592
  62.5 7.9 %collective-permute-start.10 = (bf16[2,128,512]{2,1,0:T(8,128)(2,1)}, bf16[2,128,512]{2,1,0:T(8,128)(2,1)S(1)}, u32[]{:S(2)}, u32[]{:S(2)}) collective-permute-start(bf16[2,128,512]{2,1,0:T(8,128)(2,1)} %get-tuple-element.117), channel_id=1, source_target_pairs={{0,8},{4,12},{8,0},{12,4},{16,24},{20,28},{24,16},{28,20},{1,9},{5... | collective-permute-start | bytes 786440 | tf_op jit(solution)/shard_map/ppermute | solution.py:592
  81.8 13.8 %collective-permute-done.11.refs_5_ = bf16[2,128,512]{2,1,0:T(8,128)(2,1)} collective-permute-done((bf16[2,128,512]{2,1,0:T(8,128)(2,1)}, bf16[2,128,512]{2,1,0:T(8,128)(2,1)}, u32[]{:S(2)}, u32[]{:S(2)}) %collective-permute-start.11) | collective-permute-done | bytes 262176 | tf_op jit(solution)/shard_map/ppermute | solution.py:592
  95.6 5.5 %attention.1 = (f32[16,128]{1,0:T(8,128)}, bf16[4,128,512]{2,1,0:T(8,128)(2,1)}, f32[4,256,128]{2,1,0:T(8,128)}, bf16[2,128,512]{2,1,0:T(8,128)(2,1)}, bf16[2,128,512]{2,1,0:T(8,128)(2,1)}) custom-call(s32[4]{0:T(128)} %bitcast.155, f32[2,128,512]{2,1,0:T(8,128)} %get-tuple-element.109.own_kv, bf16[272,512]{1,0:T(8,128)(2,1)} %copy-done.25, ...), custom_call_target="tpu_custom_call" | custom-call | flops 1 | bytes 1 | tf_op jit(solution)/shard_map/attention/pallas_call | solution.py:52
  116.5 14.0 %collective-permute-done.14.refs_2_ = bf16[2,128,512]{2,1,0:T(8,128)(2,1)} collective-permute-done((bf16[2,128,512]{2,1,0:T(8,128)(2,1)}, bf16[2,128,512]{2,1,0:T(8,128)(2,1)}, u32[]{:S(2)}, u32[]{:S(2)}) %collective-permute-start.14) | collective-permute-done | bytes 262176 | tf_op jit(solution)/shard_map/ppermute | solution.py:592
  153.1 5.4 %collective-permute-done.26.refs_2_ = bf16[80,640]{1,0:T(8,128)(2,1)} collective-permute-done((bf16[80,640]{1,0:T(8,128)(2,1)}, bf16[80,640]{1,0:T(8,128)(2,1)}, u32[]{:S(2)}, u32[]{:S(2)}) %collective-permute-start.26) | collective-permute-done | bytes 102432 | tf_op jit(solution)/shard_map/ppermute | solution.py:592
  161.4 6.9 %collective-permute-done.28 = bf16[80,2176]{1,0:T(8,128)(2,1)S(1)} collective-permute-done((bf16[80,2176]{1,0:T(8,128)(2,1)}, bf16[80,2176]{1,0:T(8,128)(2,1)S(1)}, u32[]{:S(2)}, u32[]{:S(2)}) %collective-permute-start.28) | collective-permute-done | bytes 348192 | tf_op jit(solution)/shard_map/ppermute | solution.py:614
  171.3 9.2 %collective-permute-done.29 = bf16[160,2176]{1,0:T(8,128)(2,1)S(1)} collective-permute-done((bf16[160,2176]{1,0:T(8,128)(2,1)S(1)}, bf16[160,2176]{1,0:T(8,128)(2,1)S(1)}, u32[]{:S(2)}, u32[]{:S(2)}) %collective-permute-start.29) | collective-permute-done | bytes 696352 | tf_op jit(solution)/shard_map/ppermute | solution.py:614
  196.3 6.2 %fusion.14.gate_up = f32[2,640,704]{2,1,0:T(8,128)} fusion(bf16[1,2048,2,704]{1,3,2,0:T(8,128)(2,1)S(1)} %bitcast.157, bf16[640,2176]{1,0:T(8,128)(2,1)S(1)} %pad_maximum_fusion.1.full), kind=kOutput, calls=%fused_computation.22 | convolution fusion | flops 3690987520 | bytes 11993088 | tf_op jit(solution)/shard_map/rd,dkf->krf/dot_general | solution.py:828
  202.5 10.2 %expert.1 = (bf16[640,704]{1,0:T(8,128)(2,1)}, bf16[640,704]{1,0:T(8,128)(2,1)}, bf16[2,640,704]{2,1,0:T(8,128)(2,1)}, bf16[2,640,704]{2,1,0:T(8,128)(2,1)}, f32[640,128]{1,0:T(8,128)}) custom-call(s32[4]{0:T(128)} %pad_add_fusion.at, f32[2,640,704]{2,1,0:T(8,128)} %fusion.14.gate_up, f32[640,704]{1,0:T(8,128)} %fusion.8.dact, bf16[640,2176]{1,0:T(8,128)(2,1)} %copy-done.2), custom_call_target="tpu_custom_call" | custom-call | flops 1 | bytes 1 | tf_op jit(solution)/shard_map/expert/pallas_call | solution.py:52
  212.7 6.9 %fusion.4 = f32[640,2048]{1,0:T(8,128)S(1)} fusion(bf16[2,640,704]{2,1,0:T(8,128)(2,1)} %get-tuple-element.145, bf16[1,2048,2,704]{1,3,2,0:T(8,128)(2,1)} %param.23), kind=kOutput, calls=%fused_computation.7 | convolution fusion | flops 3690987520 | bytes 12812288 | tf_op jit(solution)/shard_map/krf,dkf->rd/dot_general | solution.py:838
  267.1 6.1 %collective-permute-done.43.refs_2_ = bf16[128,512]{1,0:T(8,128)(2,1)S(1)} collective-permute-done((bf16[128,512]{1,0:T(8,128)(2,1)S(1)}, bf16[128,512]{1,0:T(8,128)(2,1)S(1)}, u32[]{:S(2)}, u32[]{:S(2)}) %collective-permute-start.43) | collective-permute-done | bytes 131104 | tf_op jit(solution)/shard_map/ppermute | solution.py:598
  278.6 5.5 %dcontext.1 = (bf16[512,512]{1,0:T(8,128)(2,1)}, f32[2,128,512]{2,1,0:T(8,128)}, bf16[2,128,512]{2,1,0:T(8,128)(2,1)}, bf16[2,128,512]{2,1,0:T(8,128)(2,1)}, bf16[2,128,512]{2,1,0:T(8,128)(2,1)}) custom-call(s32[4]{0:T(128)} %pad_add_fusion.at, bf16[128,512]{1,0:T(8,128)(2,1)} %copy-done.33, bf16[128,512]{1,0:T(8,128)(2,1)} %copy-done.41, ...), custom_call_target="tpu_custom_call" | custom-call | flops 1 | bytes 1 | tf_op jit(solution)/shard_map/dcontext/pallas_call | solution.py:52
  288.6 5.6 %output_grad.1 = (f32[4,256,512]{2,1,0:T(8,128)}, bf16[4,256,512]{2,1,0:T(8,128)(2,1)}) custom-call(s32[4]{0:T(128)} %pad_add_fusion.at, bf16[512,512]{1,0:T(8,128)(2,1)} %get-tuple-element.157.rows, bf16[4,512,512]{2,1,0:T(8,128)(2,1)} %get-tuple-element.158.other), custom_call_target="tpu_custom_call" | custom-call | flops 1 | bytes 1 | tf_op jit(solution)/shard_map/output_grad/pallas_call | solution.py:52
  295.7 7.6 %down_grad.1 = f32[1,704,2048]{2,1,0:T(8,128)} custom-call(s32[4]{0:T(128)} %pad_add_fusion.at, bf16[1,640,704]{2,1,0:T(8,128)(2,1)} %bitcast.158, bf16[640,2048]{1,0:T(8,128)(2,1)} %pad_maximum_fusion.2.right), custom_call_target="tpu_custom_call" | custom-call | flops 3690987520 | bytes 1 | tf_op jit(solution)/shard_map/down_grad/pallas_call | solution.py:52
  305.9 5.5 %attention_back.1 = (bf16[4,128,512]{2,1,0:T(8,128)(2,1)}, f32[8,128]{1,0:T(8,128)}) custom-call(s32[4]{0:T(128)} %pad_add_fusion.at, f32[2,128,512]{2,1,0:T(8,128)} %get-tuple-element.162.own, bf16[2,128,512]{2,1,0:T(8,128)(2,1)} %copy-done.37, bf16[2,128,512]{2,1,0:T(8,128)(2,1)} %collective-permute-done.46.refs_1_, ...), custom_call_target="tpu_custom_call" | custom-call | flops 1 | bytes 1 | tf_op jit(solution)/shard_map/attention_back/pallas_call | solution.py:52
  312.8 5.5 %collective-permute-start.49 = (bf16[4,128,512]{2,1,0:T(8,128)(2,1)}, bf16[4,128,512]{2,1,0:T(8,128)(2,1)}, u32[]{:S(2)}, u32[]{:S(2)}) collective-permute-start(bf16[4,128,512]{2,1,0:T(8,128)(2,1)} %get-tuple-element.178.refs_0_), channel_id=1, source_target_pairs={{0,16},{4,20},{8,24},{12,28},{16,0},{20,4},{24,8},{28,12},{1,17},{... | collective-permute-start | bytes 1572872 | tf_op jit(solution)/shard_map/ppermute | solution.py:592
  322.3 6.2 %collective-permute-done.50.refs_3_ = bf16[4,128,512]{2,1,0:T(8,128)(2,1)} collective-permute-done((bf16[4,128,512]{2,1,0:T(8,128)(2,1)}, bf16[4,128,512]{2,1,0:T(8,128)(2,1)}, u32[]{:S(2)}, u32[]{:S(2)}) %collective-permute-start.50) | collective-permute-done | bytes 524320 | tf_op jit(solution)/shard_map/ppermute | solution.py:592
  328.4 12.9 %up_grad.1 = f32[2,704,2048]{2,1,0:T(8,128)} custom-call(s32[4]{0:T(128)} %pad_add_fusion.at, bf16[2,640,704]{2,1,0:T(8,128)(2,1)} %get-tuple-element.172.left, bf16[640,2048]{1,0:T(8,128)(2,1)} %slice.174.right), custom_call_target="tpu_custom_call" | custom-call | flops 3690987520 | bytes 1 | tf_op jit(solution)/shard_map/up_grad/pallas_call | solution.py:52
  341.3 18.4 %collective-permute-done.49.refs_2_ = bf16[4,128,512]{2,1,0:T(8,128)(2,1)} collective-permute-done((bf16[4,128,512]{2,1,0:T(8,128)(2,1)}, bf16[4,128,512]{2,1,0:T(8,128)(2,1)}, u32[]{:S(2)}, u32[]{:S(2)}) %collective-permute-start.49) | collective-permute-done | bytes 524320 | tf_op jit(solution)/shard_map/ppermute | solution.py:592
  359.7 5.3 %query_grad.1 = (bf16[4,512,512]{2,1,0:T(8,128)(2,1)}, f32[4,256,512]{2,1,0:T(8,128)}, bf16[4,256,512]{2,1,0:T(8,128)(2,1)}) custom-call(s32[4]{0:T(128)} %pad_add_fusion.at, bf16[512,512]{1,0:T(8,128)(2,1)} %get-tuple-element.113.refs_0_.rows, f32[512,8]{1,0:T(8,128)} %get-tuple-element.114.refs_1_.refs_4_.hot, ...), custom_call_target="tpu_custom_call" | custom-call | flops 1 | bytes 1 | tf_op jit(solution)/shard_map/query_grad/pallas_call | solution.py:52
  365.0 6.2 %input.1 = (bf16[2,512,512]{2,1,0:T(8,128)(2,1)}, f32[1,512]{1,0:T(1,128)}, f32[128,512]{1,0:T(8,128)}, f32[128,512]{1,0:T(8,128)}, bf16[2,128,512]{2,1,0:T(8,128)(2,1)}) custom-call(s32[4]{0:T(128)} %pad_add_fusion.at, bf16[4,128,512]{2,1,0:T(8,128)(2,1)} %get-tuple-element.178.refs_0_, bf16[4,128,512]{2,1,0:T(8,128)(2,1)} %collective-permute-done.48.refs_1_, ...), custom_call_target="tpu_custom_call" | custom-call | flops 1 | bytes 1 | tf_op jit(solution)/shard_map/input/pallas_call | solution.py:52
  409.1 5.7 %collective-permute-start.59 = (bf16[128,512]{1,0:T(8,128)(2,1)S(1)}, bf16[128,512]{1,0:T(8,128)(2,1)S(1)}, u32[]{:S(2)}, u32[]{:S(2)}) collective-permute-start(bf16[128,512]{1,0:T(8,128)(2,1)S(1)} %fusion.20), channel_id=1, source_target_pairs={{0,0},{1,8},{2,16},{3,24},{4,4},{5,12},{6,20},{7,28},{8,1},{9,9},{... | collective-permute-start | bytes 393224 | tf_op jit(solution)/shard_map/ppermute | solution.py:606
  (347 shorter events, 240.1 us)
Async XLA Ops:
  15.7 41.1 %collective-permute-start.9 = (bf16[4,256,512]{2,1,0:T(8,128)(2,1)}, bf16[4,256,512]{2,1,0:T(8,128)(2,1)}, u32[]{:S(2)}, u32[]{:S(2)}) collective-permute-start(bf16[4,256,512]{2,1,0:T(8,128)(2,1)} %refs_7_.3), channel_id=1, source_target_pairs={{0,4},{4,0},{8,12},{12,8},{16,20},{20,16},{24,28},{28,24},{1,5},{5... | collective-permute-start | bytes 3145736 | tf_op jit(solution)/shard_map/ppermute | solution.py:595
  31.8 22.7 %collective-permute-start.7 = (bf16[272,512]{1,0:T(8,128)(2,1)}, bf16[272,512]{1,0:T(8,128)(2,1)}, u32[]{:S(2)}, u32[]{:S(2)}) collective-permute-start(bf16[272,512]{1,0:T(8,128)(2,1)} %get-tuple-element.111), channel_id=1, source_target_pairs={{0,16},{4,20},{8,24},{12,28},{16,0},{20,4},{24,8},{28,12},{1,17},{... | collective-permute-start | bytes 835592 | tf_op jit(solution)/shard_map/ppermute | solution.py:592
  34.4 20.1 %collective-permute-start.8 = (bf16[272,512]{1,0:T(8,128)(2,1)}, bf16[272,512]{1,0:T(8,128)(2,1)}, u32[]{:S(2)}, u32[]{:S(2)}) collective-permute-start(bf16[272,512]{1,0:T(8,128)(2,1)} %get-tuple-element.112), channel_id=1, source_target_pairs={{0,24},{4,28},{8,16},{12,20},{16,8},{20,12},{24,0},{28,4},{1,25},{... | collective-permute-start | bytes 835592 | tf_op jit(solution)/shard_map/ppermute | solution.py:592
  35.4 37.0 %collective-permute-start.19 = (bf16[128,512]{1,0:T(8,128)(2,1)}, bf16[128,512]{1,0:T(8,128)(2,1)S(1)}, u32[]{:S(2)}, u32[]{:S(2)}) collective-permute-start(bf16[128,512]{1,0:T(8,128)(2,1)} %param.15), channel_id=1, source_target_pairs={{0,0},{1,8},{2,16},{3,24},{4,4},{5,12},{6,20},{7,28},{8,1},{9,9},{... | collective-permute-start | bytes 393224 | tf_op jit(solution)/shard_map/ppermute | solution.py:606
  56.7 73.8 %collective-permute-start.16 = (bf16[4,256,512]{2,1,0:T(8,128)(2,1)}, bf16[4,256,512]{2,1,0:T(8,128)(2,1)}, u32[]{:S(2)}, u32[]{:S(2)}) collective-permute-start(bf16[4,256,512]{2,1,0:T(8,128)(2,1)} %refs_5_.4), channel_id=1, source_target_pairs={{0,4},{4,0},{8,12},{12,8},{16,20},{20,16},{24,28},{28,24},{1,5},{5... | collective-permute-start | bytes 3145736 | tf_op jit(solution)/shard_map/ppermute | solution.py:595
  70.5 25.1 %collective-permute-start.11 = (bf16[2,128,512]{2,1,0:T(8,128)(2,1)}, bf16[2,128,512]{2,1,0:T(8,128)(2,1)}, u32[]{:S(2)}, u32[]{:S(2)}) collective-permute-start(bf16[2,128,512]{2,1,0:T(8,128)(2,1)} %get-tuple-element.118), channel_id=1, source_target_pairs={{0,16},{4,20},{8,24},{12,28},{16,0},{20,4},{24,8},{28,12},{1,17},{... | collective-permute-start | bytes 786440 | tf_op jit(solution)/shard_map/ppermute | solution.py:592
  72.6 23.0 %collective-permute-start.12 = (bf16[2,128,512]{2,1,0:T(8,128)(2,1)}, bf16[2,128,512]{2,1,0:T(8,128)(2,1)}, u32[]{:S(2)}, u32[]{:S(2)}) collective-permute-start(bf16[2,128,512]{2,1,0:T(8,128)(2,1)} %get-tuple-element.119), channel_id=1, source_target_pairs={{0,24},{4,28},{8,16},{12,20},{16,8},{20,12},{24,0},{28,4},{1,25},{... | collective-permute-start | bytes 786440 | tf_op jit(solution)/shard_map/ppermute | solution.py:592
  74.9 26.2 %collective-permute-start.22 = (bf16[80,512]{1,0:T(8,128)(2,1)}, bf16[80,512]{1,0:T(8,128)(2,1)S(1)}, u32[]{:S(2)}, u32[]{:S(2)}) collective-permute-start(bf16[80,512]{1,0:T(8,128)(2,1)} %get-tuple-element.211), channel_id=1, source_target_pairs={{0,24},{4,28},{8,16},{12,20},{16,8},{20,12},{24,0},{28,4},{1,25},{... | collective-permute-start | bytes 245768 | tf_op jit(solution)/shard_map/ppermute | solution.py:592
  79.6 22.2 %collective-permute-start.21 = (bf16[80,512]{1,0:T(8,128)(2,1)S(1)}, bf16[80,512]{1,0:T(8,128)(2,1)}, u32[]{:S(2)}, u32[]{:S(2)}) collective-permute-start(bf16[80,512]{1,0:T(8,128)(2,1)S(1)} %get-tuple-element.212), channel_id=1, source_target_pairs={{0,16},{4,20},{8,24},{12,28},{16,0},{20,4},{24,8},{28,12},{1,17},{... | collective-permute-start | bytes 245768 | tf_op jit(solution)/shard_map/ppermute | solution.py:592
  108.5 22.1 %collective-permute-start.14 = (bf16[2,128,512]{2,1,0:T(8,128)(2,1)}, bf16[2,128,512]{2,1,0:T(8,128)(2,1)}, u32[]{:S(2)}, u32[]{:S(2)}) collective-permute-start(bf16[2,128,512]{2,1,0:T(8,128)(2,1)} %get-tuple-element.122.refs_0_), channel_id=1, source_target_pairs={{0,16},{4,20},{8,24},{12,28},{16,0},{20,4},{24,8},{28,12},{1,17},{... | collective-permute-start | bytes 786440 | tf_op jit(solution)/shard_map/ppermute | solution.py:592
  114.5 25.2 %collective-permute-start.24 = (bf16[160,2048]{1,0:T(8,128)(2,1)}, bf16[160,2048]{1,0:T(8,128)(2,1)}, u32[]{:S(2)}, u32[]{:S(2)}) collective-permute-start(bf16[160,2048]{1,0:T(8,128)(2,1)} %pad_maximum_fusion.6), channel_id=1, source_target_pairs={{0,2},{1,5},{2,0},{3,7},{4,6},{5,1},{6,4},{7,3},{8,10},{9,13},{10,... | collective-permute-start | bytes 1966088 | tf_op jit(solution)/shard_map/ppermute | solution.py:614
  223.0 43.3 %collective-permute-start.61 = (bf16[16,512]{1,0:T(8,128)(2,1)}, bf16[16,512]{1,0:T(8,128)(2,1)}, u32[]{:S(2)}, u32[]{:S(2)}) collective-permute-start(bf16[16,512]{1,0:T(8,128)(2,1)} %bitcast.60), channel_id=1, source_target_pairs={{0,0},{1,8},{2,16},{3,24},{4,4},{5,12},{6,20},{7,28},{8,1},{9,9},{... | collective-permute-start | bytes 49160 | tf_op jit(solution)/shard_map/ppermute | solution.py:606
  234.6 21.5 %collective-permute-start.34 = (bf16[320,2048]{1,0:T(8,128)(2,1)S(1)}, bf16[320,2048]{1,0:T(8,128)(2,1)}, u32[]{:S(2)}, u32[]{:S(2)}) collective-permute-start(bf16[320,2048]{1,0:T(8,128)(2,1)S(1)} %slice.330), channel_id=1, source_target_pairs={{0,1},{1,0},{2,3},{3,2},{4,5},{5,4},{6,7},{7,6},{8,9},{9,8},{10,11... | collective-permute-start | bytes 3932168 | tf_op jit(solution)/shard_map/ppermute | solution.py:598
  259.6 58.7 %collective-permute-start.35 = (bf16[160,2048]{1,0:T(8,128)(2,1)}, bf16[160,2048]{1,0:T(8,128)(2,1)}, u32[]{:S(2)}, u32[]{:S(2)}) collective-permute-start(bf16[160,2048]{1,0:T(8,128)(2,1)} %slice.332), channel_id=1, source_target_pairs={{0,2},{1,5},{2,0},{3,7},{4,6},{5,1},{6,4},{7,3},{8,10},{9,13},{10,... | collective-permute-start | bytes 1966088 | tf_op jit(solution)/shard_map/ppermute | solution.py:614
  284.2 19.1 %collective-permute-start.45 = (bf16[2,128,512]{2,1,0:T(8,128)(2,1)}, bf16[2,128,512]{2,1,0:T(8,128)(2,1)S(1)}, u32[]{:S(2)}, u32[]{:S(2)}) collective-permute-start(bf16[2,128,512]{2,1,0:T(8,128)(2,1)} %get-tuple-element.154), channel_id=1, source_target_pairs={{0,8},{4,12},{8,0},{12,4},{16,24},{20,28},{24,16},{28,20},{1,9},{5... | collective-permute-start | bytes 786440 | tf_op jit(solution)/shard_map/ppermute | solution.py:592
  284.2 21.7 %collective-permute-start.46 = (bf16[2,128,512]{2,1,0:T(8,128)(2,1)}, bf16[2,128,512]{2,1,0:T(8,128)(2,1)}, u32[]{:S(2)}, u32[]{:S(2)}) collective-permute-start(bf16[2,128,512]{2,1,0:T(8,128)(2,1)} %get-tuple-element.155), channel_id=1, source_target_pairs={{0,16},{4,20},{8,24},{12,28},{16,0},{20,4},{24,8},{28,12},{1,17},{... | collective-permute-start | bytes 786440 | tf_op jit(solution)/shard_map/ppermute | solution.py:592
  285.4 20.5 %collective-permute-start.47 = (bf16[2,128,512]{2,1,0:T(8,128)(2,1)}, bf16[2,128,512]{2,1,0:T(8,128)(2,1)}, u32[]{:S(2)}, u32[]{:S(2)}) collective-permute-start(bf16[2,128,512]{2,1,0:T(8,128)(2,1)} %get-tuple-element.156), channel_id=1, source_target_pairs={{0,24},{4,28},{8,16},{12,20},{16,8},{20,12},{24,0},{28,4},{1,25},{... | collective-permute-start | bytes 786440 | tf_op jit(solution)/shard_map/ppermute | solution.py:592
  294.1 65.6 %collective-permute-start.51 = (bf16[4,256,512]{2,1,0:T(8,128)(2,1)}, bf16[4,256,512]{2,1,0:T(8,128)(2,1)}, u32[]{:S(2)}, u32[]{:S(2)}) collective-permute-start(bf16[4,256,512]{2,1,0:T(8,128)(2,1)} %get-tuple-element.159), channel_id=1, source_target_pairs={{0,4},{4,0},{8,12},{12,8},{16,20},{20,16},{24,28},{28,24},{1,5},{5... | collective-permute-start | bytes 3145736 | tf_op jit(solution)/shard_map/ppermute | solution.py:595
  312.8 46.8 %collective-permute-start.49 = (bf16[4,128,512]{2,1,0:T(8,128)(2,1)}, bf16[4,128,512]{2,1,0:T(8,128)(2,1)}, u32[]{:S(2)}, u32[]{:S(2)}) collective-permute-start(bf16[4,128,512]{2,1,0:T(8,128)(2,1)} %get-tuple-element.178.refs_0_), channel_id=1, source_target_pairs={{0,16},{4,20},{8,24},{12,28},{16,0},{20,4},{24,8},{28,12},{1,17},{... | collective-permute-start | bytes 1572872 | tf_op jit(solution)/shard_map/ppermute | solution.py:592
  318.3 41.4 %collective-permute-start.48 = (bf16[4,128,512]{2,1,0:T(8,128)(2,1)}, bf16[4,128,512]{2,1,0:T(8,128)(2,1)}, u32[]{:S(2)}, u32[]{:S(2)}) collective-permute-start(bf16[4,128,512]{2,1,0:T(8,128)(2,1)} %get-tuple-element.178.refs_0_), channel_id=1, source_target_pairs={{0,8},{4,12},{8,0},{12,4},{16,24},{20,28},{24,16},{28,20},{1,9},{5... | collective-permute-start | bytes 1572872 | tf_op jit(solution)/shard_map/ppermute | solution.py:592
  320.7 56.0 %collective-permute-start.52 = (bf16[80,2048]{1,0:T(8,128)(2,1)S(1)}, bf16[80,2048]{1,0:T(8,128)(2,1)S(1)}, u32[]{:S(2)}, u32[]{:S(2)}) collective-permute-start(bf16[80,2048]{1,0:T(8,128)(2,1)S(1)} %slice.334), channel_id=1, source_target_pairs={{0,4},{1,3},{2,6},{3,1},{4,0},{5,7},{6,2},{7,5},{8,12},{9,11},{10,... | collective-permute-start | bytes 983048 | tf_op jit(solution)/shard_map/ppermute | solution.py:614
  375.2 29.1 %collective-permute-start.58 = (bf16[4,256,512]{2,1,0:T(8,128)(2,1)}, bf16[4,256,512]{2,1,0:T(8,128)(2,1)S(1)}, u32[]{:S(2)}, u32[]{:S(2)}) collective-permute-start(bf16[4,256,512]{2,1,0:T(8,128)(2,1)} %get-tuple-element.177), channel_id=1, source_target_pairs={{0,4},{4,0},{8,12},{12,8},{16,20},{20,16},{24,28},{28,24},{1,5},{5... | collective-permute-start | bytes 3145736 | tf_op jit(solution)/shard_map/ppermute | solution.py:595
  379.5 22.7 %collective-permute-start.53 = (bf16[80,512]{1,0:T(8,128)(2,1)}, bf16[80,512]{1,0:T(8,128)(2,1)S(1)}, u32[]{:S(2)}, u32[]{:S(2)}) collective-permute-start(bf16[80,512]{1,0:T(8,128)(2,1)} %get-tuple-element.186), channel_id=1, source_target_pairs={{0,8},{4,12},{8,0},{12,4},{16,24},{20,28},{24,16},{28,20},{1,9},{5... | collective-permute-start | bytes 245768 | tf_op jit(solution)/shard_map/ppermute | solution.py:592
  381.8 20.4 %collective-permute-start.54 = (bf16[80,512]{1,0:T(8,128)(2,1)}, bf16[80,512]{1,0:T(8,128)(2,1)S(1)}, u32[]{:S(2)}, u32[]{:S(2)}) collective-permute-start(bf16[80,512]{1,0:T(8,128)(2,1)} %get-tuple-element.187), channel_id=1, source_target_pairs={{0,16},{4,20},{8,24},{12,28},{16,0},{20,4},{24,8},{28,12},{1,17},{... | collective-permute-start | bytes 245768 | tf_op jit(solution)/shard_map/ppermute | solution.py:592
  (108 other events, 1387.7 us)

commit v6 on v3

--- a/solution.py
+++ b/solution.py
@@ -47,7 +47,7 @@
     return jax.ShapeDtypeStruct(tuple(dims), dtype)
 
 
-def run(name, body, outs, args, scratch=()):
+def run(name, body, outs, args, scratch=(), flops=1):
     vector = pl.BlockSpec(memory_space=pltpu.VMEM)
     return pl.pallas_call(
         body,
@@ -55,7 +55,7 @@
         in_specs=[pl.BlockSpec(memory_space=pltpu.SMEM)] + [vector] * (len(args) - 1),
         out_specs=tuple(vector for _ in outs),
         scratch_shapes=list(scratch),
-        cost_estimate=pl.CostEstimate(flops=1, transcendentals=0, bytes_accessed=1),
+        cost_estimate=pl.CostEstimate(flops=flops, transcendentals=0, bytes_accessed=1),
         name=name,
     )(*args)
 
@@ -564,8 +564,10 @@
         other = by_narrow(values, 2)
         return [values, by_narrow(values, 1), other, by_narrow(other, 1)]
 
-    def reduce_narrow(keep_0, keep_2, send):
+    def reduce_narrow(keep_0, keep_2, send, *others):
         got = by_narrow(send, 1)
+        if others:
+            got = after(got, *others)
         other = by_narrow((keep_2 + got[1].astype(F32)).astype(BF16), 2)
         return keep_0, got, other
 
@@ -898,6 +900,7 @@
             *all_streams,
         ],
         [pltpu.VMEM((2 + E, slice_width, local_width), BF16)],
+        flops=14 * rows_all * slice_width * local_width,
     )
     home_rows = swap(after(near, own_stats))
     gain_one_home = home_rows[0].astype(F32)
@@ -913,7 +916,7 @@
         "key_value_grad", weight_grad_body, weight_parts(2), [at, gained, dkv_all], weight_scratch
     )
     kv_grad, kv_got = weight_sum(after(kv_grad_parts, query_got))
-    keep, got, other = after(reduce_narrow(*dnormed_one), kv_grad_parts[-1], query_got)
+    keep, got, other = after(reduce_narrow(*dnormed_one, query_got), kv_grad_parts[-1])
     dnormed_one = keep + got[0].astype(F32) + other.astype(F32)
     turned_out = dhidden + dnormed_one * gain_one_plane
     home_out = swap(turned_out.astype(BF16)).astype(F32)
@@ -924,7 +927,7 @@
     )
 
     small = jnp.concatenate([mlp_terms, gain_row, router_term], axis=0)
-    small = sum_subs(after(sum_narrow(small), kv_got))
+    small = sum_subs(sum_narrow(after(small, query_got)))
     mine = lax.dynamic_slice_in_dim(small, sub * shard_rows, shard_rows, 1)
     router_one_grad = mine[6:10]
     gain_one_grad = mine[5] + jnp.sum(

time: 425 us -> 434 us (1.021)
  starting transfers between devices: 97.6 us -> 104 us
    ppermute x18, waiting for transfers between devices: 24.6 us -> 15.3 us  [by_narrow(): lax.ppermute(values, 'narrow', [(i, i ^ k) for i in range(narrow_count)])]
    ppermute x8, waiting for transfers between devices: 25.6 us -> 18.2 us  [by_side(): return lax.ppermute(values, ('wide', 'narrow'), pairs)]
    ppermute x8, waiting for transfers between devices: 10.2 us -> 16.2 us  [by_sub(): return lax.ppermute(values, 'wide', [(i, i ^ k) for i in range(wide_count)])]
    ppermute x6, waiting for transfers between devices: 8.91 us -> 14.7 us  [swap(): return lax.ppermute(values, ('wide', 'narrow'), pairs)]
  transfers between devices with their start and end apart: 69 -> 69, of which waited for: 35 -> 31; matrix products, arithmetic and copies ran while one was open for 14% -> 15% of each run, Pallas kernels for 13% -> 13%
where the time goes in v6:
time: 434 us; the launch traced here: 431 us
  waiting for transfers between devices  163 us (38%)
  starting transfers between devices  104 us (24%)
  Pallas kernels  61.9 us (14%)
  matrix products  46.4 us (11%)
  other arithmetic  36.5 us (8%)
  local copies, waits for them, and re-layouts  17.2 us (4%)
    ppermute x29, waiting for transfers between devices, by_plane(): lax.ppermute(values, 'wide', [(i, i ^ k * subs) for i in range(wide_count)])  98.3 us
    pallas_call x16, Pallas kernels, run(): pl.pallas_call(body, out_shape=tuple(outs), in_specs=[pl.BlockSpec(memory...  61.9 us
    ppermute x29, starting transfers between devices, by_plane(): lax.ppermute(values, 'wide', [(i, i ^ k * subs) for i in range(wide_count)])  55.1 us
    ppermute x6, starting transfers between devices, swap(): return lax.ppermute(values, ('wide', 'narrow'), pairs)  22.8 us
    dot_general x7, matrix products, dot(): lax.dot_general(left, right, ((contract[0], contract[1]), ((), ())), prec...  18.5 us
    ppermute x8, waiting for transfers between devices, by_side(): return lax.ppermute(values, ('wide', 'narrow'), pairs)  18.2 us
    ppermute x8, waiting for transfers between devices, by_sub(): return lax.ppermute(values, 'wide', [(i, i ^ k) for i in range(wide_count)])  16.2 us
    ppermute x18, waiting for transfers between devices, by_narrow(): lax.ppermute(values, 'narrow', [(i, i ^ k) for i in range(narrow_count)])  15.3 us
  transfers between devices with their start and end apart: 69, of which 31 were waited for; matrix products, arithmetic and copies ran while one was open for 15% of the time, Pallas kernels for 13%

profile of v6, /device:TPU:2, one launch (start us, length us, event | category | flops | bytes accessed | tf_op | source)
XLA Modules:
  0.0 430.9 jit_solution(6611445303543766774)
XLA Ops:
  38.7 7.1 %collective-permute-done.6.refs_1_.refs_0_ = bf16[272,512]{1,0:T(8,128)(2,1)S(1)} collective-permute-done((bf16[272,512]{1,0:T(8,128)(2,1)}, bf16[272,512]{1,0:T(8,128)(2,1)S(1)}, u32[]{:S(2)}, u32[]{:S(2)}) %collective-permute-start.6) | collective-permute-done | bytes 278560 | tf_op jit(solution)/shard_map/ppermute | solution.py:519
  45.8 9.2 %collective-permute-done.7.refs_2_.refs_1_ = bf16[272,512]{1,0:T(8,128)(2,1)} collective-permute-done((bf16[272,512]{1,0:T(8,128)(2,1)}, bf16[272,512]{1,0:T(8,128)(2,1)}, u32[]{:S(2)}, u32[]{:S(2)}) %collective-permute-start.7) | collective-permute-done | bytes 278560 | tf_op jit(solution)/shard_map/ppermute | solution.py:519
  62.2 8.4 %collective-permute-start.10 = (bf16[2,128,512]{2,1,0:T(8,128)(2,1)}, bf16[2,128,512]{2,1,0:T(8,128)(2,1)S(1)}, u32[]{:S(2)}, u32[]{:S(2)}) collective-permute-start(bf16[2,128,512]{2,1,0:T(8,128)(2,1)} %get-tuple-element.113), channel_id=1, source_target_pairs={{0,8},{4,12},{8,0},{12,4},{16,24},{20,28},{24,16},{28,20},{1,9},{5... | collective-permute-start | bytes 786440 | tf_op jit(solution)/shard_map/ppermute | solution.py:519
  82.0 13.8 %collective-permute-done.11.refs_5_ = bf16[2,128,512]{2,1,0:T(8,128)(2,1)} collective-permute-done((bf16[2,128,512]{2,1,0:T(8,128)(2,1)}, bf16[2,128,512]{2,1,0:T(8,128)(2,1)}, u32[]{:S(2)}, u32[]{:S(2)}) %collective-permute-start.11) | collective-permute-done | bytes 262176 | tf_op jit(solution)/shard_map/ppermute | solution.py:519
  96.5 5.4 %attention.1 = (f32[16,128]{1,0:T(8,128)}, bf16[4,128,512]{2,1,0:T(8,128)(2,1)}, f32[4,256,128]{2,1,0:T(8,128)}, bf16[2,128,512]{2,1,0:T(8,128)(2,1)}, bf16[2,128,512]{2,1,0:T(8,128)(2,1)}) custom-call(s32[4]{0:T(128)} %bitcast.188, f32[2,128,512]{2,1,0:T(8,128)} %get-tuple-element.105.own_kv, bf16[272,512]{1,0:T(8,128)(2,1)} %copy-done.26, ...), custom_call_target="tpu_custom_call" | custom-call | flops 1 | bytes 1 | tf_op jit(solution)/shard_map/attention/pallas_call | solution.py:52
  116.7 13.4 %collective-permute-done.14.refs_2_ = bf16[2,128,512]{2,1,0:T(8,128)(2,1)S(1)} collective-permute-done((bf16[2,128,512]{2,1,0:T(8,128)(2,1)}, bf16[2,128,512]{2,1,0:T(8,128)(2,1)S(1)}, u32[]{:S(2)}, u32[]{:S(2)}) %collective-permute-start.14) | collective-permute-done | bytes 262176 | tf_op jit(solution)/shard_map/ppermute | solution.py:519
  130.8 4.6 %output.1 = (bf16[4,512,512]{2,1,0:T(8,128)(2,1)}, f32[128,512]{1,0:T(8,128)}, f32[128,512]{1,0:T(8,128)}, bf16[2,128,512]{2,1,0:T(8,128)(2,1)}) custom-call(s32[4]{0:T(128)} %pad_add_fusion.at, bf16[2,128,512]{2,1,0:T(8,128)(2,1)} %get-tuple-element.118.refs_0_, bf16[2,128,512]{2,1,0:T(8,128)(2,1)} %collective-permute-done.13.refs_1_, ...), custom_call_target="tpu_custom_call" | custom-call | flops 1 | bytes 1 | tf_op jit(solution)/shard_map/output/pallas_call | solution.py:52
  152.8 5.2 %collective-permute-done.26.refs_2_ = bf16[80,640]{1,0:T(8,128)(2,1)S(1)} collective-permute-done((bf16[80,640]{1,0:T(8,128)(2,1)}, bf16[80,640]{1,0:T(8,128)(2,1)S(1)}, u32[]{:S(2)}, u32[]{:S(2)}) %collective-permute-start.26) | collective-permute-done | bytes 102432 | tf_op jit(solution)/shard_map/ppermute | solution.py:519
  162.6 6.0 %collective-permute-done.28 = bf16[80,2176]{1,0:T(8,128)(2,1)S(1)} collective-permute-done((bf16[80,2176]{1,0:T(8,128)(2,1)}, bf16[80,2176]{1,0:T(8,128)(2,1)S(1)}, u32[]{:S(2)}, u32[]{:S(2)}) %collective-permute-start.28) | collective-permute-done | bytes 348192 | tf_op jit(solution)/shard_map/ppermute | solution.py:541
  173.2 7.7 %collective-permute-done.29 = bf16[160,2176]{1,0:T(8,128)(2,1)S(1)} collective-permute-done((bf16[160,2176]{1,0:T(8,128)(2,1)S(1)}, bf16[160,2176]{1,0:T(8,128)(2,1)S(1)}, u32[]{:S(2)}, u32[]{:S(2)}) %collective-permute-start.29) | collective-permute-done | bytes 696352 | tf_op jit(solution)/shard_map/ppermute | solution.py:541
  194.1 4.8 %fusion.18 = f32[2,640,704]{1,2,0:T(8,128)S(1)} fusion(bf16[1,2048,2,704]{1,3,2,0:T(8,128)(2,1)S(1)} %bitcast.190, bf16[640,2176]{1,0:T(8,128)(2,1)S(1)} %pad_maximum_fusion.1), kind=kOutput, calls=%fused_computation.32 | convolution fusion | flops 3690987520 | bytes 11993088 | tf_op jit(solution)/shard_map/rd,dkf->krf/dot_general | solution.py:759
  202.7 14.7 %fusion.4 = f32[640,2048]{1,0:T(8,128)S(1)} fusion(bf16[1,2048,2,704]{1,3,2,0:T(8,128)(2,1)S(1)} %bitcast.190, bf16[1,640,704]{1,2,0:T(8,128)(2,1)S(1)} %bitcast.157, bf16[1,640,704]{1,2,0:T(8,128)(2,1)S(1)} %bitcast.158), kind=kOutput, calls=%fused_computation.7 | convolution fusion | flops 3691888640 | bytes 12812288 | tf_op jit(solution)/shard_map/krf,dkf->rd/dot_general | solution.py:770
  278.1 4.8 %output_grad.1 = (f32[4,256,512]{2,1,0:T(8,128)}, bf16[4,256,512]{2,1,0:T(8,128)(2,1)}) custom-call(s32[4]{0:T(128)} %pad_add_fusion.at, bf16[512,512]{1,0:T(8,128)(2,1)} %get-tuple-element.150.rows, bf16[4,512,512]{2,1,0:T(8,128)(2,1)} %get-tuple-element.151.other), custom_call_target="tpu_custom_call" | custom-call | flops 1 | bytes 1 | tf_op jit(solution)/shard_map/output_grad/pallas_call | solution.py:52
  284.4 6.8 %fusion.39 = f32[704,2048]{1,0:T(8,128)} fusion(bf16[640,704]{0,1:T(8,128)(2,1)} %get-tuple-element.153, bf16[320,2048]{1,0:T(8,128)(2,1)} %copy-done.86, bf16[160,2048]{1,0:T(8,128)(2,1)} %collective-permute-done.24, bf16[80,2048]{1,0:T(8,128)(2,1)} %copy-done.20, bf16[80,2048]{1,0:T(8,128)(2,1)S(1)} %copy-done.10), kind=kOutput, calls=%fused_computation.73 | convolution fusion | flops 1855979520 | bytes 9289728 | tf_op jit(solution)/shard_map/dot_general | solution.py:22
  291.2 5.9 %collective-permute-done.46.refs_1_ = bf16[2,128,512]{2,1,0:T(8,128)(2,1)} collective-permute-done((bf16[2,128,512]{2,1,0:T(8,128)(2,1)}, bf16[2,128,512]{2,1,0:T(8,128)(2,1)}, u32[]{:S(2)}, u32[]{:S(2)}) %collective-permute-start.46) | collective-permute-done | bytes 262176 | tf_op jit(solution)/shard_map/ppermute | solution.py:519
  297.1 5.1 %attention_back.1 = (bf16[4,128,512]{2,1,0:T(8,128)(2,1)}, f32[8,128]{1,0:T(8,128)}) custom-call(s32[4]{0:T(128)} %pad_add_fusion.at, f32[2,128,512]{2,1,0:T(8,128)} %get-tuple-element.154.own, bf16[2,128,512]{2,1,0:T(8,128)(2,1)} %copy-done.38, bf16[2,128,512]{2,1,0:T(8,128)(2,1)} %collective-permute-done.46.refs_1_, ...), custom_call_target="tpu_custom_call" | custom-call | flops 1 | bytes 1 | tf_op jit(solution)/shard_map/attention_back/pallas_call | solution.py:52
  309.1 4.8 %collective-permute-start.49 = (bf16[4,128,512]{2,1,0:T(8,128)(2,1)S(1)}, bf16[4,128,512]{2,1,0:T(8,128)(2,1)S(1)}, u32[]{:S(2)}, u32[]{:S(2)}) collective-permute-start(bf16[4,128,512]{2,1,0:T(8,128)(2,1)S(1)} %copy-done.14), channel_id=1, source_target_pairs={{0,16},{4,20},{8,24},{12,28},{16,0},{20,4},{24,8},{28,12},{1,17},{... | collective-permute-start | bytes 1572872 | tf_op jit(solution)/shard_map/ppermute | solution.py:519
  318.0 7.6 %fusion.13 = f32[2048,2,704]{0,2,1:T(8,128)} fusion(bf16[640,2,704]{0,2,1:T(8,128)(2,1)S(1)} %copy-done.17, bf16[640,2176]{1,0:T(8,128)(2,1)S(1)} %copy-done.9), kind=kOutput, calls=%fused_computation.19 | convolution fusion | flops 3690987520 | bytes 15958016 | tf_op jit(solution)/shard_map/rd,rkf->dkf/dot_general | solution.py:879
  325.6 24.9 %collective-permute-done.49.refs_2_ = bf16[4,128,512]{2,1,0:T(8,128)(2,1)S(1)} collective-permute-done((bf16[4,128,512]{2,1,0:T(8,128)(2,1)S(1)}, bf16[4,128,512]{2,1,0:T(8,128)(2,1)S(1)}, u32[]{:S(2)}, u32[]{:S(2)}) %collective-permute-start.49) | collective-permute-done | bytes 524320 | tf_op jit(solution)/shard_map/ppermute | solution.py:519
  351.4 5.3 %query_grad.1 = (bf16[4,512,512]{2,1,0:T(8,128)(2,1)}, f32[4,256,512]{2,1,0:T(8,128)}, bf16[4,256,512]{2,1,0:T(8,128)(2,1)}) custom-call(s32[4]{0:T(128)} %pad_add_fusion.at, bf16[512,512]{1,0:T(8,128)(2,1)} %get-tuple-element.109.refs_0_.rows, f32[512,8]{1,0:T(8,128)} %get-tuple-element.110.refs_1_.refs_4_.hot, ...), custom_call_target="tpu_custom_call" | custom-call | flops 1 | bytes 1 | tf_op jit(solution)/shard_map/query_grad/pallas_call | solution.py:52
  356.7 6.2 %input.1 = (bf16[2,512,512]{2,1,0:T(8,128)(2,1)}, f32[1,512]{1,0:T(1,128)}, f32[128,512]{1,0:T(8,128)}, f32[128,512]{1,0:T(8,128)}, bf16[2,128,512]{2,1,0:T(8,128)(2,1)}) custom-call(s32[4]{0:T(128)} %pad_add_fusion.at, bf16[4,128,512]{2,1,0:T(8,128)(2,1)} %get-tuple-element.169.refs_0_, bf16[4,128,512]{2,1,0:T(8,128)(2,1)} %copy-done.16, ...), custom_call_target="tpu_custom_call" | custom-call | flops 1879048192 | bytes 1 | tf_op jit(solution)/shard_map/input/pallas_call | solution.py:52
  401.2 9.6 %collective-permute-done.67 = f32[10,512]{1,0:T(8,128)S(1)} collective-permute-done((f32[10,512]{1,0:T(8,128)S(1)}, f32[10,512]{1,0:T(8,128)S(1)}, u32[]{:S(2)}, u32[]{:S(2)}) %collective-permute-start.67) | collective-permute-done | bytes 20512 | tf_op jit(solution)/shard_map/ppermute | solution.py:522
  414.5 5.7 %collective-permute-start.59 = (bf16[128,512]{1,0:T(8,128)(2,1)S(1)}, bf16[128,512]{1,0:T(8,128)(2,1)S(1)}, u32[]{:S(2)}, u32[]{:S(2)}) collective-permute-start(bf16[128,512]{1,0:T(8,128)(2,1)S(1)} %fusion.34), channel_id=1, source_target_pairs={{0,0},{1,8},{2,16},{3,24},{4,4},{5,12},{6,20},{7,28},{8,1},{9,9},{... | collective-permute-start | bytes 393224 | tf_op jit(solution)/shard_map/ppermute | solution.py:533
  420.8 6.9 %collective-permute-done.59 = bf16[128,512]{1,0:T(8,128)(2,1)S(1)} collective-permute-done((bf16[128,512]{1,0:T(8,128)(2,1)S(1)}, bf16[128,512]{1,0:T(8,128)(2,1)S(1)}, u32[]{:S(2)}, u32[]{:S(2)}) %collective-permute-start.59) | collective-permute-done | bytes 131104 | tf_op jit(solution)/shard_map/ppermute | solution.py:533
  (403 shorter events, 235.0 us)
Async XLA Ops:
  15.7 41.6 %collective-permute-start.9 = (bf16[4,256,512]{2,1,0:T(8,128)(2,1)}, bf16[4,256,512]{2,1,0:T(8,128)(2,1)}, u32[]{:S(2)}, u32[]{:S(2)}) collective-permute-start(bf16[4,256,512]{2,1,0:T(8,128)(2,1)} %refs_7_.3), channel_id=1, source_target_pairs={{0,4},{4,0},{8,12},{12,8},{16,20},{20,16},{24,28},{28,24},{1,5},{5... | collective-permute-start | bytes 3145736 | tf_op jit(solution)/shard_map/ppermute | solution.py:522
  32.3 22.7 %collective-permute-start.7 = (bf16[272,512]{1,0:T(8,128)(2,1)}, bf16[272,512]{1,0:T(8,128)(2,1)}, u32[]{:S(2)}, u32[]{:S(2)}) collective-permute-start(bf16[272,512]{1,0:T(8,128)(2,1)} %get-tuple-element.107), channel_id=1, source_target_pairs={{0,16},{4,20},{8,24},{12,28},{16,0},{20,4},{24,8},{28,12},{1,17},{... | collective-permute-start | bytes 835592 | tf_op jit(solution)/shard_map/ppermute | solution.py:519
  34.9 20.1 %collective-permute-start.8 = (bf16[272,512]{1,0:T(8,128)(2,1)}, bf16[272,512]{1,0:T(8,128)(2,1)}, u32[]{:S(2)}, u32[]{:S(2)}) collective-permute-start(bf16[272,512]{1,0:T(8,128)(2,1)} %get-tuple-element.108), channel_id=1, source_target_pairs={{0,24},{4,28},{8,16},{12,20},{16,8},{20,12},{24,0},{28,4},{1,25},{... | collective-permute-start | bytes 835592 | tf_op jit(solution)/shard_map/ppermute | solution.py:519
  35.4 37.2 %collective-permute-start.19 = (bf16[128,512]{1,0:T(8,128)(2,1)}, bf16[128,512]{1,0:T(8,128)(2,1)S(1)}, u32[]{:S(2)}, u32[]{:S(2)}) collective-permute-start(bf16[128,512]{1,0:T(8,128)(2,1)} %param.15), channel_id=1, source_target_pairs={{0,0},{1,8},{2,16},{3,24},{4,4},{5,12},{6,20},{7,28},{8,1},{9,9},{... | collective-permute-start | bytes 393224 | tf_op jit(solution)/shard_map/ppermute | solution.py:533
  57.2 72.8 %collective-permute-start.16 = (bf16[4,256,512]{2,1,0:T(8,128)(2,1)}, bf16[4,256,512]{2,1,0:T(8,128)(2,1)}, u32[]{:S(2)}, u32[]{:S(2)}) collective-permute-start(bf16[4,256,512]{2,1,0:T(8,128)(2,1)} %refs_5_.4), channel_id=1, source_target_pairs={{0,4},{4,0},{8,12},{12,8},{16,20},{20,16},{24,28},{28,24},{1,5},{5... | collective-permute-start | bytes 3145736 | tf_op jit(solution)/shard_map/ppermute | solution.py:522
  62.2 17.6 %collective-permute-start.10 = (bf16[2,128,512]{2,1,0:T(8,128)(2,1)}, bf16[2,128,512]{2,1,0:T(8,128)(2,1)S(1)}, u32[]{:S(2)}, u32[]{:S(2)}) collective-permute-start(bf16[2,128,512]{2,1,0:T(8,128)(2,1)} %get-tuple-element.113), channel_id=1, source_target_pairs={{0,8},{4,12},{8,0},{12,4},{16,24},{20,28},{24,16},{28,20},{1,9},{5... | collective-permute-start | bytes 786440 | tf_op jit(solution)/shard_map/ppermute | solution.py:519
  70.7 25.1 %collective-permute-start.11 = (bf16[2,128,512]{2,1,0:T(8,128)(2,1)}, bf16[2,128,512]{2,1,0:T(8,128)(2,1)}, u32[]{:S(2)}, u32[]{:S(2)}) collective-permute-start(bf16[2,128,512]{2,1,0:T(8,128)(2,1)} %get-tuple-element.114), channel_id=1, source_target_pairs={{0,16},{4,20},{8,24},{12,28},{16,0},{20,4},{24,8},{28,12},{1,17},{... | collective-permute-start | bytes 786440 | tf_op jit(solution)/shard_map/ppermute | solution.py:519
  72.8 23.0 %collective-permute-start.12 = (bf16[2,128,512]{2,1,0:T(8,128)(2,1)}, bf16[2,128,512]{2,1,0:T(8,128)(2,1)S(1)}, u32[]{:S(2)}, u32[]{:S(2)}) collective-permute-start(bf16[2,128,512]{2,1,0:T(8,128)(2,1)} %get-tuple-element.115), channel_id=1, source_target_pairs={{0,24},{4,28},{8,16},{12,20},{16,8},{20,12},{24,0},{28,4},{1,25},{... | collective-permute-start | bytes 786440 | tf_op jit(solution)/shard_map/ppermute | solution.py:519
  75.1 26.9 %collective-permute-start.22 = (bf16[80,512]{1,0:T(8,128)(2,1)}, bf16[80,512]{1,0:T(8,128)(2,1)}, u32[]{:S(2)}, u32[]{:S(2)}) collective-permute-start(bf16[80,512]{1,0:T(8,128)(2,1)} %get-tuple-element.217), channel_id=1, source_target_pairs={{0,24},{4,28},{8,16},{12,20},{16,8},{20,12},{24,0},{28,4},{1,25},{... | collective-permute-start | bytes 245768 | tf_op jit(solution)/shard_map/ppermute | solution.py:519
  79.8 22.2 %collective-permute-start.21 = (bf16[80,512]{1,0:T(8,128)(2,1)}, bf16[80,512]{1,0:T(8,128)(2,1)}, u32[]{:S(2)}, u32[]{:S(2)}) collective-permute-start(bf16[80,512]{1,0:T(8,128)(2,1)} %get-tuple-element.218), channel_id=1, source_target_pairs={{0,16},{4,20},{8,24},{12,28},{16,0},{20,4},{24,8},{28,12},{1,17},{... | collective-permute-start | bytes 245768 | tf_op jit(solution)/shard_map/ppermute | solution.py:519
  108.8 21.3 %collective-permute-start.14 = (bf16[2,128,512]{2,1,0:T(8,128)(2,1)}, bf16[2,128,512]{2,1,0:T(8,128)(2,1)S(1)}, u32[]{:S(2)}, u32[]{:S(2)}) collective-permute-start(bf16[2,128,512]{2,1,0:T(8,128)(2,1)} %get-tuple-element.118.refs_0_), channel_id=1, source_target_pairs={{0,16},{4,20},{8,24},{12,28},{16,0},{20,4},{24,8},{28,12},{1,17},{... | collective-permute-start | bytes 786440 | tf_op jit(solution)/shard_map/ppermute | solution.py:519
  112.2 17.9 %collective-permute-start.13 = (bf16[2,128,512]{2,1,0:T(8,128)(2,1)}, bf16[2,128,512]{2,1,0:T(8,128)(2,1)}, u32[]{:S(2)}, u32[]{:S(2)}) collective-permute-start(bf16[2,128,512]{2,1,0:T(8,128)(2,1)} %get-tuple-element.118.refs_0_), channel_id=1, source_target_pairs={{0,8},{4,12},{8,0},{12,4},{16,24},{20,28},{24,16},{28,20},{1,9},{5... | collective-permute-start | bytes 786440 | tf_op jit(solution)/shard_map/ppermute | solution.py:519
  115.4 24.0 %collective-permute-start.24 = (bf16[160,2048]{1,0:T(8,128)(2,1)}, bf16[160,2048]{1,0:T(8,128)(2,1)}, u32[]{:S(2)}, u32[]{:S(2)}) collective-permute-start(bf16[160,2048]{1,0:T(8,128)(2,1)} %pad_maximum_fusion.7), channel_id=1, source_target_pairs={{0,2},{1,5},{2,0},{3,7},{4,6},{5,1},{6,4},{7,3},{8,10},{9,13},{10,... | collective-permute-start | bytes 1966088 | tf_op jit(solution)/shard_map/ppermute | solution.py:541
  265.5 39.2 %collective-permute-start.34 = (bf16[160,2048]{1,0:T(8,128)(2,1)}, bf16[160,2048]{1,0:T(8,128)(2,1)}, u32[]{:S(2)}, u32[]{:S(2)}) collective-permute-start(bf16[160,2048]{1,0:T(8,128)(2,1)} %slice.399), channel_id=1, source_target_pairs={{0,2},{1,5},{2,0},{3,7},{4,6},{5,1},{6,4},{7,3},{8,10},{9,13},{10,... | collective-permute-start | bytes 1966088 | tf_op jit(solution)/shard_map/ppermute | solution.py:541
  273.7 17.4 %collective-permute-start.45 = (bf16[2,128,512]{2,1,0:T(8,128)(2,1)}, bf16[2,128,512]{2,1,0:T(8,128)(2,1)S(1)}, u32[]{:S(2)}, u32[]{:S(2)}) collective-permute-start(bf16[2,128,512]{2,1,0:T(8,128)(2,1)} %get-tuple-element.147), channel_id=1, source_target_pairs={{0,8},{4,12},{8,0},{12,4},{16,24},{20,28},{24,16},{28,20},{1,9},{5... | collective-permute-start | bytes 786440 | tf_op jit(solution)/shard_map/ppermute | solution.py:519
  275.4 21.7 %collective-permute-start.46 = (bf16[2,128,512]{2,1,0:T(8,128)(2,1)}, bf16[2,128,512]{2,1,0:T(8,128)(2,1)}, u32[]{:S(2)}, u32[]{:S(2)}) collective-permute-start(bf16[2,128,512]{2,1,0:T(8,128)(2,1)} %get-tuple-element.148), channel_id=1, source_target_pairs={{0,16},{4,20},{8,24},{12,28},{16,0},{20,4},{24,8},{28,12},{1,17},{... | collective-permute-start | bytes 786440 | tf_op jit(solution)/shard_map/ppermute | solution.py:519
  277.4 19.7 %collective-permute-start.47 = (bf16[2,128,512]{2,1,0:T(8,128)(2,1)}, bf16[2,128,512]{2,1,0:T(8,128)(2,1)}, u32[]{:S(2)}, u32[]{:S(2)}) collective-permute-start(bf16[2,128,512]{2,1,0:T(8,128)(2,1)} %get-tuple-element.149), channel_id=1, source_target_pairs={{0,24},{4,28},{8,16},{12,20},{16,8},{20,12},{24,0},{28,4},{1,25},{... | collective-permute-start | bytes 786440 | tf_op jit(solution)/shard_map/ppermute | solution.py:519
  282.9 67.6 %collective-permute-start.51 = (bf16[4,256,512]{2,1,0:T(8,128)(2,1)}, bf16[4,256,512]{2,1,0:T(8,128)(2,1)}, u32[]{:S(2)}, u32[]{:S(2)}) collective-permute-start(bf16[4,256,512]{2,1,0:T(8,128)(2,1)} %get-tuple-element.152), channel_id=1, source_target_pairs={{0,4},{4,0},{8,12},{12,8},{16,20},{20,16},{24,28},{28,24},{1,5},{5... | collective-permute-start | bytes 3145736 | tf_op jit(solution)/shard_map/ppermute | solution.py:522
  307.6 65.5 %collective-permute-start.52 = (bf16[80,2048]{1,0:T(8,128)(2,1)}, bf16[80,2048]{1,0:T(8,128)(2,1)}, u32[]{:S(2)}, u32[]{:S(2)}) collective-permute-start(bf16[80,2048]{1,0:T(8,128)(2,1)} %slice.401), channel_id=1, source_target_pairs={{0,4},{1,3},{2,6},{3,1},{4,0},{5,7},{6,2},{7,5},{8,12},{9,11},{10,... | collective-permute-start | bytes 983048 | tf_op jit(solution)/shard_map/ppermute | solution.py:541
  309.1 41.4 %collective-permute-start.49 = (bf16[4,128,512]{2,1,0:T(8,128)(2,1)S(1)}, bf16[4,128,512]{2,1,0:T(8,128)(2,1)S(1)}, u32[]{:S(2)}, u32[]{:S(2)}) collective-permute-start(bf16[4,128,512]{2,1,0:T(8,128)(2,1)S(1)} %copy-done.14), channel_id=1, source_target_pairs={{0,16},{4,20},{8,24},{12,28},{16,0},{20,4},{24,8},{28,12},{1,17},{... | collective-permute-start | bytes 1572872 | tf_op jit(solution)/shard_map/ppermute | solution.py:519
  313.8 36.6 %collective-permute-start.48 = (bf16[4,128,512]{2,1,0:T(8,128)(2,1)S(1)}, bf16[4,128,512]{2,1,0:T(8,128)(2,1)S(1)}, u32[]{:S(2)}, u32[]{:S(2)}) collective-permute-start(bf16[4,128,512]{2,1,0:T(8,128)(2,1)S(1)} %copy-done.14), channel_id=1, source_target_pairs={{0,8},{4,12},{8,0},{12,4},{16,24},{20,28},{24,16},{28,20},{1,9},{5... | collective-permute-start | bytes 1572872 | tf_op jit(solution)/shard_map/ppermute | solution.py:519
  365.1 25.1 %collective-permute-start.57 = (bf16[4,256,512]{2,1,0:T(8,128)(2,1)}, bf16[4,256,512]{2,1,0:T(8,128)(2,1)}, u32[]{:S(2)}, u32[]{:S(2)}) collective-permute-start(bf16[4,256,512]{2,1,0:T(8,128)(2,1)} %get-tuple-element.168), channel_id=1, source_target_pairs={{0,4},{4,0},{8,12},{12,8},{16,20},{20,16},{24,28},{28,24},{1,5},{5... | collective-permute-start | bytes 3145736 | tf_op jit(solution)/shard_map/ppermute | solution.py:522
  378.1 17.2 %collective-permute-start.56 = (bf16[2,128,512]{2,1,0:T(8,128)(2,1)}, bf16[2,128,512]{2,1,0:T(8,128)(2,1)S(1)}, u32[]{:S(2)}, u32[]{:S(2)}) collective-permute-start(bf16[2,128,512]{2,1,0:T(8,128)(2,1)} %get-tuple-element.181), channel_id=1, source_target_pairs={{0,1},{1,0},{2,3},{3,2},{4,5},{5,4},{6,7},{7,6},{8,9},{9,8},{10,11... | collective-permute-start | bytes 786440 | tf_op jit(solution)/shard_map/ppermute | solution.py:525
  395.5 34.0 %collective-permute-start.68 = (bf16[2,256,512]{2,1,0:T(8,128)(2,1)}, bf16[2,256,512]{2,1,0:T(8,128)(2,1)S(1)}, u32[]{:S(2)}, u32[]{:S(2)}) collective-permute-start(bf16[2,256,512]{2,1,0:T(8,128)(2,1)} %get-tuple-element.196), channel_id=1, source_target_pairs={{0,4},{4,0},{8,12},{12,8},{16,20},{20,16},{24,28},{28,24},{1,5},{5... | collective-permute-start | bytes 1572872 | tf_op jit(solution)/shard_map/ppermute | solution.py:522
  (134 other events, 1528.7 us)

commit v7 on v3

--- a/solution.py
+++ b/solution.py
@@ -47,7 +47,7 @@
     return jax.ShapeDtypeStruct(tuple(dims), dtype)
 
 
-def run(name, body, outs, args, scratch=()):
+def run(name, body, outs, args, scratch=(), flops=1):
     vector = pl.BlockSpec(memory_space=pltpu.VMEM)
     return pl.pallas_call(
         body,
@@ -55,7 +55,7 @@
         in_specs=[pl.BlockSpec(memory_space=pltpu.SMEM)] + [vector] * (len(args) - 1),
         out_specs=tuple(vector for _ in outs),
         scratch_shapes=list(scratch),
-        cost_estimate=pl.CostEstimate(flops=1, transcendentals=0, bytes_accessed=1),
+        cost_estimate=pl.CostEstimate(flops=flops, transcendentals=0, bytes_accessed=1),
         name=name,
     )(*args)
 
@@ -898,6 +898,7 @@
             *all_streams,
         ],
         [pltpu.VMEM((2 + E, slice_width, local_width), BF16)],
+        flops=14 * rows_all * slice_width * local_width,
     )
     home_rows = swap(after(near, own_stats))
     gain_one_home = home_rows[0].astype(F32)
@@ -910,7 +911,7 @@
     dlogit_scaled = dlogit_one * scale_one
     router_term = swap(dot(dlogit_scaled, gained_home, ((1,), (0,)), PRECISE))
     kv_grad_parts = run(
-        "key_value_grad", weight_grad_body, weight_parts(2), [at, gained, dkv_all], weight_scratch
+        "key_value_grad", weight_grad_body, weight_parts(2), [at, gained, dkv_all], weight_scratch, 14 * rows_all * slice_width * local_width
     )
     kv_grad, kv_got = weight_sum(after(kv_grad_parts, query_got))
     keep, got, other = after(reduce_narrow(*dnormed_one), kv_grad_parts[-1], query_got)

time: 425 us -> 423 us (level)
  no operation moved by 1% of the time
where the time goes in v7:
time: 423 us; the launch traced here: 419 us
  waiting for transfers between devices  166 us (39%)
  starting transfers between devices  97 us (23%)
  Pallas kernels  61.8 us (15%)
  matrix products  45.7 us (11%)
  other arithmetic  32.8 us (8%)
  local copies, waits for them, and re-layouts  14.6 us (3%)
    ppermute x29, waiting for transfers between devices, by_plane(): lax.ppermute(values, 'wide', [(i, i ^ k * subs) for i in range(wide_count)])  99 us
    pallas_call x16, Pallas kernels, run(): pl.pallas_call(body, out_shape=tuple(outs), in_specs=[pl.BlockSpec(memory...  61.8 us
    ppermute x29, starting transfers between devices, by_plane(): lax.ppermute(values, 'wide', [(i, i ^ k * subs) for i in range(wide_count)])  54.4 us
    ppermute x8, waiting for transfers between devices, by_side(): return lax.ppermute(values, ('wide', 'narrow'), pairs)  24.2 us
    ppermute x18, waiting for transfers between devices, by_narrow(): lax.ppermute(values, 'narrow', [(i, i ^ k) for i in range(narrow_count)])  21.6 us
    ppermute x6, starting transfers between devices, swap(): return lax.ppermute(values, ('wide', 'narrow'), pairs)  21.2 us
    dot_general x7, matrix products, dot(): lax.dot_general(left, right, ((contract[0], contract[1]), ((), ())), prec...  17.9 us
    dot_general x1, matrix products, local(): jnp.einsum('krf,dkf->rd', jnp.stack([dgate_pre, dup_pre]), weight_in, pre...  14.5 us
  transfers between devices with their start and end apart: 69, of which 35 were waited for; matrix products, arithmetic and copies ran while one was open for 14% of the time, Pallas kernels for 13%

profile of v7, /device:TPU:2, one launch (start us, length us, event | category | flops | bytes accessed | tf_op | source)
XLA Modules:
  0.0 419.3 jit_solution(2834839422256164436)
XLA Ops:
  38.2 7.6 %collective-permute-done.6.refs_1_.refs_0_ = bf16[272,512]{1,0:T(8,128)(2,1)S(1)} collective-permute-done((bf16[272,512]{1,0:T(8,128)(2,1)}, bf16[272,512]{1,0:T(8,128)(2,1)S(1)}, u32[]{:S(2)}, u32[]{:S(2)}) %collective-permute-start.6) | collective-permute-done | bytes 278560 | tf_op jit(solution)/shard_map/ppermute | solution.py:519
  45.8 8.7 %collective-permute-done.7.refs_2_.refs_1_ = bf16[272,512]{1,0:T(8,128)(2,1)} collective-permute-done((bf16[272,512]{1,0:T(8,128)(2,1)}, bf16[272,512]{1,0:T(8,128)(2,1)}, u32[]{:S(2)}, u32[]{:S(2)}) %collective-permute-start.7) | collective-permute-done | bytes 278560 | tf_op jit(solution)/shard_map/ppermute | solution.py:519
  62.2 7.9 %collective-permute-start.10 = (bf16[2,128,512]{2,1,0:T(8,128)(2,1)}, bf16[2,128,512]{2,1,0:T(8,128)(2,1)S(1)}, u32[]{:S(2)}, u32[]{:S(2)}) collective-permute-start(bf16[2,128,512]{2,1,0:T(8,128)(2,1)} %get-tuple-element.112), channel_id=1, source_target_pairs={{0,8},{4,12},{8,0},{12,4},{16,24},{20,28},{24,16},{28,20},{1,9},{5... | collective-permute-start | bytes 786440 | tf_op jit(solution)/shard_map/ppermute | solution.py:519
  81.4 13.8 %collective-permute-done.11.refs_5_ = bf16[2,128,512]{2,1,0:T(8,128)(2,1)} collective-permute-done((bf16[2,128,512]{2,1,0:T(8,128)(2,1)}, bf16[2,128,512]{2,1,0:T(8,128)(2,1)}, u32[]{:S(2)}, u32[]{:S(2)}) %collective-permute-start.11) | collective-permute-done | bytes 262176 | tf_op jit(solution)/shard_map/ppermute | solution.py:519
  96.0 5.4 %attention.1 = (f32[16,128]{1,0:T(8,128)}, bf16[4,128,512]{2,1,0:T(8,128)(2,1)}, f32[4,256,128]{2,1,0:T(8,128)}, bf16[2,128,512]{2,1,0:T(8,128)(2,1)}, bf16[2,128,512]{2,1,0:T(8,128)(2,1)}) custom-call(s32[4]{0:T(128)} %bitcast.189, f32[2,128,512]{2,1,0:T(8,128)} %get-tuple-element.104.own_kv, bf16[272,512]{1,0:T(8,128)(2,1)} %copy-done.25, ...), custom_call_target="tpu_custom_call" | custom-call | flops 1 | bytes 1 | tf_op jit(solution)/shard_map/attention/pallas_call | solution.py:52
  116.2 14.2 %collective-permute-done.14.refs_2_ = bf16[2,128,512]{2,1,0:T(8,128)(2,1)} collective-permute-done((bf16[2,128,512]{2,1,0:T(8,128)(2,1)}, bf16[2,128,512]{2,1,0:T(8,128)(2,1)}, u32[]{:S(2)}, u32[]{:S(2)}) %collective-permute-start.14) | collective-permute-done | bytes 262176 | tf_op jit(solution)/shard_map/ppermute | solution.py:519
  152.9 5.3 %collective-permute-done.26.refs_2_ = bf16[80,640]{1,0:T(8,128)(2,1)} collective-permute-done((bf16[80,640]{1,0:T(8,128)(2,1)}, bf16[80,640]{1,0:T(8,128)(2,1)}, u32[]{:S(2)}, u32[]{:S(2)}) %collective-permute-start.26) | collective-permute-done | bytes 102432 | tf_op jit(solution)/shard_map/ppermute | solution.py:519
  161.5 6.9 %collective-permute-done.28 = bf16[80,2176]{1,0:T(8,128)(2,1)S(1)} collective-permute-done((bf16[80,2176]{1,0:T(8,128)(2,1)}, bf16[80,2176]{1,0:T(8,128)(2,1)S(1)}, u32[]{:S(2)}, u32[]{:S(2)}) %collective-permute-start.28) | collective-permute-done | bytes 348192 | tf_op jit(solution)/shard_map/ppermute | solution.py:541
  171.4 9.1 %collective-permute-done.29 = bf16[160,2176]{1,0:T(8,128)(2,1)S(1)} collective-permute-done((bf16[160,2176]{1,0:T(8,128)(2,1)S(1)}, bf16[160,2176]{1,0:T(8,128)(2,1)S(1)}, u32[]{:S(2)}, u32[]{:S(2)}) %collective-permute-start.29) | collective-permute-done | bytes 696352 | tf_op jit(solution)/shard_map/ppermute | solution.py:541
  193.8 4.8 %fusion.18 = f32[2,640,704]{1,2,0:T(8,128)S(1)} fusion(bf16[1,2048,2,704]{1,3,2,0:T(8,128)(2,1)S(1)} %bitcast.191, bf16[640,2176]{1,0:T(8,128)(2,1)S(1)} %pad_maximum_fusion.1), kind=kOutput, calls=%fused_computation.32 | convolution fusion | flops 3690987520 | bytes 11993088 | tf_op jit(solution)/shard_map/rd,dkf->krf/dot_general | solution.py:757
  202.4 14.5 %fusion.4 = f32[640,2048]{1,0:T(8,128)S(1)} fusion(bf16[1,2048,2,704]{1,3,2,0:T(8,128)(2,1)S(1)} %bitcast.191, bf16[1,640,704]{1,2,0:T(8,128)(2,1)S(1)} %bitcast.159, bf16[1,640,704]{1,2,0:T(8,128)(2,1)S(1)} %bitcast.160), kind=kOutput, calls=%fused_computation.7 | convolution fusion | flops 3691888640 | bytes 12812288 | tf_op jit(solution)/shard_map/krf,dkf->rd/dot_general | solution.py:768
  238.4 5.8 %collective-permute-done.38.got = bf16[80,2176]{1,0:T(8,128)(2,1)} collective-permute-done((bf16[80,2176]{1,0:T(8,128)(2,1)S(1)}, bf16[80,2176]{1,0:T(8,128)(2,1)}, u32[]{:S(2)}, u32[]{:S(2)}) %collective-permute-start.38) | collective-permute-done | bytes 348192 | tf_op jit(solution)/shard_map/ppermute | solution.py:541
  274.9 4.8 %output_grad.1 = (f32[4,256,512]{2,1,0:T(8,128)}, bf16[4,256,512]{2,1,0:T(8,128)(2,1)}) custom-call(s32[4]{0:T(128)} %pad_add_fusion.at, bf16[512,512]{1,0:T(8,128)(2,1)} %get-tuple-element.149.rows, bf16[4,512,512]{2,1,0:T(8,128)(2,1)} %get-tuple-element.150.other), custom_call_target="tpu_custom_call" | custom-call | flops 1 | bytes 1 | tf_op jit(solution)/shard_map/output_grad/pallas_call | solution.py:52
  280.7 6.8 %fusion.39 = f32[704,2048]{1,0:T(8,128)} fusion(bf16[640,704]{0,1:T(8,128)(2,1)} %get-tuple-element.152, bf16[320,2048]{1,0:T(8,128)(2,1)} %copy-done.60, bf16[160,2048]{1,0:T(8,128)(2,1)} %collective-permute-done.24, bf16[80,2048]{1,0:T(8,128)(2,1)} %copy-done.20, bf16[80,2048]{1,0:T(8,128)(2,1)S(1)} %copy-done.10), kind=kOutput, calls=%fused_computation.73 | convolution fusion | flops 1855979520 | bytes 9289728 | tf_op jit(solution)/shard_map/dot_general | solution.py:22
  287.4 6.4 %collective-permute-done.46.refs_1_ = bf16[2,128,512]{2,1,0:T(8,128)(2,1)} collective-permute-done((bf16[2,128,512]{2,1,0:T(8,128)(2,1)}, bf16[2,128,512]{2,1,0:T(8,128)(2,1)}, u32[]{:S(2)}, u32[]{:S(2)}) %collective-permute-start.46) | collective-permute-done | bytes 262176 | tf_op jit(solution)/shard_map/ppermute | solution.py:519
  293.8 5.1 %attention_back.1 = (bf16[4,128,512]{2,1,0:T(8,128)(2,1)}, f32[8,128]{1,0:T(8,128)}) custom-call(s32[4]{0:T(128)} %pad_add_fusion.at, f32[2,128,512]{2,1,0:T(8,128)} %get-tuple-element.153.own, bf16[2,128,512]{2,1,0:T(8,128)(2,1)} %collective-permute-done.45.refs_0_, bf16[2,128,512]{2,1,0:T(8,128)(2,1)} %collective-permute-done.46.refs_1_, ...), custom_call_target="tpu_custom_call" | custom-call | flops 1 | bytes 1 | tf_op jit(solution)/shard_map/attention_back/pallas_call | solution.py:52
  305.3 4.8 %collective-permute-start.49 = (bf16[4,128,512]{2,1,0:T(8,128)(2,1)S(1)}, bf16[4,128,512]{2,1,0:T(8,128)(2,1)S(1)}, u32[]{:S(2)}, u32[]{:S(2)}) collective-permute-start(bf16[4,128,512]{2,1,0:T(8,128)(2,1)S(1)} %copy-done.14), channel_id=1, source_target_pairs={{0,16},{4,20},{8,24},{12,28},{16,0},{20,4},{24,8},{28,12},{1,17},{... | collective-permute-start | bytes 1572872 | tf_op jit(solution)/shard_map/ppermute | solution.py:519
  310.1 5.3 %collective-permute-done.50.refs_3_ = bf16[4,128,512]{2,1,0:T(8,128)(2,1)} collective-permute-done((bf16[4,128,512]{2,1,0:T(8,128)(2,1)}, bf16[4,128,512]{2,1,0:T(8,128)(2,1)}, u32[]{:S(2)}, u32[]{:S(2)}) %collective-permute-start.50) | collective-permute-done | bytes 524320 | tf_op jit(solution)/shard_map/ppermute | solution.py:519
  315.4 7.6 %fusion.13 = f32[2048,2,704]{0,2,1:T(8,128)} fusion(bf16[640,2,704]{0,2,1:T(8,128)(2,1)S(1)} %copy-done.17, bf16[640,2176]{1,0:T(8,128)(2,1)S(1)} %copy-done.9), kind=kOutput, calls=%fused_computation.19 | convolution fusion | flops 3690987520 | bytes 15958016 | tf_op jit(solution)/shard_map/rd,rkf->dkf/dot_general | solution.py:877
  323.0 24.2 %collective-permute-done.49.refs_2_ = bf16[4,128,512]{2,1,0:T(8,128)(2,1)S(1)} collective-permute-done((bf16[4,128,512]{2,1,0:T(8,128)(2,1)S(1)}, bf16[4,128,512]{2,1,0:T(8,128)(2,1)S(1)}, u32[]{:S(2)}, u32[]{:S(2)}) %collective-permute-start.49) | collective-permute-done | bytes 524320 | tf_op jit(solution)/shard_map/ppermute | solution.py:519
  348.2 5.3 %query_grad.1 = (bf16[4,512,512]{2,1,0:T(8,128)(2,1)}, f32[4,256,512]{2,1,0:T(8,128)}, bf16[4,256,512]{2,1,0:T(8,128)(2,1)}) custom-call(s32[4]{0:T(128)} %pad_add_fusion.at, bf16[512,512]{1,0:T(8,128)(2,1)} %get-tuple-element.108.refs_0_.rows, f32[512,8]{1,0:T(8,128)} %get-tuple-element.109.refs_1_.refs_4_.hot, ...), custom_call_target="tpu_custom_call" | custom-call | flops 1 | bytes 1 | tf_op jit(solution)/shard_map/query_grad/pallas_call | solution.py:52
  353.4 6.2 %input.1 = (bf16[2,512,512]{2,1,0:T(8,128)(2,1)}, f32[1,512]{1,0:T(1,128)}, f32[128,512]{1,0:T(8,128)}, f32[128,512]{1,0:T(8,128)}, bf16[2,128,512]{2,1,0:T(8,128)(2,1)}) custom-call(s32[4]{0:T(128)} %pad_add_fusion.at, bf16[4,128,512]{2,1,0:T(8,128)(2,1)} %get-tuple-element.168.refs_0_, bf16[4,128,512]{2,1,0:T(8,128)(2,1)} %copy-done.16, ...), custom_call_target="tpu_custom_call" | custom-call | flops 1879048192 | bytes 1 | tf_op jit(solution)/shard_map/input/pallas_call | solution.py:52
  394.2 5.1 %collective-permute-start.59 = (bf16[128,512]{1,0:T(8,128)(2,1)S(1)}, bf16[128,512]{1,0:T(8,128)(2,1)S(1)}, u32[]{:S(2)}, u32[]{:S(2)}) collective-permute-start(bf16[128,512]{1,0:T(8,128)(2,1)S(1)} %fusion.34), channel_id=1, source_target_pairs={{0,0},{1,8},{2,16},{3,24},{4,4},{5,12},{6,20},{7,28},{8,1},{9,9},{... | collective-permute-start | bytes 393224 | tf_op jit(solution)/shard_map/ppermute | solution.py:533
  402.8 5.1 %collective-permute-done.59 = bf16[128,512]{1,0:T(8,128)(2,1)S(1)} collective-permute-done((bf16[128,512]{1,0:T(8,128)(2,1)S(1)}, bf16[128,512]{1,0:T(8,128)(2,1)S(1)}, u32[]{:S(2)}, u32[]{:S(2)}) %collective-permute-start.59) | collective-permute-done | bytes 131104 | tf_op jit(solution)/shard_map/ppermute | solution.py:533
  (355 shorter events, 226.7 us)
Async XLA Ops:
  15.7 41.0 %collective-permute-start.9 = (bf16[4,256,512]{2,1,0:T(8,128)(2,1)}, bf16[4,256,512]{2,1,0:T(8,128)(2,1)}, u32[]{:S(2)}, u32[]{:S(2)}) collective-permute-start(bf16[4,256,512]{2,1,0:T(8,128)(2,1)} %refs_7_.3), channel_id=1, source_target_pairs={{0,4},{4,0},{8,12},{12,8},{16,20},{20,16},{24,28},{28,24},{1,5},{5... | collective-permute-start | bytes 3145736 | tf_op jit(solution)/shard_map/ppermute | solution.py:522
  31.8 22.7 %collective-permute-start.7 = (bf16[272,512]{1,0:T(8,128)(2,1)}, bf16[272,512]{1,0:T(8,128)(2,1)}, u32[]{:S(2)}, u32[]{:S(2)}) collective-permute-start(bf16[272,512]{1,0:T(8,128)(2,1)} %get-tuple-element.106), channel_id=1, source_target_pairs={{0,16},{4,20},{8,24},{12,28},{16,0},{20,4},{24,8},{28,12},{1,17},{... | collective-permute-start | bytes 835592 | tf_op jit(solution)/shard_map/ppermute | solution.py:519
  34.4 20.1 %collective-permute-start.8 = (bf16[272,512]{1,0:T(8,128)(2,1)}, bf16[272,512]{1,0:T(8,128)(2,1)}, u32[]{:S(2)}, u32[]{:S(2)}) collective-permute-start(bf16[272,512]{1,0:T(8,128)(2,1)} %get-tuple-element.107), channel_id=1, source_target_pairs={{0,24},{4,28},{8,16},{12,20},{16,8},{20,12},{24,0},{28,4},{1,25},{... | collective-permute-start | bytes 835592 | tf_op jit(solution)/shard_map/ppermute | solution.py:519
  35.3 36.7 %collective-permute-start.19 = (bf16[128,512]{1,0:T(8,128)(2,1)}, bf16[128,512]{1,0:T(8,128)(2,1)S(1)}, u32[]{:S(2)}, u32[]{:S(2)}) collective-permute-start(bf16[128,512]{1,0:T(8,128)(2,1)} %param.15), channel_id=1, source_target_pairs={{0,0},{1,8},{2,16},{3,24},{4,4},{5,12},{6,20},{7,28},{8,1},{9,9},{... | collective-permute-start | bytes 393224 | tf_op jit(solution)/shard_map/ppermute | solution.py:533
  56.7 73.7 %collective-permute-start.16 = (bf16[4,256,512]{2,1,0:T(8,128)(2,1)}, bf16[4,256,512]{2,1,0:T(8,128)(2,1)}, u32[]{:S(2)}, u32[]{:S(2)}) collective-permute-start(bf16[4,256,512]{2,1,0:T(8,128)(2,1)} %refs_5_.4), channel_id=1, source_target_pairs={{0,4},{4,0},{8,12},{12,8},{16,20},{20,16},{24,28},{28,24},{1,5},{5... | collective-permute-start | bytes 3145736 | tf_op jit(solution)/shard_map/ppermute | solution.py:522
  70.1 25.1 %collective-permute-start.11 = (bf16[2,128,512]{2,1,0:T(8,128)(2,1)}, bf16[2,128,512]{2,1,0:T(8,128)(2,1)}, u32[]{:S(2)}, u32[]{:S(2)}) collective-permute-start(bf16[2,128,512]{2,1,0:T(8,128)(2,1)} %get-tuple-element.113), channel_id=1, source_target_pairs={{0,16},{4,20},{8,24},{12,28},{16,0},{20,4},{24,8},{28,12},{1,17},{... | collective-permute-start | bytes 786440 | tf_op jit(solution)/shard_map/ppermute | solution.py:519
  72.3 23.0 %collective-permute-start.12 = (bf16[2,128,512]{2,1,0:T(8,128)(2,1)}, bf16[2,128,512]{2,1,0:T(8,128)(2,1)S(1)}, u32[]{:S(2)}, u32[]{:S(2)}) collective-permute-start(bf16[2,128,512]{2,1,0:T(8,128)(2,1)} %get-tuple-element.114), channel_id=1, source_target_pairs={{0,24},{4,28},{8,16},{12,20},{16,8},{20,12},{24,0},{28,4},{1,25},{... | collective-permute-start | bytes 786440 | tf_op jit(solution)/shard_map/ppermute | solution.py:519
  74.6 26.9 %collective-permute-start.22 = (bf16[80,512]{1,0:T(8,128)(2,1)}, bf16[80,512]{1,0:T(8,128)(2,1)}, u32[]{:S(2)}, u32[]{:S(2)}) collective-permute-start(bf16[80,512]{1,0:T(8,128)(2,1)} %get-tuple-element.215), channel_id=1, source_target_pairs={{0,24},{4,28},{8,16},{12,20},{16,8},{20,12},{24,0},{28,4},{1,25},{... | collective-permute-start | bytes 245768 | tf_op jit(solution)/shard_map/ppermute | solution.py:519
  79.3 22.2 %collective-permute-start.21 = (bf16[80,512]{1,0:T(8,128)(2,1)}, bf16[80,512]{1,0:T(8,128)(2,1)}, u32[]{:S(2)}, u32[]{:S(2)}) collective-permute-start(bf16[80,512]{1,0:T(8,128)(2,1)} %get-tuple-element.216), channel_id=1, source_target_pairs={{0,16},{4,20},{8,24},{12,28},{16,0},{20,4},{24,8},{28,12},{1,17},{... | collective-permute-start | bytes 245768 | tf_op jit(solution)/shard_map/ppermute | solution.py:519
  108.3 22.1 %collective-permute-start.14 = (bf16[2,128,512]{2,1,0:T(8,128)(2,1)}, bf16[2,128,512]{2,1,0:T(8,128)(2,1)}, u32[]{:S(2)}, u32[]{:S(2)}) collective-permute-start(bf16[2,128,512]{2,1,0:T(8,128)(2,1)} %get-tuple-element.117.refs_0_), channel_id=1, source_target_pairs={{0,16},{4,20},{8,24},{12,28},{16,0},{20,4},{24,8},{28,12},{1,17},{... | collective-permute-start | bytes 786440 | tf_op jit(solution)/shard_map/ppermute | solution.py:519
  111.7 18.7 %collective-permute-start.13 = (bf16[2,128,512]{2,1,0:T(8,128)(2,1)}, bf16[2,128,512]{2,1,0:T(8,128)(2,1)}, u32[]{:S(2)}, u32[]{:S(2)}) collective-permute-start(bf16[2,128,512]{2,1,0:T(8,128)(2,1)} %get-tuple-element.117.refs_0_), channel_id=1, source_target_pairs={{0,8},{4,12},{8,0},{12,4},{16,24},{20,28},{24,16},{28,20},{1,9},{5... | collective-permute-start | bytes 786440 | tf_op jit(solution)/shard_map/ppermute | solution.py:519
  114.2 25.2 %collective-permute-start.24 = (bf16[160,2048]{1,0:T(8,128)(2,1)}, bf16[160,2048]{1,0:T(8,128)(2,1)}, u32[]{:S(2)}, u32[]{:S(2)}) collective-permute-start(bf16[160,2048]{1,0:T(8,128)(2,1)} %pad_maximum_fusion.7), channel_id=1, source_target_pairs={{0,2},{1,5},{2,0},{3,7},{4,6},{5,1},{6,4},{7,3},{8,10},{9,13},{10,... | collective-permute-start | bytes 1966088 | tf_op jit(solution)/shard_map/ppermute | solution.py:541
  171.3 17.6 %collective-permute-start.35 = (bf16[320,2048]{1,0:T(8,128)(2,1)S(1)}, bf16[320,2048]{1,0:T(8,128)(2,1)S(1)}, u32[]{:S(2)}, u32[]{:S(2)}) collective-permute-start(bf16[320,2048]{1,0:T(8,128)(2,1)S(1)} %pad_maximum_fusion.5), channel_id=1, source_target_pairs={{0,1},{1,0},{2,3},{3,2},{4,5},{5,4},{6,7},{7,6},{8,9},{9,8},{10,11... | collective-permute-start | bytes 3932168 | tf_op jit(solution)/shard_map/ppermute | solution.py:525
  261.3 39.4 %collective-permute-start.34 = (bf16[160,2048]{1,0:T(8,128)(2,1)}, bf16[160,2048]{1,0:T(8,128)(2,1)}, u32[]{:S(2)}, u32[]{:S(2)}) collective-permute-start(bf16[160,2048]{1,0:T(8,128)(2,1)} %slice.402), channel_id=1, source_target_pairs={{0,2},{1,5},{2,0},{3,7},{4,6},{5,1},{6,4},{7,3},{8,10},{9,13},{10,... | collective-permute-start | bytes 1966088 | tf_op jit(solution)/shard_map/ppermute | solution.py:541
  272.2 21.7 %collective-permute-start.46 = (bf16[2,128,512]{2,1,0:T(8,128)(2,1)}, bf16[2,128,512]{2,1,0:T(8,128)(2,1)}, u32[]{:S(2)}, u32[]{:S(2)}) collective-permute-start(bf16[2,128,512]{2,1,0:T(8,128)(2,1)} %get-tuple-element.147), channel_id=1, source_target_pairs={{0,16},{4,20},{8,24},{12,28},{16,0},{20,4},{24,8},{28,12},{1,17},{... | collective-permute-start | bytes 786440 | tf_op jit(solution)/shard_map/ppermute | solution.py:519
  273.1 20.8 %collective-permute-start.47 = (bf16[2,128,512]{2,1,0:T(8,128)(2,1)}, bf16[2,128,512]{2,1,0:T(8,128)(2,1)}, u32[]{:S(2)}, u32[]{:S(2)}) collective-permute-start(bf16[2,128,512]{2,1,0:T(8,128)(2,1)} %get-tuple-element.148), channel_id=1, source_target_pairs={{0,24},{4,28},{8,16},{12,20},{16,8},{20,12},{24,0},{28,4},{1,25},{... | collective-permute-start | bytes 786440 | tf_op jit(solution)/shard_map/ppermute | solution.py:519
  279.7 67.5 %collective-permute-start.51 = (bf16[4,256,512]{2,1,0:T(8,128)(2,1)}, bf16[4,256,512]{2,1,0:T(8,128)(2,1)}, u32[]{:S(2)}, u32[]{:S(2)}) collective-permute-start(bf16[4,256,512]{2,1,0:T(8,128)(2,1)} %get-tuple-element.151), channel_id=1, source_target_pairs={{0,4},{4,0},{8,12},{12,8},{16,20},{20,16},{24,28},{28,24},{1,5},{5... | collective-permute-start | bytes 3145736 | tf_op jit(solution)/shard_map/ppermute | solution.py:522
  303.6 59.2 %collective-permute-start.52 = (bf16[80,2048]{1,0:T(8,128)(2,1)}, bf16[80,2048]{1,0:T(8,128)(2,1)}, u32[]{:S(2)}, u32[]{:S(2)}) collective-permute-start(bf16[80,2048]{1,0:T(8,128)(2,1)} %slice.404), channel_id=1, source_target_pairs={{0,4},{1,3},{2,6},{3,1},{4,0},{5,7},{6,2},{7,5},{8,12},{9,11},{10,... | collective-permute-start | bytes 983048 | tf_op jit(solution)/shard_map/ppermute | solution.py:541
  305.3 41.8 %collective-permute-start.49 = (bf16[4,128,512]{2,1,0:T(8,128)(2,1)S(1)}, bf16[4,128,512]{2,1,0:T(8,128)(2,1)S(1)}, u32[]{:S(2)}, u32[]{:S(2)}) collective-permute-start(bf16[4,128,512]{2,1,0:T(8,128)(2,1)S(1)} %copy-done.14), channel_id=1, source_target_pairs={{0,16},{4,20},{8,24},{12,28},{16,0},{20,4},{24,8},{28,12},{1,17},{... | collective-permute-start | bytes 1572872 | tf_op jit(solution)/shard_map/ppermute | solution.py:519
  310.1 37.1 %collective-permute-start.48 = (bf16[4,128,512]{2,1,0:T(8,128)(2,1)S(1)}, bf16[4,128,512]{2,1,0:T(8,128)(2,1)S(1)}, u32[]{:S(2)}, u32[]{:S(2)}) collective-permute-start(bf16[4,128,512]{2,1,0:T(8,128)(2,1)S(1)} %copy-done.14), channel_id=1, source_target_pairs={{0,8},{4,12},{8,0},{12,4},{16,24},{20,28},{24,16},{28,20},{1,9},{5... | collective-permute-start | bytes 1572872 | tf_op jit(solution)/shard_map/ppermute | solution.py:519
  361.1 29.1 %collective-permute-start.58 = (bf16[4,256,512]{2,1,0:T(8,128)(2,1)}, bf16[4,256,512]{2,1,0:T(8,128)(2,1)}, u32[]{:S(2)}, u32[]{:S(2)}) collective-permute-start(bf16[4,256,512]{2,1,0:T(8,128)(2,1)} %get-tuple-element.167), channel_id=1, source_target_pairs={{0,4},{4,0},{8,12},{12,8},{16,20},{20,16},{24,28},{28,24},{1,5},{5... | collective-permute-start | bytes 3145736 | tf_op jit(solution)/shard_map/ppermute | solution.py:522
  365.0 22.5 %collective-permute-start.53 = (bf16[80,512]{1,0:T(8,128)(2,1)}, bf16[80,512]{1,0:T(8,128)(2,1)}, u32[]{:S(2)}, u32[]{:S(2)}) collective-permute-start(bf16[80,512]{1,0:T(8,128)(2,1)} %get-tuple-element.176), channel_id=1, source_target_pairs={{0,8},{4,12},{8,0},{12,4},{16,24},{20,28},{24,16},{28,20},{1,9},{5... | collective-permute-start | bytes 245768 | tf_op jit(solution)/shard_map/ppermute | solution.py:519
  365.0 22.5 %collective-permute-start.54 = (bf16[80,512]{1,0:T(8,128)(2,1)}, bf16[80,512]{1,0:T(8,128)(2,1)}, u32[]{:S(2)}, u32[]{:S(2)}) collective-permute-start(bf16[80,512]{1,0:T(8,128)(2,1)} %get-tuple-element.177), channel_id=1, source_target_pairs={{0,16},{4,20},{8,24},{12,28},{16,0},{20,4},{24,8},{28,12},{1,17},{... | collective-permute-start | bytes 245768 | tf_op jit(solution)/shard_map/ppermute | solution.py:519
  391.4 17.2 %collective-permute-start.60 = (bf16[128,512]{1,0:T(8,128)(2,1)S(1)}, bf16[128,512]{1,0:T(8,128)(2,1)S(1)}, u32[]{:S(2)}, u32[]{:S(2)}) collective-permute-start(bf16[128,512]{1,0:T(8,128)(2,1)S(1)} %fusion.54), channel_id=1, source_target_pairs={{0,0},{1,8},{2,16},{3,24},{4,4},{5,12},{6,20},{7,28},{8,1},{9,9},{... | collective-permute-start | bytes 393224 | tf_op jit(solution)/shard_map/ppermute | solution.py:533
  (110 other events, 1232.0 us)
